TPU v7x, 32 devices: a whole 2x2x4 slice. The times are simulated.
32 devices in a mesh: scene: 2 (over x), az: 8 (over z, y), rg: 2 (over core).
Axes of the slice: x: 2, y: 2, z: 4, core: 2. Of those that a mesh axis runs over, the one named last changes fastest.
Arguments:
- complex_phase_image: float32 [2, 1024, 1024], P(None, ('scene', 'az'), 'rg'), parts along dimension 1, may hold values from -6 to 6
- phase_to_topography_factor: float32 [1024, 1024], P(('scene', 'az'), 'rg'), parts along dimension 0, may hold values from 0.5 to 3
- terrain_model_heights: float32 [128, 16, 1024], P(('scene', 'az'), 'rg'), parts along dimension 0, may hold values from -6 to 6
- radar_parcel_listing: int32 [32, 9], P(('scene', 'az', 'rg')), parts along dimension 0, may hold values from -1 to 1023, as said below
- pixel_terrain_position: int32 [1024, 1024], P(('scene', 'az'), 'rg'), parts along dimension 0, may hold values from 0 to 9215, as said below
- multilook_receiving_patch: int32 [65536, 1], P(('scene', 'az', 'rg')), parts along dimension 0, may hold values from 0 to 15; in each aligned block of 2048 rows (0 to 2047, 2048 to 4095, ...) at most 256 rows name the same one
- multilook_base_point: int32 [65536], P(('scene', 'az', 'rg')), parts along dimension 0, may hold values from 0 to 2047
- multilook_splat_shares: float32 [4, 65536], P(None, ('scene', 'az', 'rg')), parts along dimension 1, may hold values from 0 to 1
Outputs:
- geocoded: float32 [2, 256, 256], P(None, ('scene', 'az'), 'rg'), parts along dimension 1
There are 2 independent parts, one for each index of `scene`. A program takes and returns all parts, laid end to end along the dimension named above; each array names one. Nothing has to cross between parts.
Inputs may be any that keep to these rules, and one draw needn't show every extreme that they name: `radar_parcel_listing`: entries are sub-block numbers lat * 16 + lon; each tile lists a rectangle of at most 3 x 3 sub-blocks in row-major order, then -1 padding. Tile (a, r) lists only sub-blocks with c * 8 - 1 <= lat <= (c + 1) * 8 for one map latitude row c (any row, not tied to a) and r * 8 - 1 <= lon <= (r + 1) * 8. Some tile has exactly 9 listed blocks. pixel_terrain_position // 1024 is a listed, non-padding slot of the pixel's own tile. `multilook_receiving_patch`: among the rows of one device (aligned blocks of 2048 rows) at most 256 name one map tile; some map tile is named by exactly 256 rows of some device.
All inputs are finite; a program needn't handle non-finite values.
Results may differ from a plain program's by a relative error of at most 0.00015.
Values sent between devices are 32-bit elements; how exact they have to be, the bound alone decides.
No kernel may reach another device: no remote copies, remote signals or barrier semaphores. Data moves between devices by JAX's collectives and lax.ppermute only.
A program may use at most 64 MiB of HBM per device.

v0:
```python
import math

import jax
import jax.numpy as jnp
from jax import lax
from jax.sharding import PartitionSpec as P

PATCH = 64
LOOK = 4


EPS = 1e-06
HIGH = lax.Precision.HIGHEST


def padded_2(value, sides, width):
    for axis, dim in sides:
        size, length = (lax.axis_size(axis), value.shape[dim])
        up = [(i, (i + 1) % size) for i in range(size - 1)]
        down = [(j, i) for i, j in up]
        last = lax.slice_in_dim(value, length - width, length, axis=dim)
        first = lax.slice_in_dim(value, 0, width, axis=dim)
        before = lax.ppermute(last, axis, up)
        after = lax.ppermute(first, axis, down)
        value = jnp.concatenate([before, value, after], axis=dim)
    return value


def passed_along(value, axis, steps):
    count = lax.axis_size(axis)
    first, last = (max(0, -steps), min(count, count - steps))
    return lax.ppermute(value, axis, [(source, source + steps) for source in range(first, last)])


def box_mean(magnitude):
    summed = jnp.zeros_like(magnitude)
    for shift_a in (-1, 0, 1):
        for shift_b in (-1, 0, 1):
            summed = summed + jnp.roll(jnp.roll(magnitude, shift_a, axis=1), shift_b, axis=2)
    return summed / 9.0


def dft_tables():
    steps_idx = jnp.arange(PATCH, dtype=jnp.int32)
    product = steps_idx[:, None] * steps_idx[None, :] % PATCH
    angle_table = product.astype(jnp.float32) * (2.0 * math.pi / PATCH)
    return (jnp.cos(angle_table), jnp.sin(angle_table))


def goldstein(patches):
    cosine_table, sine_table = dft_tables()
    forward = jnp.block([[cosine_table, -sine_table], [sine_table, cosine_table]])
    inverse = jnp.block([[cosine_table, sine_table], [-sine_table, cosine_table]])
    columns = jnp.einsum("phw,wk->phk", patches, forward, precision=HIGH)
    left_cos = jnp.einsum("kh,phc->pkc", cosine_table, columns, precision=HIGH)
    left_sin = jnp.einsum("kh,phc->pkc", sine_table, columns, precision=HIGH)
    spec_re = left_cos[..., :PATCH] + left_sin[..., PATCH:]
    spec_im = left_cos[..., PATCH:] - left_sin[..., :PATCH]
    smooth = box_mean(jnp.sqrt(spec_re * spec_re + spec_im * spec_im))
    spectral_gain = jnp.sqrt(smooth / (jnp.mean(smooth, axis=(1, 2), keepdims=True) + EPS))
    weighted = jnp.concatenate([spec_re * spectral_gain, spec_im * spectral_gain], axis=-1)
    back_cos = jnp.einsum("kh,phc->pkc", cosine_table, weighted, precision=HIGH)
    back_sin = jnp.einsum("kh,phc->pkc", sine_table, weighted, precision=HIGH)
    rows_re = back_cos[..., :PATCH] - back_sin[..., PATCH:]
    rows_im = back_cos[..., PATCH:] + back_sin[..., :PATCH]
    restored = jnp.concatenate([rows_re, rows_im], axis=-1)
    return jnp.einsum("phw,wk->phk", restored, inverse, precision=HIGH) / float(PATCH * PATCH)


def block_coords(block_lists, nlon_count):
    clipped = jnp.maximum(block_lists, 0)
    return (clipped // nlon_count, clipped % nlon_count)


def entry_rank(owner_key, is_valid):
    slots = owner_key.shape[-1]
    same_owner = (owner_key[:, :, None] == owner_key[:, None, :]) & is_valid[:, None, :]
    slot_ids = jnp.arange(slots, dtype=jnp.int32)
    earlier = slot_ids[None, :] < slot_ids[:, None]
    return jnp.sum((same_owner & earlier[None]).astype(jnp.int32), axis=2)


def pack_blocks(block_lists, owner_key, local_block, source_rows, self_key):
    slots = block_lists.shape[-1]
    is_valid = block_lists >= 0
    rank_within = entry_rank(owner_key, is_valid)
    slot_ids = jnp.arange(slots, dtype=jnp.int32)
    matches = (is_valid & (owner_key == self_key))[:, :, None] & (
        rank_within[:, :, None] == slot_ids[None, None, :]
    )
    picked = jnp.sum(jnp.where(matches, local_block[:, :, None], 0), axis=1)
    present = jnp.any(matches, axis=1)
    return jnp.where(present[..., None], source_rows[picked], 0.0)


def unpack_blocks(own_list, owner_key, received):
    slots = own_list.shape[-1]
    is_valid = own_list >= 0
    rank_within = entry_rank(owner_key[None], is_valid[None])[0]
    position = jnp.where(is_valid, owner_key * slots + rank_within, 0)
    return received.reshape(-1, received.shape[-1])[position]


def lookup_heights(height_lookup_table, positions, samples):
    lane_width = min(128, samples)
    table_rows = height_lookup_table.reshape(-1, lane_width)
    row_count = table_rows.shape[0]
    lines, width = positions.shape
    row_ids = jnp.arange(row_count, dtype=jnp.int32)
    lane_ids = jnp.arange(lane_width, dtype=jnp.int32)

    def lookup_block(block_positions):
        flat_positions = block_positions.reshape(-1)
        selector = (flat_positions[:, None] // lane_width == row_ids[None, :]).astype(jnp.float32)
        picked_rows = jnp.dot(
            selector, table_rows, precision=HIGH, preferred_element_type=jnp.float32
        )
        lane_match = (flat_positions % lane_width)[:, None] == lane_ids[None, :]
        return jnp.sum(jnp.where(lane_match, picked_rows, 0.0), axis=1).reshape(
            block_positions.shape
        )

    blocked = positions.reshape(lines // 8, 8, width)
    return lax.map(lookup_block, blocked).reshape(lines, width)


def body(
    complex_phase_image,
    phase_to_topography_factor,
    terrain_model_heights,
    radar_parcel_listing,
    pixel_terrain_position,
    multilook_receiving_patch,
    multilook_base_point,
    multilook_splat_shares,
):
    count_az = lax.axis_size("az")
    count_rg = lax.axis_size("rg")
    tiles = count_az * count_rg
    self_az = lax.axis_index("az")
    self_rg = lax.axis_index("rg")
    parcel_north_coordinate, parcel_east_coordinate, number_terrain_points = (
        terrain_model_heights.shape
    )
    nlon_count = parcel_east_coordinate * count_rg
    own_list = radar_parcel_listing[0]
    lat_own, lon_own = block_coords(own_list, nlon_count)
    all_lists = lax.all_gather(radar_parcel_listing, ("az", "rg"), axis=0, tiled=True)
    lat_all, lon_all = block_coords(all_lists, nlon_count)
    key_all = lat_all // parcel_north_coordinate * count_rg + lon_all // parcel_east_coordinate
    local_all = (lat_all - self_az * parcel_north_coordinate) * parcel_east_coordinate + (
        lon_all - self_rg * parcel_east_coordinate
    )
    outgoing = pack_blocks(
        all_lists,
        key_all,
        local_all,
        terrain_model_heights.reshape(
            parcel_north_coordinate * parcel_east_coordinate, number_terrain_points
        ),
        self_az * count_rg + self_rg,
    )
    received = lax.all_to_all(outgoing, ("az", "rg"), split_axis=0, concat_axis=0, tiled=True)
    key_own = lat_own // parcel_north_coordinate * count_rg + lon_own // parcel_east_coordinate
    height_lookup_table = unpack_blocks(own_list, key_own, received)
    height_values = lookup_heights(
        height_lookup_table, pixel_terrain_position, number_terrain_points
    )
    topo_phase = phase_to_topography_factor * height_values
    cosine_phase = jnp.cos(topo_phase)
    sine_phase = jnp.sin(topo_phase)
    real_part = complex_phase_image[0] * cosine_phase + complex_phase_image[1] * sine_phase
    imag_part = complex_phase_image[1] * cosine_phase - complex_phase_image[0] * sine_phase
    flattened = jnp.stack([real_part, imag_part])
    rim = PATCH // 4
    step = PATCH // 2
    az_lines, rg_samples = phase_to_topography_factor.shape
    padded = padded_2(flattened, (("az", 1), ("rg", 2)), rim)
    block_rows = az_lines // step
    block_cols = rg_samples // step
    row_pieces = padded.reshape(2, block_rows + 1, step, rg_samples + 2 * rim)
    strips = jnp.concatenate([row_pieces[:, :-1], row_pieces[:, 1:]], axis=2)
    col_pieces = strips.reshape(2, block_rows, PATCH, block_cols + 1, step)
    paired = jnp.concatenate([col_pieces[..., :-1, :], col_pieces[..., 1:, :]], axis=-1)
    patches = paired.transpose(1, 3, 2, 0, 4).reshape(block_rows * block_cols, PATCH, 2 * PATCH)
    restored = goldstein(patches).reshape(block_rows, block_cols, PATCH, 2, PATCH)
    core_cells = restored[:, :, rim : rim + step, :, rim : rim + step]
    filtered = core_cells.transpose(3, 0, 2, 1, 4).reshape(2, az_lines, rg_samples)
    map_lat = az_lines // LOOK
    map_lon = rg_samples // LOOK
    look_values = (
        filtered.reshape(2, map_lat, LOOK, map_lon, LOOK)
        .mean(axis=(2, 4))
        .reshape(2, map_lat * map_lon)
    )
    look_total = map_lat * map_lon
    capacity = 2 * look_total // tiles
    owner_tile = multilook_receiving_patch[:, 0]
    tile_ids = jnp.arange(tiles, dtype=jnp.int32)
    counts = jnp.sum((owner_tile[:, None] == tile_ids[None, :]).astype(jnp.int32), axis=0)
    starts = jnp.cumsum(counts) - counts
    sort_order = jnp.argsort(owner_tile, stable=True)
    sorted_owner = owner_tile[sort_order]
    rank_sorted = jnp.arange(look_total, dtype=jnp.int32) - starts[sorted_owner]
    slot_index = (
        jnp.zeros((look_total,), jnp.int32)
        .at[sort_order]
        .set(sorted_owner * capacity + rank_sorted)
    )
    payload = jnp.concatenate([look_values, multilook_splat_shares], axis=0)
    payload_buffer = jnp.zeros((6, tiles * capacity), jnp.float32).at[:, slot_index].set(payload)
    cell_buffer = jnp.zeros((tiles * capacity,), jnp.int32).at[slot_index].set(multilook_base_point)
    got_values, got_cells = (
        lax.all_to_all(
            payload_buffer.reshape(6, tiles, capacity),
            ("az", "rg"),
            split_axis=1,
            concat_axis=1,
            tiled=True,
        ),
        lax.all_to_all(
            cell_buffer.reshape(1, tiles, capacity),
            ("az", "rg"),
            split_axis=1,
            concat_axis=1,
            tiled=True,
        ),
    )
    got_values = got_values.reshape(6, tiles * capacity)
    got_cells = got_cells.reshape(tiles * capacity)
    stride = map_lon + 1
    base = got_cells // map_lon * stride + got_cells % map_lon
    corners = jnp.concatenate([base, base + 1, base + stride, base + stride + 1])
    weights = got_values[2:].reshape(-1)
    contributions = jnp.stack(
        [jnp.tile(got_values[0], 4) * weights, jnp.tile(got_values[1], 4) * weights, weights]
    )
    extended = jnp.zeros((3, (map_lat + 1) * stride), jnp.float32).at[:, corners].add(contributions)
    extended = extended.reshape(3, map_lat + 1, stride)
    carried_col = passed_along(extended[:, :, map_lon], "rg", 1)
    extended = extended.at[:, :, 0].add(carried_col)
    carried_row = passed_along(extended[:, map_lat, :map_lon], "az", 1)
    extended = extended.at[:, 0, :map_lon].add(carried_row)
    main_cells = extended[:, :map_lat, :map_lon]
    return main_cells[:2] / jnp.maximum(main_cells[2:3], 1.0)


def solution(mesh):
    return jax.shard_map(
        body,
        mesh=mesh,
        in_specs=(
            P(None, ("scene", "az"), "rg"),
            P(("scene", "az"), "rg"),
            P(("scene", "az"), "rg", None),
            P(("scene", "az", "rg"), None),
            P(("scene", "az"), "rg"),
            P(("scene", "az", "rg"), None),
            P(("scene", "az", "rg")),
            P(None, ("scene", "az", "rg")),
        ),
        out_specs=P(None, ("scene", "az"), "rg"),
        check_vma=False,
    )
```

profile of v0, /device:TPU:0, one launch (start us, length us, event | category | flops | bytes accessed | tf_op | source)
XLA Modules:
  0.0 290.7 jit_solution(13959791806732536806)
XLA Ops:
  0.0 23.4 %all-gather = s32[16,1,9]{2,1,0:T(1,128)S(1)} all-gather(s32[1,1,9]{2,1,0:T(1,128)} %bitcast.272), channel_id=1, replica_groups=mesh['scene'=2,'az'=8,'rg'=2] {'az','rg'}, dimensions={0}, use_global_device_ids=true | all-gather | bytes 612 | tf_op jit(solution)/shard_map/all_gather | solution.py:148
  26.5 3.7 %all-to-all-start.1 = ((f32[16,9,1024]{2,1,0:T(8,128)}), f32[16,9,1024]{2,1,0:T(8,128)S(1)}, u32[]{:S(2)}, u32[]{:S(2)}) async-start(f32[16,9,1024]{2,1,0:T(8,128)} %broadcast_select_fusion), calls=%async_computation.1 | async-start | bytes 2097152 | tf_op jit(solution)/shard_map/all_to_all | solution.py:163
  31.3 5.0 %sort.17 = (s32[2048]{0:T(1024)}, s32[2048]{0:T(1024)S(1)}) sort(s32[2048]{0:T(1024)S(1)} %bitcast.245, s32[2048]{0:T(1024)S(1)} %iota.50), dimensions={0}, to_apply=%region_0.1 | sort | flops 22528 | bytes 32768 | tf_op jit(solution)/shard_map/jit(argsort)/sort | solution.py:202
  36.4 11.8 %gather_fusion = s32[2048]{0:T(1024)S(1)} fusion(s32[2048]{0:T(1024)S(1)} %bitcast.246, s32[2048]{0:T(1024)S(1)} %get-tuple-element.187), kind=kCustom, calls=%fused_computation | custom fusion | bytes 24576 | tf_op jit(solution)/shard_map/gather | solution.py:203
  48.2 4.3 %compare_select_fusion.2 = (s32[2048,1]{0,1:T(1,128)S(1)}, s32[2048,1]{0,1:T(1,128)S(1)}) fusion(s32[]{:T(128)} %bitcast.12, s32[]{:T(128)} %bitcast.13, s32[]{:T(128)} %bitcast.14, s32[]{:T(128)} %bitcast.15, s32[]{:T(128)} %bitcast.16, s32[]{:T(128)} %bitcast.18, s32[]{:T(128)} %bitcast.17, s32[2048,1]{0,1:T(1,128)S(1)} %bitcast.257), kind=kLoop, calls=%fused_computation.144 | loop fusion | flops 30720 | bytes 24604 | tf_op jit(solution)/shard_map/gather | solution.py:204
  52.7 5.7 %fusion.81 = s32[2048]{0:T(1024)S(1)} fusion(pred[2048]{0:T(1024)(128)(4,1)S(1)} %get-tuple-element.131, pred[2048]{0:T(1024)(128)(4,1)S(1)} %get-tuple-element.130, pred[2048]{0:T(1024)(128)(4,1)S(1)} %get-tuple-element.129, pred[2048]{0:T(1024)(128)(4,1)S(1)} %get-tuple-element.128, pred[2048]{0:T(1024)(128)(4,1)S(1)} %get-tuple-element.127, ...), kind=kLoop, calls=%fused_computation.192 | loop fusion | flops 24576 | bytes 43044 | tf_op jit(solution)/shard_map/add | solution.py:208
  58.4 8.0 %scatter_custom_fusion = s32[2048]{0:T(1024)S(1)} fusion(s32[2048]{0:T(1024)S(1)} %get-tuple-element.188, s32[2048]{0:T(1024)S(1)} %fusion.81, s32[]{:T(128)} %constant.279.clone.1), kind=kCustom, calls=%fused_computation.213 | custom fusion | bytes 8196 | tf_op jit(solution)/shard_map/scatter | solution.py:208
  66.4 8.8 %scatter_custom_fusion.1 = s32[4096]{0:T(1024)} fusion(s32[2048]{0:T(1024)S(1)} %compare_select_fusion.9, s32[2048]{0:T(1024)} %param.20, s32[]{:T(128)} %constant.279.clone.1), kind=kCustom, calls=%fused_computation.200 | custom fusion | bytes 16896 | tf_op jit(solution)/shard_map/scatter | solution.py:212
  75.9 6.0 %all-to-all-start = ((s32[1,16,256]{2,0,1:T(1,128)}), s32[1,16,256]{2,0,1:T(1,128)S(1)}, u32[]{:S(2)}, u32[]{:S(2)}) async-start(s32[1,16,256]{2,0,1:T(1,128)} %bitcast.20), calls=%async_computation | async-start | bytes 32768 | tf_op jit(solution)/shard_map/all_to_all | solution.py:221
  82.6 20.8 %while.15 = (s32[]{:T(128)}, f32[8,8,512]{2,1,0:T(8,128)S(1)}, s32[8,8,512]{2,1,0:T(8,128)}, f32[72,128]{1,0:T(8,128)S(1)}, s32[]{:T(128)}) while((s32[]{:T(128)}, f32[8,8,512]{2,1,0:T(8,128)S(1)}, s32[8,8,512]{2,1,0:T(8,128)}, f32[72,128]{1,0:T(8,128)S(1)}, s32[]{:T(128)}) %tuple.91), condition=%wide.region_11.12_spmd.clone, body=%wide.region_9.11_spmd.clone.sunk | while | flops 454926336 | bytes 266309 | solution.py:124
  83.4 1.8 fusion.136
  86.0 1.8 fusion.136
  88.6 1.8 fusion.136
  91.2 1.8 fusion.136
  93.8 1.8 fusion.136
  96.4 1.8 fusion.136
  99.0 1.8 fusion.136
  101.6 1.8 fusion.136
  104.0 3.8 %collective-permute-start = (f32[2,16,512]{2,1,0:T(8,128)S(1)}, f32[2,16,512]{2,1,0:T(8,128)S(1)}, u32[]{:S(2)}, u32[]{:S(2)}) collective-permute-start(f32[2,16,512]{2,1,0:T(8,128)S(1)} %get-tuple-element.179), channel_id=1, source_target_pairs={{0,2},{2,4},{4,6},{6,8},{8,10},{10,12},{12,14},{1,3},{3,5},{5,7},{... | collective-permute-start | bytes 196616 | tf_op jit(solution)/shard_map/ppermute | solution.py:23
  109.7 4.3 %collective-permute-done.1 = f32[2,16,512]{2,1,0:T(8,128)S(1)} collective-permute-done((f32[2,16,512]{2,1,0:T(8,128)S(1)}, f32[2,16,512]{2,1,0:T(8,128)S(1)}, u32[]{:S(2)}, u32[]{:S(2)}) %collective-permute-start.1) | collective-permute-done | bytes 65568 | tf_op jit(solution)/shard_map/ppermute | solution.py:24
  119.7 2.4 copy.63
  122.1 2.8 reshape.876
  131.8 2.3 fusion.116
  142.4 4.5 %reshape_reshape.3 = f32[2,16,4,128,4]{4,3,2,1,0:T(8,128)} reshape(f32[2,2,32,16,32]{4,3,2,1,0:T(8,128)S(1)} %bitcast.249) | data formatting | bytes 524288 | tf_op jit(solution)/shard_map/reshape;reshape | solution.py:192
  146.9 4.0 %reduce_sum.77 = f32[2,16,128]{2,1,0:T(8,128)S(1)} reduce(f32[2,16,4,128,4]{4,3,2,1,0:T(8,128)} %reshape_reshape.3, f32[]{:T(128)} %constant.278.clone.1), dimensions={2,4}, to_apply=%region_13.14 | reduce | flops 61440 | bytes 278532 | tf_op jit(solution)/shard_map/reduce_sum | solution.py:193
  151.4 6.2 %scatter_custom_fusion.2 = f32[6,4096]{0,1:T(8,128)S(1)} fusion(s32[2048]{0:T(1024)} %copy-done.7, f32[2048,6]{1,0:T(8,128)S(1)} %copy.65, f32[]{:T(128)} %constant.278.clone.1), kind=kCustom, calls=%fused_computation.68 | custom fusion | bytes 98816 | tf_op jit(solution)/shard_map/scatter | solution.py:211
  158.9 5.5 %all-to-all-start.2 = ((f32[6,16,256]{2,0,1:T(8,128)}), f32[6,16,256]{2,0,1:T(8,128)S(1)}, u32[]{:S(2)}, u32[]{:S(2)}) async-start(f32[6,16,256]{2,0,1:T(8,128)} %copy.66), calls=%async_computation.2 | async-start | bytes 262144 | tf_op jit(solution)/shard_map/all_to_all | solution.py:214
  164.6 7.8 %all-to-all-done.2 = f32[6,16,256]{2,0,1:T(8,128)S(1)} async-done(((f32[6,16,256]{2,0,1:T(8,128)}), f32[6,16,256]{2,0,1:T(8,128)S(1)}, u32[]{:S(2)}, u32[]{:S(2)}) %all-to-all-start.2) | async-done | bytes 98336 | tf_op jit(solution)/shard_map/all_to_all | solution.py:214
  173.0 5.1 %copy.68 = f32[16384,3]{1,0:T(8,128)} copy(f32[16384,3]{0,1:T(4,128)S(1)} %maximum_bitcast_fusion.1) | data formatting | bytes 393216 | tf_op jit(solution)/shard_map/stack | solution.py:235
  178.1 95.3 %scatter_custom_fusion.3 = f32[3,2193]{0,1:T(8,128)S(1)} fusion(s32[16384]{0:T(1024)S(1)} %bitcast.260, f32[16384,3]{1,0:T(8,128)} %copy.68, f32[]{:T(128)} %constant.278.clone.1), kind=kCustom, calls=%fused_computation.71 | custom fusion | flops 49152 | bytes 26828 | tf_op jit(solution)/shard_map/scatter-add | solution.py:238
  274.0 11.4 %collective-permute-start.4 = (f32[3,17]{1,0:T(4,128)S(1)}, f32[3,17]{1,0:T(4,128)S(1)}, u32[]{:S(2)}, u32[]{:S(2)}) collective-permute-start(f32[3,17]{1,0:T(4,128)S(1)} %slice_reduce_fusion), channel_id=1, source_target_pairs={{0,1},{2,3},{4,5},{6,7},{8,9},{10,11},{12,13},{14,15},{16,17},{18,... | collective-permute-start | bytes 620 | tf_op jit(solution)/shard_map/ppermute | solution.py:32
  286.4 2.1 collective-permute-start.5
  (164 shorter events, 41.0 us)
Async XLA Ops:
  0.0 24.4 %copy-start = (f32[8,8,1024]{2,1,0:T(8,128)S(1)}, f32[8,8,1024]{2,1,0:T(8,128)}, u32[]{:S(2)}) copy-start(f32[8,8,1024]{2,1,0:T(8,128)} %param.16) | copy-start | bytes 786436
  25.4 4.8 %copy-start.2 = (s32[2048,1]{0,1:T(1,128)S(1)}, s32[2048,1]{0,1:T(1,128)}, u32[]{:S(2)}) copy-start(s32[2048,1]{0,1:T(1,128)} %param.19) | copy-start | bytes 24580
  26.5 49.4 %all-to-all-start.1 = ((f32[16,9,1024]{2,1,0:T(8,128)}), f32[16,9,1024]{2,1,0:T(8,128)S(1)}, u32[]{:S(2)}, u32[]{:S(2)}) async-start(f32[16,9,1024]{2,1,0:T(8,128)} %broadcast_select_fusion), calls=%async_computation.1 | async-start | bytes 2097152 | tf_op jit(solution)/shard_map/all_to_all | solution.py:163
  36.4 38.9 %copy-start.8 = (s32[1,9]{1,0:T(1,128)S(1)}, s32[1,9]{1,0:T(1,128)}, u32[]{:S(2)}) copy-start(s32[1,9]{1,0:T(1,128)} %param.17) | copy-start | bytes 112
  66.4 15.5 %copy-start.7 = (s32[2048]{0:T(1024)}, s32[2048]{0:T(1024)S(1)}, u32[]{:S(2)}) copy-start(s32[2048]{0:T(1024)S(1)} %compare_select_fusion.9) | copy-start | bytes 24580
  75.9 33.2 %all-to-all-start = ((s32[1,16,256]{2,0,1:T(1,128)}), s32[1,16,256]{2,0,1:T(1,128)S(1)}, u32[]{:S(2)}, u32[]{:S(2)}) async-start(s32[1,16,256]{2,0,1:T(1,128)} %bitcast.20), calls=%async_computation | async-start | bytes 32768 | tf_op jit(solution)/shard_map/all_to_all | solution.py:221
  82.6 20.8 %copy-start.3 = (f32[2,64,512]{2,1,0:T(8,128)S(1)}, f32[2,64,512]{2,1,0:T(8,128)}, u32[]{:S(2)}) copy-start(f32[2,64,512]{2,1,0:T(8,128)} %param.14) | copy-start | bytes 786436
  82.6 20.8 %copy-start.4 = (f32[64,512]{1,0:T(8,128)S(1)}, f32[64,512]{1,0:T(8,128)}, u32[]{:S(2)}) copy-start(f32[64,512]{1,0:T(8,128)} %param.15) | copy-start | bytes 393220
  104.0 5.7 %collective-permute-start = (f32[2,16,512]{2,1,0:T(8,128)S(1)}, f32[2,16,512]{2,1,0:T(8,128)S(1)}, u32[]{:S(2)}, u32[]{:S(2)}) collective-permute-start(f32[2,16,512]{2,1,0:T(8,128)S(1)} %get-tuple-element.179), channel_id=1, source_target_pairs={{0,2},{2,4},{4,6},{6,8},{8,10},{10,12},{12,14},{1,3},{3,5},{5,7},{... | collective-permute-start | bytes 196616 | tf_op jit(solution)/shard_map/ppermute | solution.py:23
  107.8 6.2 %collective-permute-start.1 = (f32[2,16,512]{2,1,0:T(8,128)S(1)}, f32[2,16,512]{2,1,0:T(8,128)S(1)}, u32[]{:S(2)}, u32[]{:S(2)}) collective-permute-start(f32[2,16,512]{2,1,0:T(8,128)S(1)} %get-tuple-element.180), channel_id=1, source_target_pairs={{2,0},{4,2},{6,4},{8,6},{10,8},{12,10},{14,12},{3,1},{5,3},{7,5},{... | collective-permute-start | bytes 196616 | tf_op jit(solution)/shard_map/ppermute | solution.py:24
  114.1 3.2 %collective-permute-start.2 = (f32[2,96,16]{2,1,0:T(8,128)S(1)}, f32[2,96,16]{2,1,0:T(8,128)S(1)}, u32[]{:S(2)}, u32[]{:S(2)}) collective-permute-start(f32[2,96,16]{2,1,0:T(8,128)S(1)} %get-tuple-element.177), channel_id=1, source_target_pairs={{0,1},{2,3},{4,5},{6,7},{8,9},{10,11},{12,13},{14,15},{16,17},{18,... | collective-permute-start | bytes 36872 | tf_op jit(solution)/shard_map/ppermute | solution.py:23
  115.4 3.2 %collective-permute-start.3 = (f32[2,96,16]{2,1,0:T(8,128)S(1)}, f32[2,96,16]{2,1,0:T(8,128)S(1)}, u32[]{:S(2)}, u32[]{:S(2)}) collective-permute-start(f32[2,96,16]{2,1,0:T(8,128)S(1)} %get-tuple-element.178), channel_id=1, source_target_pairs={{1,0},{3,2},{5,4},{7,6},{9,8},{11,10},{13,12},{15,14},{17,16},{19,... | collective-permute-start | bytes 36872 | tf_op jit(solution)/shard_map/ppermute | solution.py:24
  146.9 4.1 %copy-start.6 = (f32[4,2048]{1,0:T(4,128)S(1)}, f32[4,2048]{1,0:T(4,128)}, u32[]{:S(2)}) copy-start(f32[4,2048]{1,0:T(4,128)} %param.21) | copy-start | bytes 98308
  151.4 13.1 %copy-start.5 = (s32[4096]{0:T(1024)S(1)}, s32[4096]{0:T(1024)}, u32[]{:S(2)}) copy-start(s32[4096]{0:T(1024)} %get-tuple-element.186) | copy-start | bytes 49156
  158.9 13.5 %all-to-all-start.2 = ((f32[6,16,256]{2,0,1:T(8,128)}), f32[6,16,256]{2,0,1:T(8,128)S(1)}, u32[]{:S(2)}, u32[]{:S(2)}) async-start(f32[6,16,256]{2,0,1:T(8,128)} %copy.66), calls=%async_computation.2 | async-start | bytes 262144 | tf_op jit(solution)/shard_map/all_to_all | solution.py:214
  173.0 117.7 %copy-start.1 = (f32[8,8,1024]{2,1,0:T(8,128)S(1)}, f32[8,8,1024]{2,1,0:T(8,128)}, u32[]{:S(2)}) copy-start(f32[8,8,1024]{2,1,0:T(8,128)} %param.16) | copy-start | bytes 786436
  274.0 12.2 %collective-permute-start.4 = (f32[3,17]{1,0:T(4,128)S(1)}, f32[3,17]{1,0:T(4,128)S(1)}, u32[]{:S(2)}, u32[]{:S(2)}) collective-permute-start(f32[3,17]{1,0:T(4,128)S(1)} %slice_reduce_fusion), channel_id=1, source_target_pairs={{0,1},{2,3},{4,5},{6,7},{8,9},{10,11},{12,13},{14,15},{16,17},{18,... | collective-permute-start | bytes 620 | tf_op jit(solution)/shard_map/ppermute | solution.py:32
  286.4 3.4 %collective-permute-start.5 = (f32[3,128]{1,0:T(4,128)S(1)}, f32[3,128]{1,0:T(4,128)S(1)}, u32[]{:S(2)}, u32[]{:S(2)}) collective-permute-start(f32[3,128]{1,0:T(4,128)S(1)} %bitcast.270), channel_id=1, source_target_pairs={{0,2},{2,4},{4,6},{6,8},{8,10},{10,12},{12,14},{1,3},{3,5},{5,7},{... | collective-permute-start | bytes 4616 | tf_op jit(solution)/shard_map/ppermute | solution.py:32
where the time goes:
time: 294 us; the launch traced here: 291 us
  other arithmetic  126 us (43%)
  local copies, waits for them, and re-layouts  65.9 us (22%)
  starting transfers between devices  36.4 us (12%)
  blocking collectives  23.4 us (8%)
  matrix products  21.5 us (7%)
  waiting for transfers between devices  16 us (5%)
    scatter-add x1, other arithmetic, body(): jnp.zeros((3, (map_lat + 1) * stride), jnp.float32).at[:, corners]  95.3 us
    all_gather x1, blocking collectives, body(): lax.all_gather(radar_parcel_listing, ('az', 'rg'), axis=0, tiled=True)  23.4 us
    dot_general x8, matrix products, lookup_block(): jnp.dot(selector, table_rows, precision=HIGH, preferred_element_type=jnp....  14.3 us
    ppermute x2, starting transfers between devices, passed_along(): lax.ppermute(value, axis, [(source, source + steps) for source in range(f...  13.5 us
    gather x1, local copies, waits for them, and re-layouts, body(): sorted_owner = owner_tile[sort_order]  11.8 us
    scatter x1, local copies, waits for them, and re-layouts, body(): jnp.zeros((tiles * capacity,), jnp.int32).at[slot_index]  8.79 us
    scatter x1, local copies, waits for them, and re-layouts, body(): slot_index = jnp.zeros((look_total,), jnp.int32).at[sort_order].set(sorte...  8.05 us
    all_to_all x1, waiting for transfers between devices, body(): lax.all_to_all(payload_buffer.reshape(6, tiles, capacity), ('az', 'rg'),...  7.81 us
  transfers between devices with their start and end apart: 9, of which 6 were waited for; matrix products, arithmetic and copies ran while one was open for 23% of the time, Pallas kernels for 0%

commit v1 on v0

v1 whole, which is shorter than its diff:
```python
import functools
import math

import jax
import jax.numpy as jnp
import numpy as np
from jax import lax
from jax.experimental import pallas as pl
from jax.experimental.pallas import tpu as pltpu
from jax.sharding import PartitionSpec as P

PATCH = 64
LOOK = 4
EPS = 1e-06
LANES = 128
RIM = PATCH // 4
STEP = PATCH // 2
HALF = PATCH // 2
F32 = jnp.float32
BF16 = jnp.bfloat16
I32 = jnp.int32
VMEM = pltpu.VMEM
VSPEC = pl.BlockSpec(memory_space=pltpu.VMEM)
SSPEC = pl.BlockSpec(memory_space=pltpu.SMEM)


def call(kernel, outs, args, scratch=(), smem=(), cost=(1_000_000, 1_000_000)):
    return pl.pallas_call(
        kernel,
        out_shape=outs,
        in_specs=[SSPEC if i in smem else VSPEC for i in range(len(args))],
        out_specs=jax.tree.map(lambda _: VSPEC, outs),
        scratch_shapes=list(scratch),
        cost_estimate=pl.CostEstimate(flops=cost[0], bytes_accessed=cost[1], transcendentals=0),
    )(*args)


def sds(shape, dtype=F32):
    return jax.ShapeDtypeStruct(shape, dtype)


def split(x):
    hi = x.astype(BF16)
    return hi, (x - hi.astype(F32)).astype(BF16)


def dot(a, b):
    return jnp.dot(a, b, preferred_element_type=F32)


def dot_nt(a, b):
    return lax.dot_general(a, b, (((1,), (1,)), ((), ())), preferred_element_type=F32)


def lane_iota(shape):
    return lax.broadcasted_iota(I32, shape, len(shape) - 1)


def row_iota(shape):
    return lax.broadcasted_iota(I32, shape, 0)


def roll(x, shift, axis):
    shift = shift % x.shape[axis]
    return x if shift == 0 else pltpu.roll(x, shift, axis)


def lane_gather(row, index):
    return jnp.take_along_axis(jnp.broadcast_to(row, index.shape), index, axis=1)


def host_split(x):
    hi = np.asarray(x, np.float32).astype(BF16)
    lo = (np.asarray(x, np.float64) - hi.astype(np.float64)).astype(BF16)
    return hi, lo


def filter_tables(block_rows):
    turn = 2.0 * math.pi / PATCH
    step = np.arange(PATCH)
    cosine = np.cos(turn * (step[:, None] * step[None, :] % PATCH))
    sine = np.sin(turn * (step[:, None] * step[None, :] % PATCH))
    rows = block_rows * STEP + 2 * RIM
    count = block_rows * PATCH
    az = np.zeros((2 * count, 2 * rows))
    for u in range(block_rows):
        k = slice(u * PATCH, (u + 1) * PATCH)
        ki = slice(count + u * PATCH, count + (u + 1) * PATCH)
        h = slice(u * STEP, u * STEP + PATCH)
        hi = slice(rows + u * STEP, rows + u * STEP + PATCH)
        az[k, h], az[k, hi] = cosine, sine
        az[ki, h], az[ki, hi] = -sine, cosine
    pieces = LANES // HALF
    rg = np.zeros((2 * LANES, pieces * 2 * PATCH))
    for q in range(pieces):
        w = slice(q * HALF, (q + 1) * HALF)
        wi = slice(LANES + q * HALF, LANES + (q + 1) * HALF)
        lr = slice(q * 2 * PATCH, q * 2 * PATCH + PATCH)
        li = slice(q * 2 * PATCH + PATCH, (q + 1) * 2 * PATCH)
        rg[w, lr], rg[wi, lr] = cosine[:HALF], sine[:HALF]
        rg[w, li], rg[wi, li] = -sine[:HALF], cosine[:HALF]
    looks = STEP // LOOK
    core = cosine[RIM : RIM + STEP].reshape(looks, LOOK, PATCH).mean(axis=1)
    core_s = sine[RIM : RIM + STEP].reshape(looks, LOOK, PATCH).mean(axis=1)
    back = np.zeros((2 * block_rows * looks, count))
    for u in range(block_rows):
        k = slice(u * PATCH, (u + 1) * PATCH)
        back[u * looks : (u + 1) * looks, k] = core / PATCH
        back[(block_rows + u) * looks : (block_rows + u + 1) * looks, k] = core_s / PATCH
    c_l, s_l = core.T / PATCH, core_s.T / PATCH
    reps = LANES // looks
    last = np.concatenate(
        [
            np.concatenate([np.tile(c_l, reps), np.tile(s_l, reps)], axis=1),
            np.concatenate([np.tile(-s_l, reps), np.tile(c_l, reps)], axis=1),
            np.concatenate([np.tile(-s_l, reps), np.tile(c_l, reps)], axis=1),
            np.concatenate([np.tile(-c_l, reps), np.tile(-s_l, reps)], axis=1),
        ],
        axis=0,
    )
    return az, rg, back, last


def slice_kernel(width, dem_ref, list_ref, out_ref):
    tiles = out_ref.shape[0]
    lats, lons, _ = dem_ref.shape
    packed = LANES // width
    groups = lats // packed
    slots = list_ref.shape[1]
    lane = lane_iota((lons, LANES))
    listed = list_ref[...].astype(F32)
    for q in range(tiles):
        tile, offset = divmod(q * width, LANES)
        for g in range(groups):
            total = None
            for p in range(packed):
                x = dem_ref[p * groups + g, :, tile * LANES : (tile + 1) * LANES]
                x = roll(x, p * width - offset, 1)
                total = x if total is None else jnp.where(lane // width == p, x, total)
            out_ref[q, g * lons : (g + 1) * lons, :] = total
        out_ref[q, groups * lons : groups * lons + 1, 0:slots] = listed


def halo_kernel(par_ref, image_ref, factor_ref, position_ref, one_ref, two_ref):
    even = par_ref[0] == 0
    lines = factor_ref.shape[0]
    fields = (
        lambda s: image_ref[0, s, :],
        lambda s: image_ref[1, s, :],
        lambda s: factor_ref[s, :],
        lambda s: position_ref[s, :].astype(F32),
    )
    for i, field in enumerate(fields):
        first = field(slice(0, RIM))
        last = field(slice(lines - RIM, lines))
        one_ref[i] = jnp.where(even, last, first)
        two_ref[i] = jnp.where(even, first, last)


def border_rows(b0, b1, n_rg):
    tiles = b0.shape[0]
    dest = row_iota(b0.shape)
    shifted = roll(b1, 1, 1)
    below = roll(b0, n_rg, 0)
    beside = roll(shifted, n_rg, 0)
    diagonal = jnp.where(dest % n_rg > 0, roll(shifted, n_rg + 1, 0), 0.0)
    beside = jnp.where(lane_iota(b0.shape) == 0, diagonal, beside)
    return jnp.where(dest >= n_rg, below + beside, 0.0)


def pack_kernel(n_rg, cap_rows, owner_ref, base_ref, share_ref, early_ref, im_ref, in_ref, mask_ref, col_ref, hot_ref, lhs_ref):
    tiles = early_ref.shape[0]
    height, width = owner_ref.shape
    owner = owner_ref[...]
    batch = min(tiles, 16)
    tri = (row_iota((width, width)) < lane_iota((width, width))).astype(BF16)
    ones = jnp.ones((width, width), BF16)
    size = batch * height
    r, c = row_iota((size, size)), lane_iota((size, size))
    lower = ((r // height == c // height) & (c < r)).astype(BF16)
    rank = jnp.zeros((height, width), F32)
    for b in range(tiles // batch):
        hot = jnp.concatenate([(owner == b * batch + o).astype(F32) for o in range(batch)], axis=0)
        hot16 = hot.astype(BF16)
        before = dot(hot16, tri) + dot(lower, dot(hot16, ones).astype(BF16))
        kept = hot * before
        for o in range(batch):
            rank = rank + kept[o * height : (o + 1) * height]
    rank = rank.astype(I32)
    base = base_ref[...]
    column = base % width
    line = base // width
    cap = cap_rows * LANES
    for m in range(height):
        cut = slice(m * width, (m + 1) * width)
        hot_ref[:, cut] = (row_iota((cap, width)) == rank[m : m + 1]).astype(F32).astype(BF16)
        col_ref[:, cut] = (row_iota((width, width)) == column[m : m + 1]).astype(F32).astype(BF16)
        mine = row_iota((tiles, width)) == owner[m : m + 1]
        lhs_ref[0:tiles, cut] = mine.astype(F32).astype(BF16)
        lhs_ref[tiles : 2 * tiles, cut] = jnp.where(mine, float(m), 0.0).astype(BF16)
        lhs_ref[2 * tiles :, cut] = jnp.where(mine, lane_iota((tiles, width)).astype(F32), 0.0).astype(BF16)
        edge = mine & (line[m : m + 1] == height - 1)
        mask_ref[0:tiles, cut] = jnp.where(edge, share_ref[2, m : m + 1, :], 0.0)
        mask_ref[tiles:, cut] = jnp.where(edge, share_ref[3, m : m + 1, :], 0.0)
    found = dot_nt(lhs_ref[...], hot_ref[...])
    valid = found[0:tiles] > 0.5
    at_m = found[tiles : 2 * tiles].astype(I32)
    at_n = found[2 * tiles :].astype(I32)
    im_ref[...] = at_m
    in_ref[...] = at_n
    cell = base.astype(F32)
    for channel in range(5):
        for k in range(cap_rows):
            cut = slice(k * LANES, (k + 1) * LANES)
            total = jnp.zeros((tiles, LANES), F32)
            for m in range(height):
                row = cell[m : m + 1] if channel == 4 else share_ref[channel, m : m + 1, :]
                total = jnp.where(at_m[:, cut] == m, lane_gather(row, at_n[:, cut]), total)
            early_ref[:, channel * cap_rows + k, :] = jnp.where(valid[:, cut], total, 0.0)
    high, low = split(mask_ref[...])
    border = dot_nt(high, col_ref[...]) + dot_nt(low, col_ref[...])
    early_ref[:, 5 * cap_rows, :] = border_rows(border[:tiles], border[tiles:], n_rg)


def request_kernel(n_rg, grid, width, table_rows, list_ref, got_ref, early_ref, out_ref):
    lats, lons = grid
    tiles, slots = list_ref.shape
    packed = LANES // width
    groups = lats // packed
    nlon = lons * n_rg
    for t in range(tiles):
        for f in range(slots):
            g = jnp.maximum(list_ref[t, f], 0)
            lat, lon = g // nlon, g % nlon
            key = lat // lats * n_rg + lon // lons
            inner, side = lat % lats, lon % lons
            piece = inner // groups
            row = got_ref[key, pl.ds(inner % groups * lons + side, 1), :]
            aligned = row
            for p in range(1, packed):
                aligned = jnp.where(piece == p, roll(row, -p * width, 1), aligned)
            for n, dest in ((0, t + n_rg), (1, t), (2, t - n_rg)):
                if 0 <= dest < tiles:
                    place, line = divmod(n * slots + f, table_rows)
                    put = roll(aligned, place * width, 1)
                    cut = slice(place * width, (place + 1) * width)
                    out_ref[dest, line : line + 1, cut] = put[:, cut]
        out_ref[t, table_rows:, :] = early_ref[t]


def sincos(x):
    n = jnp.floor(x * (2.0 / math.pi) + 0.5)
    r = x - n * 1.5703125
    r = r - n * 4.837512969970703e-4
    r = r - n * 7.549789954891882e-8
    z = r * r
    s = ((-1.9515295891e-4 * z + 8.3321608736e-3) * z - 1.6666654611e-1) * z * r + r
    c = ((2.443315711809948e-5 * z - 1.388731625493765e-3) * z + 4.166664568298827e-2) * z * z - 0.5 * z + 1.0
    q = n.astype(I32)
    odd = (q & 1) == 1
    sine = jnp.where(odd, c, s)
    cosine = jnp.where(odd, s, c)
    sine = jnp.where((q & 2) == 2, -sine, sine)
    cosine = jnp.where(((q + 1) & 2) == 2, -cosine, cosine)
    return cosine, sine


def flatten_kernel(width, table_rows, slots, par_ref, got_ref, image_ref, factor_ref, position_ref, one_ref, two_ref, flat_ref, edge_ref, tab_ref, in_ref, at_ref):
    even = par_ref[0] == 0
    lines, samples = factor_ref.shape
    packed = LANES // width
    tiles = got_ref.shape[0]
    parts = tiles // packed
    lane = lane_iota((table_rows, LANES))
    for k in range(parts):
        for place in range(packed):
            total = None
            for j in range(packed):
                x = roll(got_ref[k * packed + j, 0:table_rows, :], (j - place) * width, 1)
                total = x if total is None else jnp.where(lane // width == j, x, total)
            tab_ref[k, place] = total
    for i in range(3):
        top = jnp.where(even, two_ref[i], one_ref[i])
        low = jnp.where(even, one_ref[i], two_ref[i])
        in_ref[i, 0:RIM] = top
        in_ref[i, RIM + lines :] = low
    in_ref[0, RIM : RIM + lines] = image_ref[0]
    in_ref[1, RIM : RIM + lines] = image_ref[1]
    in_ref[2, RIM : RIM + lines] = factor_ref[...]
    at_ref[0:RIM] = jnp.where(even, two_ref[3], one_ref[3]).astype(I32)
    at_ref[RIM : RIM + lines] = position_ref[...]
    at_ref[RIM + lines :] = jnp.where(even, one_ref[3], two_ref[3]).astype(I32)
    cols = samples // LANES
    chunk = 16

    def block(table, start):
        at = at_ref[pl.ds(start, chunk), :]
        lanes = [at[:, j * LANES : (j + 1) * LANES] & (LANES - 1) for j in range(cols)]
        lines_at = [at[:, j * LANES : (j + 1) * LANES] // LANES for j in range(cols)]
        height = [jnp.zeros((chunk, LANES), F32) for _ in range(cols)]
        for f in range(slots):
            place, line = divmod(table * slots + f, table_rows)
            for k in range(parts):
                row = jnp.broadcast_to(tab_ref[k, place, line : line + 1, :], (chunk, LANES))
                for j in range(cols):
                    found = jnp.take_along_axis(row, lanes[j], axis=1)
                    height[j] = jnp.where(lines_at[j] == f * parts + k, found, height[j])
        for j in range(cols):
            cut = slice(j * LANES, (j + 1) * LANES)
            cosine, sine = sincos(in_ref[2, pl.ds(start, chunk), cut] * height[j])
            a, b = in_ref[0, pl.ds(start, chunk), cut], in_ref[1, pl.ds(start, chunk), cut]
            flat_ref[0, pl.ds(start, chunk), cut] = a * cosine + b * sine
            flat_ref[1, pl.ds(start, chunk), cut] = b * cosine - a * sine

    block(0, 0)

    @pl.loop(0, lines // chunk)
    def _(i):
        block(1, pl.multiple_of(RIM + i * chunk, chunk))

    block(2, RIM + lines)
    edge = lane_iota((lines + 2 * RIM, LANES))
    for c in range(2):
        first = flat_ref[c, :, 0:LANES]
        last = roll(flat_ref[c, :, samples - LANES : samples], 2 * RIM, 1)
        edge_ref[c] = jnp.where(edge < RIM, first, jnp.where(edge < 2 * RIM, last, 0.0))


def filter_kernel(n_rg, cap_rows, block_rows, rg_ref, flat_ref, edge_ref, az_h, az_l, rg_h, rg_l, back_ref, last_h, last_l, im_ref, in_ref, mask_ref, col_ref, out_ref, x_ref, d_ref, z_ref, look_ref):
    _, rows, samples = flat_ref.shape
    cols = samples // LANES
    lane = lane_iota((rows, LANES))
    left = rg_ref[0] > 0
    right = rg_ref[0] < n_rg - 1
    for c in range(2):
        halo = edge_ref[c]
        before = jnp.where(left, roll(halo, -RIM, 1), 0.0)
        after = jnp.where(right, roll(halo, RIM, 1), 0.0)
        for j in range(cols):
            now = roll(flat_ref[c, :, j * LANES : (j + 1) * LANES], RIM, 1)
            x_ref[c * rows : (c + 1) * rows, j * LANES : (j + 1) * LANES] = jnp.where(lane < RIM, before, now)
            before = now
        x_ref[c * rows : (c + 1) * rows, cols * LANES :] = jnp.where(
            lane < RIM, before, jnp.where(lane < 2 * RIM, after, 0.0)
        )
    high, low = split(x_ref[...])
    g = dot(az_h[...], high) + dot(az_h[...], low) + dot(az_l[...], high)
    count = block_rows * PATCH
    pieces = LANES // HALF
    for j in range(cols + 1):
        cut = slice(j * LANES, (j + 1) * LANES)
        both = jnp.concatenate([g[:count, cut], g[count:, cut]], axis=1)
        bh, bl = split(both)
        used = pieces if j < cols else 1
        wide = slice(0, used * 2 * PATCH)
        d = dot(bh, rg_h[:, wide]) + dot(bl, rg_h[:, wide]) + dot(bh, rg_l[:, wide])
        for q in range(used):
            d_ref[j * pieces + q] = d[:, q * 2 * PATCH : (q + 1) * 2 * PATCH]
    sign = jnp.where(lane_iota((1, LANES)) % 2 == 0, 1.0, -1.0)
    patches = samples // STEP

    @pl.loop(0, patches)
    def _(v):
        z = d_ref[v] + sign * d_ref[v + 1]
        q = z * z
        q = q + pltpu.roll(q, PATCH, 1)
        magnitude = jnp.sqrt(q)
        s = magnitude + pltpu.roll(magnitude, 1, 1) + pltpu.roll(magnitude, LANES - 1, 1)
        parts = []
        for u in range(block_rows):
            cut = slice(u * PATCH, (u + 1) * PATCH)
            su = s[cut]
            su = su + pltpu.roll(su, 1, 0) + pltpu.roll(su, PATCH - 1, 0)
            mean = jnp.sum(magnitude[cut], keepdims=True) * (1.0 / (2 * PATCH * PATCH))
            factor = 1.0 / (9.0 * (mean + EPS))
            parts.append(z[cut] * jnp.sqrt(su * factor))
        high, low = split(jnp.concatenate(parts, axis=0))
        at = pl.multiple_of(v * LANES, LANES)
        z_ref[0:count, pl.ds(at, LANES)] = high
        z_ref[count:, pl.ds(at, LANES)] = low

    t = dot(back_ref[...], z_ref[...])
    looks = block_rows * STEP // LOOK
    t = t[: 2 * looks] + t[2 * looks :]
    stacked = jnp.concatenate(
        [
            jnp.concatenate([t[:looks, v * LANES : (v + 1) * LANES], t[looks:, v * LANES : (v + 1) * LANES]], axis=1)
            for v in range(patches)
        ],
        axis=0,
    )
    sh, sl = split(stacked)
    y = dot(sh, last_h[...]) + dot(sl, last_h[...]) + dot(sh, last_l[...])
    group = lane_iota((looks, LANES)) // (STEP // LOOK)
    for c in range(2):
        total = jnp.zeros((looks, LANES), F32)
        for v in range(patches):
            part = y[v * looks : (v + 1) * looks, c * LANES : (c + 1) * LANES]
            total = jnp.where(group == v, part, total)
        look_ref[c] = total
    tiles = out_ref.shape[0]
    for k in range(cap_rows):
        cut = slice(k * LANES, (k + 1) * LANES)
        at_m, at_n = im_ref[:, cut], in_ref[:, cut]
        for c in range(2):
            total = jnp.zeros((tiles, LANES), F32)
            for m in range(looks):
                total = jnp.where(at_m == m, lane_gather(look_ref[c, m : m + 1, :], at_n), total)
            out_ref[:, c * cap_rows + k, :] = total
    for c in range(2):
        weighted = jnp.concatenate(
            [mask_ref[:, m * LANES : (m + 1) * LANES] * look_ref[c, m : m + 1, :] for m in range(looks)], axis=1
        )
        wh, wl = split(weighted)
        border = dot_nt(wh, col_ref[...]) + dot_nt(wl, col_ref[...])
        out_ref[:, 2 * cap_rows + c, :] = border_rows(border[:tiles], border[tiles:], n_rg)


def prepare_kernel(cap_rows, table_rows, map_lat, got_ref, hot_ref, row_ref, sum_ref, carry_ref):
    tiles = got_ref.shape[0]
    for t in range(tiles):
        for k in range(cap_rows):
            def channel(c):
                return got_ref[t, table_rows + c * cap_rows + k : table_rows + c * cap_rows + k + 1, :]

            cell = channel(4).astype(I32)
            line, column = cell // LANES, cell % LANES
            at = (t * cap_rows + k) * LANES
            cut = slice(at, at + LANES)
            hot_ref[:, cut] = (row_iota((LANES, LANES)) == column).astype(F32).astype(BF16)
            rows = row_iota((map_lat, LANES))
            here, next_line = rows == line, rows == line + 1
            for d in range(2):
                row_ref[d * map_lat : (d + 1) * map_lat, cut] = jnp.where(here, channel(d), 0.0) + jnp.where(
                    next_line, channel(2 + d), 0.0
                )
    high, low = split(row_ref[...])
    acc = dot_nt(high, hot_ref[...]) + dot_nt(low, hot_ref[...])
    shifted = roll(acc[map_lat:], 1, 1)
    lane = lane_iota(shifted.shape)
    edge = got_ref[0, table_rows + 5 * cap_rows : table_rows + 5 * cap_rows + 1, :]
    for t in range(1, tiles):
        edge = edge + got_ref[t, table_rows + 5 * cap_rows : table_rows + 5 * cap_rows + 1, :]
    total = acc[:map_lat] + jnp.where(lane == 0, 0.0, shifted)
    sum_ref[...] = total + jnp.where(row_iota(shifted.shape) == 0, edge, 0.0)
    carry_ref[...] = jnp.where(lane == 0, shifted, 0.0)


def splat_kernel(cap_rows, map_lat, got_ref, hot_ref, row_ref, sum_ref, carry_ref, x_ref):
    tiles = got_ref.shape[0]
    wide = 2 * map_lat
    for t in range(tiles):
        for k in range(cap_rows):
            cut = slice((t * cap_rows + k) * LANES, (t * cap_rows + k + 1) * LANES)
            for c in range(2):
                value = got_ref[t, c * cap_rows + k : c * cap_rows + k + 1, :]
                high, low = split(row_ref[:, cut] * value)
                x_ref[c * wide : (c + 1) * wide, cut] = high
                x_ref[(2 + c) * wide : (3 + c) * wide, cut] = low
    acc = dot_nt(x_ref[...], hot_ref[...])
    acc = acc[: 2 * wide] + acc[2 * wide :]
    for c in range(2):
        row = 2 * cap_rows + c
        edge = got_ref[0, row : row + 1, :]
        for t in range(1, tiles):
            edge = edge + got_ref[t, row : row + 1, :]
        shifted = roll(acc[c * wide + map_lat : (c + 1) * wide], 1, 1)
        lane = lane_iota(shifted.shape)
        total = acc[c * wide : c * wide + map_lat] + jnp.where(lane == 0, 0.0, shifted)
        sum_ref[c] = total + jnp.where(row_iota(shifted.shape) == 0, edge, 0.0)
        carry_ref[c] = jnp.where(lane == 0, shifted, 0.0)


def swap_pairs(count, first):
    return [p for i in range(first, count - 1, 2) for p in ((i, i + 1), (i + 1, i))]


def body(image, factor, heights, listing, position, owner, base, shares):
    n_az, n_rg = lax.axis_size("az"), lax.axis_size("rg")
    tiles = n_az * n_rg
    both = ("az", "rg")
    lats, lons, points = heights.shape
    slots = listing.shape[1]
    width = points // tiles
    packed = LANES // width
    lines, samples = factor.shape
    map_lat, map_lon = lines // LOOK, samples // LOOK
    block_rows = lines // STEP
    capacity = 2 * map_lat * map_lon // tiles
    cap_rows = -(-capacity // LANES)
    table_rows = -(-3 * slots // packed)
    table_rows = -(-table_rows // 8) * 8
    early_rows = -(-(5 * cap_rows + 1) // 8) * 8
    late_rows = -(-(2 * cap_rows + 2) // 8) * 8
    slice_rows = lats * lons // packed
    parity = (lax.axis_index("az") % 2).astype(I32).reshape(1)
    rg = lax.axis_index("rg").astype(I32).reshape(1)

    def exchange(x):
        return lax.all_to_all(x, both, split_axis=0, concat_axis=0, tiled=True)

    slices = call(
        functools.partial(slice_kernel, width),
        sds((tiles, slice_rows + 8, LANES)),
        (heights, listing),
    )
    got_slices = exchange(slices)
    one, two = call(halo_kernel, [sds((4, RIM, samples))] * 2, (parity, image, factor, position), smem=(0,))
    one = lax.ppermute(one, "az", swap_pairs(n_az, 0))
    two = lax.ppermute(two, "az", swap_pairs(n_az, 1))
    total = map_lat * map_lon
    early, at_m, at_n, edge_mask, edge_col = call(
        functools.partial(pack_kernel, n_rg, cap_rows),
        [
            sds((tiles, early_rows, LANES)),
            sds((tiles, cap_rows * LANES), I32),
            sds((tiles, cap_rows * LANES), I32),
            sds((2 * tiles, total)),
            sds((map_lon, total), BF16),
        ],
        (owner.reshape(map_lat, map_lon), base.reshape(map_lat, map_lon), shares.reshape(4, map_lat, map_lon)),
        scratch=(VMEM((cap_rows * LANES, total), BF16), VMEM((3 * tiles, total), BF16)),
    )
    lists = got_slices[:, slice_rows, :slots].astype(I32)
    request = call(
        functools.partial(request_kernel, n_rg, (lats, lons), width, table_rows),
        sds((tiles, table_rows + early_rows, LANES)),
        (lists, got_slices, early),
        smem=(0,),
    )
    tables = exchange(request)
    flat, edge = call(
        functools.partial(flatten_kernel, width, table_rows, slots),
        [sds((2, lines + 2 * RIM, samples)), sds((2, lines + 2 * RIM, LANES))],
        (parity, tables, image, factor, position, one, two),
        smem=(0,),
        scratch=(
            VMEM((tiles // packed, packed, table_rows, LANES), F32),
            VMEM((3, lines + 2 * RIM, samples), F32),
            VMEM((lines + 2 * RIM, samples), I32),
        ),
    )
    edge = lax.ppermute(edge, "rg", swap_pairs(n_rg, 0))
    az, rgt, back, last = filter_tables(block_rows)
    az_h, az_l = host_split(az)
    rg_h, rg_l = host_split(rgt)
    back_h, back_l = host_split(back)
    back_all = np.concatenate(
        [np.concatenate([back_h, back_h], axis=1), np.concatenate([back_l, np.zeros_like(back_l)], axis=1)], axis=0
    )
    last_h, last_l = host_split(last)
    rows = lines + 2 * RIM
    patches = samples // STEP
    count = block_rows * PATCH
    packed_looks = call(
        functools.partial(filter_kernel, n_rg, cap_rows, block_rows),
        sds((tiles, late_rows, LANES)),
        (rg, flat, edge, az_h, az_l, rg_h, rg_l, back_all, last_h, last_l, at_m, at_n, edge_mask, edge_col),
        smem=(0,),
        scratch=(
            VMEM((2 * rows, samples + LANES), F32),
            VMEM((patches + 1 + 3, count, 2 * PATCH), F32),
            VMEM((2 * count, patches * LANES), BF16),
            VMEM((2, map_lat, map_lon), F32),
        ),
    )
    got = exchange(packed_looks)
    wide = tiles * cap_rows * LANES
    hot, row_weights, weight_sum, weight_carry = call(
        functools.partial(prepare_kernel, cap_rows, table_rows, map_lat),
        [sds((LANES, wide), BF16), sds((2 * map_lat, wide)), sds((map_lat, map_lon)), sds((map_lat, map_lon))],
        (tables,),
    )
    right = [(i, i + 1) for i in range(n_rg - 1)]
    weight_sum = weight_sum + lax.ppermute(weight_carry, "rg", right)
    sums, carry = call(
        functools.partial(splat_kernel, cap_rows, map_lat),
        [sds((2, map_lat, map_lon)), sds((2, map_lat, map_lon))],
        (got, hot, row_weights),
        scratch=(VMEM((8 * map_lat, wide), BF16),),
    )
    sums = sums + lax.ppermute(carry, "rg", right)
    return sums / jnp.maximum(weight_sum, 1.0)[None]


def solution(mesh):
    return jax.shard_map(
        body,
        mesh=mesh,
        in_specs=(
            P(None, ("scene", "az"), "rg"),
            P(("scene", "az"), "rg"),
            P(("scene", "az"), "rg", None),
            P(("scene", "az", "rg"), None),
            P(("scene", "az"), "rg"),
            P(("scene", "az", "rg"), None),
            P(("scene", "az", "rg")),
            P(None, ("scene", "az", "rg")),
        ),
        out_specs=P(None, ("scene", "az"), "rg"),
        check_vma=False,
    )
```

time: 294 us -> 85.5 us (0.29)
  other arithmetic: 126 us -> 1.27 us
  local copies, waits for them, and re-layouts: 65.9 us -> 3.38 us
  Pallas kernels: 0 us -> 38.7 us
  blocking collectives: 23.4 us -> 0 us
  matrix products: 21.5 us -> 0 us
  starting transfers between devices: 36.4 us -> 22.9 us
    scatter-add x1 -> x0, other arithmetic: 95.3 us -> none  [body(): jnp.zeros((3, (map_lat + 1) * stride), jnp.float32).at[:, corners]]
    pallas_call x0 -> x8, Pallas kernels: none -> 38.7 us  [call(): pl.pallas_call(kernel, out_shape=outs, in_specs=[SSPEC if i in smem else...]
    all_gather x1 -> x0, blocking collectives: 23.4 us -> none  [body(): lax.all_gather(radar_parcel_listing, ('az', 'rg'), axis=0, tiled=True)]
    scatter x3 -> x0, local copies, waits for them, and re-layouts: 23.1 us -> none  [the longest x1 8.79 us: body(): jnp.zeros((tiles * capacity,), jnp.int32).at[slot_index]]
    dot_general x14 -> x0, matrix products: 21.5 us -> none  [the longest x8 14.3 us: lookup_block(): jnp.dot(selector, table_rows, precision=HIGH, preferred_element_type=jnp....]
    ppermute x6 -> x5, starting transfers between devices: 21.2 us -> 6.33 us  [the longest x1 2.3 us: body(): weight_sum = weight_sum + lax.ppermute(weight_carry, 'rg', right)]
    gather x5 -> x0, local copies, waits for them, and re-layouts: 14 us -> none  [the longest x1 11.8 us: body(): sorted_owner = owner_tile[sort_order]]
    another operation x4 -> x0, local copies, waits for them, and re-layouts: 9.81 us -> none  [the longest x1 5.08 us: body(): jnp.stack([jnp.tile(got_values[0], 4) * weights, jnp.tile(got_values[1],...]
  transfers between devices with their start and end apart: 9 -> 8, of which waited for: 6 -> 5; matrix products, arithmetic and copies ran while one was open for 23% -> 1% of each run, Pallas kernels for 0% -> 12%
where the time goes in v1:
time: 85.5 us; the launch traced here: 84.8 us
  Pallas kernels  38.7 us (45%)
  starting transfers between devices  22.9 us (27%)
  waiting for transfers between devices  18.5 us (22%)
  local copies, waits for them, and re-layouts  3.38 us (4%)
  other arithmetic  1.27 us (1%)
    pallas_call x8, Pallas kernels, call(): pl.pallas_call(kernel, out_shape=outs, in_specs=[SSPEC if i in smem else...  38.7 us
    all_to_all x3, starting transfers between devices, exchange(): return lax.all_to_all(x, both, split_axis=0, concat_axis=0, tiled=True)  16.5 us
    all_to_all x3, waiting for transfers between devices, exchange(): return lax.all_to_all(x, both, split_axis=0, concat_axis=0, tiled=True)  9.15 us
    ppermute x1, waiting for transfers between devices, body(): one = lax.ppermute(one, 'az', swap_pairs(n_az, 0))  6.8 us
    unnamed x19, local copies, waits for them, and re-layouts  3.38 us
    ppermute x1, starting transfers between devices, body(): weight_sum = weight_sum + lax.ppermute(weight_carry, 'rg', right)  2.3 us
    ppermute x1, starting transfers between devices, body(): one = lax.ppermute(one, 'az', swap_pairs(n_az, 0))  1.8 us
  transfers between devices with their start and end apart: 8, of which 5 were waited for; matrix products, arithmetic and copies ran while one was open for 1% of the time, Pallas kernels for 12%

profile of v1, /device:TPU:0, one launch (start us, length us, event | category | flops | bytes accessed | tf_op | source)
XLA Modules:
  0.0 84.8 jit_solution(16414665236464538176)
XLA Ops:
  0.0 1.8 %shard_map.145 = f32[16,40,128]{2,1,0:T(8,128)} custom-call(f32[8,8,1024]{2,1,0:T(8,128)} %dem_ref.1, s32[1,9]{1,0:T(1,128)} %list_ref.1), custom_call_target="tpu_custom_call" | custom-call | flops 1000000 | bytes 1000000 | tf_op jit(solution)/shard_map/pallas_call | solution.py:28
  1.8 7.5 %all-to-all-start = ((f32[16,40,128]{2,1,0:T(8,128)}), f32[16,40,128]{2,1,0:T(8,128)S(1)}, u32[]{:S(2)}, u32[]{:S(2)}) async-start(f32[16,40,128]{2,1,0:T(8,128)} %shard_map.145), calls=%async_computation | async-start | bytes 655360 | tf_op jit(solution)/shard_map/all_to_all | solution.py:500
  9.4 0.6 copy.18
  10.0 3.1 %shard_map.146 = (f32[16,16,128]{2,1,0:T(8,128)}, s32[16,256]{1,0:T(8,128)}, s32[16,256]{1,0:T(8,128)}, f32[32,2048]{1,0:T(8,128)}, bf16[128,2048]{1,0:T(8,128)(2,1)}) custom-call(s32[16,128]{1,0:T(8,128)} %bitcast.12, s32[16,128]{1,0:T(8,128)} %bitcast.13, f32[4,16,128]{2,1,0:T(8,128)} %bitcast.9), custom_call_target="tpu_custom_call" | custom-call | flops 1000000 | bytes 1000000 | tf_op jit(solution)/shard_map/pallas_call | solution.py:28
  13.1 7.3 %all-to-all-done.got_ref = f32[16,40,128]{2,1,0:T(8,128)S(1)} async-done(((f32[16,40,128]{2,1,0:T(8,128)}), f32[16,40,128]{2,1,0:T(8,128)S(1)}, u32[]{:S(2)}, u32[]{:S(2)}) %all-to-all-start) | async-done | bytes 327712 | tf_op jit(solution)/shard_map/all_to_all | solution.py:500
  20.4 0.6 slice_convert_fusion
  21.1 0.1 copy-done.1
  21.2 4.8 %shard_map.147 = f32[16,32,128]{2,1,0:T(8,128)} custom-call(s32[16,9]{1,0:T(8,128)} %bitcast.10, f32[16,40,128]{2,1,0:T(8,128)} %copy-done.1, f32[16,16,128]{2,1,0:T(8,128)} %get-tuple-element.20.early_ref), custom_call_target="tpu_custom_call" | custom-call | flops 1000000 | bytes 1000000 | tf_op jit(solution)/shard_map/pallas_call | solution.py:28
  26.0 3.5 %all-to-all-start.1 = ((f32[16,32,128]{2,1,0:T(8,128)}), f32[16,32,128]{2,1,0:T(8,128)S(1)}, u32[]{:S(2)}, u32[]{:S(2)}) async-start(f32[16,32,128]{2,1,0:T(8,128)} %shard_map.147), calls=%async_computation.1 | async-start | bytes 524288 | tf_op jit(solution)/shard_map/all_to_all | solution.py:500
  29.6 1.8 %shard_map.148 = (f32[4,16,512]{2,1,0:T(8,128)}, f32[4,16,512]{2,1,0:T(8,128)}) custom-call(s32[1]{0:T(128)} %bitcast.1.par_ref, f32[2,64,512]{2,1,0:T(8,128)} %image_ref.3, f32[64,512]{1,0:T(8,128)} %factor_ref.3, s32[64,512]{1,0:T(8,128)} %position_ref.3), custom_call_target="tpu_custom_call" | custom-call | flops 1000000 | bytes 1000000 | tf_op jit(solution)/shard_map/pallas_call | solution.py:28
  31.4 1.8 %collective-permute-start = (f32[4,16,512]{2,1,0:T(8,128)}, f32[4,16,512]{2,1,0:T(8,128)S(1)}, u32[]{:S(2)}, u32[]{:S(2)}) collective-permute-start(f32[4,16,512]{2,1,0:T(8,128)} %get-tuple-element.21), channel_id=1, source_target_pairs={{0,2},{2,0},{4,6},{6,4},{8,10},{10,8},{12,14},{14,12},{1,3},{3,1},... | collective-permute-start | bytes 393224 | tf_op jit(solution)/shard_map/ppermute | solution.py:509
  33.2 0.7 collective-permute-start.1
  33.8 6.8 %collective-permute-done.one_ref = f32[4,16,512]{2,1,0:T(8,128)S(1)} collective-permute-done((f32[4,16,512]{2,1,0:T(8,128)}, f32[4,16,512]{2,1,0:T(8,128)S(1)}, u32[]{:S(2)}, u32[]{:S(2)}) %collective-permute-start) | collective-permute-done | bytes 131104 | tf_op jit(solution)/shard_map/ppermute | solution.py:509
  40.6 0.0 collective-permute-done.1.two_ref
  40.6 0.6 copy-done.3
  41.3 0.0 copy-done.4
  41.3 0.7 copy-done
  42.0 12.4 %shard_map.149 = (f32[2,96,512]{2,1,0:T(8,128)}, f32[2,96,128]{2,1,0:T(8,128)}) custom-call(s32[1]{0:T(128)} %bitcast.1.par_ref, f32[16,32,128]{2,1,0:T(8,128)} %copy-done, f32[2,64,512]{2,1,0:T(8,128)} %image_ref.3, f32[64,512]{1,0:T(8,128)} %factor_ref.3, s32[64,512]{1,0:T(8,128)} %position_ref.3, f32[4,16,512]{2,1,0:T(8,128)} %copy-done.3, ...), custom_call_target="tpu_custom_call" | custom-call | flops 1000000 | bytes 1000000 | tf_op jit(solution)/shard_map/pallas_call | solution.py:28
  54.4 0.0 collective-permute-start.2
  54.4 1.5 %collective-permute-done.2.edge_ref = f32[2,96,128]{2,1,0:T(8,128)S(1)} collective-permute-done((f32[2,96,128]{2,1,0:T(8,128)}, f32[2,96,128]{2,1,0:T(8,128)S(1)}, u32[]{:S(2)}, u32[]{:S(2)}) %collective-permute-start.2) | collective-permute-done | bytes 98336 | tf_op jit(solution)/shard_map/ppermute | solution.py:543
  56.0 0.6 copy-done.5
  56.6 9.4 %shard_map.150 = f32[16,8,128]{2,1,0:T(8,128)} custom-call(s32[1]{0:T(128)} %bitcast.rg_ref, f32[2,96,512]{2,1,0:T(8,128)} %get-tuple-element.23.flat_ref, f32[2,96,128]{2,1,0:T(8,128)} %copy-done.5, bf16[256,192]{1,0:T(8,128)(2,1)} %constant.37.clone.az_h, bf16[256,192]{1,0:T(8,128)(2,1)} %constant.38.clone.az_l, bf16[256,512]{1,0:T(8,128)(2,1)} %constant.39.clone.rg_h, ...), custom_call_target="tpu_custom_call" | custom-call | flops 1000000 | bytes 1000000 | tf_op jit(solution)/shard_map/pallas_call | solution.py:28
  66.0 5.5 %all-to-all-start.2 = ((f32[16,8,128]{2,1,0:T(8,128)}), f32[16,8,128]{2,1,0:T(8,128)S(1)}, u32[]{:S(2)}, u32[]{:S(2)}) async-start(f32[16,8,128]{2,1,0:T(8,128)} %shard_map.150), calls=%async_computation.2 | async-start | bytes 131072 | tf_op jit(solution)/shard_map/all_to_all | solution.py:500
  71.4 2.8 %shard_map.151 = (bf16[128,4096]{1,0:T(8,128)(2,1)}, f32[32,4096]{1,0:T(8,128)}, f32[16,128]{1,0:T(8,128)}, f32[16,128]{1,0:T(8,128)}) custom-call(f32[16,32,128]{2,1,0:T(8,128)} %copy-done), custom_call_target="tpu_custom_call" | custom-call | flops 1000000 | bytes 1000000 | tf_op jit(solution)/shard_map/pallas_call | solution.py:28
  74.2 2.3 %collective-permute-start.4 = (f32[16,128]{1,0:T(8,128)}, f32[16,128]{1,0:T(8,128)S(1)}, u32[]{:S(2)}, u32[]{:S(2)}) collective-permute-start(f32[16,128]{1,0:T(8,128)} %get-tuple-element.34), channel_id=1, source_target_pairs={{0,1},{2,3},{4,5},{6,7},{8,9},{10,11},{12,13},{14,15},{16,17},{18,... | collective-permute-start | bytes 24584 | tf_op jit(solution)/shard_map/ppermute | solution.py:575
  76.5 1.8 %all-to-all-done.2.got_ref = f32[16,8,128]{2,1,0:T(8,128)S(1)} async-done(((f32[16,8,128]{2,1,0:T(8,128)}), f32[16,8,128]{2,1,0:T(8,128)S(1)}, u32[]{:S(2)}, u32[]{:S(2)}) %all-to-all-start.2) | async-done | bytes 65568 | tf_op jit(solution)/shard_map/all_to_all | solution.py:500
  78.3 0.6 copy-done.2
  79.0 2.6 %shard_map.152 = (f32[2,16,128]{2,1,0:T(8,128)}, f32[2,16,128]{2,1,0:T(8,128)}) custom-call(f32[16,8,128]{2,1,0:T(8,128)} %copy-done.2, bf16[128,4096]{1,0:T(8,128)(2,1)} %get-tuple-element.29.hot_ref, f32[32,4096]{1,0:T(8,128)} %get-tuple-element.30.row_ref), custom_call_target="tpu_custom_call" | custom-call | flops 1000000 | bytes 1000000 | tf_op jit(solution)/shard_map/pallas_call | solution.py:28
  81.6 1.6 %collective-permute-start.3 = (f32[2,16,128]{2,1,0:T(8,128)}, f32[2,16,128]{2,1,0:T(8,128)S(1)}, u32[]{:S(2)}, u32[]{:S(2)}) collective-permute-start(f32[2,16,128]{2,1,0:T(8,128)} %get-tuple-element.32), channel_id=1, source_target_pairs={{0,1},{2,3},{4,5},{6,7},{8,9},{10,11},{12,13},{14,15},{16,17},{18,... | collective-permute-start | bytes 49160 | tf_op jit(solution)/shard_map/ppermute | solution.py:582
  83.1 0.0 collective-permute-done.4
  83.2 1.0 %collective-permute-done.3 = f32[2,16,128]{2,1,0:T(8,128)S(1)} collective-permute-done((f32[2,16,128]{2,1,0:T(8,128)}, f32[2,16,128]{2,1,0:T(8,128)S(1)}, u32[]{:S(2)}, u32[]{:S(2)}) %collective-permute-start.3) | collective-permute-done | bytes 16416 | tf_op jit(solution)/shard_map/ppermute | solution.py:582
  84.2 0.6 add_divide_fusion
  (14 shorter events, 0.0 us)
Async XLA Ops:
  1.8 7.6 %copy-start.6 = (f32[4,2048]{1,0:T(4,128)S(1)}, f32[4,2048]{1,0:T(4,128)}, u32[]{:S(2)}) copy-start(f32[4,2048]{1,0:T(4,128)} %param.22) | copy-start | bytes 98308
  1.8 18.6 %all-to-all-start = ((f32[16,40,128]{2,1,0:T(8,128)}), f32[16,40,128]{2,1,0:T(8,128)S(1)}, u32[]{:S(2)}, u32[]{:S(2)}) async-start(f32[16,40,128]{2,1,0:T(8,128)} %shard_map.145), calls=%async_computation | async-start | bytes 655360 | tf_op jit(solution)/shard_map/all_to_all | solution.py:500
  20.4 0.7 copy-start.1
  26.0 14.6 %all-to-all-start.1 = ((f32[16,32,128]{2,1,0:T(8,128)}), f32[16,32,128]{2,1,0:T(8,128)S(1)}, u32[]{:S(2)}, u32[]{:S(2)}) async-start(f32[16,32,128]{2,1,0:T(8,128)} %shard_map.147), calls=%async_computation.1 | async-start | bytes 524288 | tf_op jit(solution)/shard_map/all_to_all | solution.py:500
  31.4 9.3 %collective-permute-start = (f32[4,16,512]{2,1,0:T(8,128)}, f32[4,16,512]{2,1,0:T(8,128)S(1)}, u32[]{:S(2)}, u32[]{:S(2)}) collective-permute-start(f32[4,16,512]{2,1,0:T(8,128)} %get-tuple-element.21), channel_id=1, source_target_pairs={{0,2},{2,0},{4,6},{6,4},{8,10},{10,8},{12,14},{14,12},{1,3},{3,1},... | collective-permute-start | bytes 393224 | tf_op jit(solution)/shard_map/ppermute | solution.py:509
  33.2 7.5 %collective-permute-start.1 = (f32[4,16,512]{2,1,0:T(8,128)}, f32[4,16,512]{2,1,0:T(8,128)S(1)}, u32[]{:S(2)}, u32[]{:S(2)}) collective-permute-start(f32[4,16,512]{2,1,0:T(8,128)} %get-tuple-element.22), channel_id=1, source_target_pairs={{2,4},{4,2},{6,8},{8,6},{10,12},{12,10},{3,5},{5,3},{7,9},{9,7},{1... | collective-permute-start | bytes 393224 | tf_op jit(solution)/shard_map/ppermute | solution.py:510
  40.6 0.6 copy-start.3
  40.6 0.7 copy-start.4
  41.3 0.7 copy-start
  54.4 1.5 %collective-permute-start.2 = (f32[2,96,128]{2,1,0:T(8,128)}, f32[2,96,128]{2,1,0:T(8,128)S(1)}, u32[]{:S(2)}, u32[]{:S(2)}) collective-permute-start(f32[2,96,128]{2,1,0:T(8,128)} %get-tuple-element.24), channel_id=1, source_target_pairs={{0,1},{1,0},{2,3},{3,2},{4,5},{5,4},{6,7},{7,6},{8,9},{9,8},{10,11... | collective-permute-start | bytes 294920 | tf_op jit(solution)/shard_map/ppermute | solution.py:543
  56.0 0.6 copy-start.5
  66.0 12.4 %all-to-all-start.2 = ((f32[16,8,128]{2,1,0:T(8,128)}), f32[16,8,128]{2,1,0:T(8,128)S(1)}, u32[]{:S(2)}, u32[]{:S(2)}) async-start(f32[16,8,128]{2,1,0:T(8,128)} %shard_map.150), calls=%async_computation.2 | async-start | bytes 131072 | tf_op jit(solution)/shard_map/all_to_all | solution.py:500
  74.2 8.9 %collective-permute-start.4 = (f32[16,128]{1,0:T(8,128)}, f32[16,128]{1,0:T(8,128)S(1)}, u32[]{:S(2)}, u32[]{:S(2)}) collective-permute-start(f32[16,128]{1,0:T(8,128)} %get-tuple-element.34), channel_id=1, source_target_pairs={{0,1},{2,3},{4,5},{6,7},{8,9},{10,11},{12,13},{14,15},{16,17},{18,... | collective-permute-start | bytes 24584 | tf_op jit(solution)/shard_map/ppermute | solution.py:575
  78.3 0.6 copy-start.2
  79.0 4.2 %copy-start.8 = (f32[16,128]{1,0:T(8,128)S(1)}, f32[16,128]{1,0:T(8,128)}, u32[]{:S(2)}) copy-start(f32[16,128]{1,0:T(8,128)} %get-tuple-element.33) | copy-start | bytes 24580
  81.6 2.6 %copy-start.7 = (f32[2,16,128]{2,1,0:T(8,128)S(1)}, f32[2,16,128]{2,1,0:T(8,128)}, u32[]{:S(2)}) copy-start(f32[2,16,128]{2,1,0:T(8,128)} %get-tuple-element.31) | copy-start | bytes 49156
  81.6 2.6 %collective-permute-start.3 = (f32[2,16,128]{2,1,0:T(8,128)}, f32[2,16,128]{2,1,0:T(8,128)S(1)}, u32[]{:S(2)}, u32[]{:S(2)}) collective-permute-start(f32[2,16,128]{2,1,0:T(8,128)} %get-tuple-element.32), channel_id=1, source_target_pairs={{0,1},{2,3},{4,5},{6,7},{8,9},{10,11},{12,13},{14,15},{16,17},{18,... | collective-permute-start | bytes 49160 | tf_op jit(solution)/shard_map/ppermute | solution.py:582

commit v2 on v1

v2 whole, which is shorter than its diff:
```python
import functools
import math

import jax
import jax.numpy as jnp
import numpy as np
from jax import lax
from jax.experimental import pallas as pl
from jax.experimental.pallas import tpu as pltpu
from jax.sharding import PartitionSpec as P

PATCH = 64
LOOK = 4
EPS = 1e-06
LANES = 128
RIM = PATCH // 4
STEP = PATCH // 2
HALF = PATCH // 2
F32 = jnp.float32
BF16 = jnp.bfloat16
I32 = jnp.int32
VMEM = pltpu.VMEM
VSPEC = pl.BlockSpec(memory_space=pltpu.VMEM)
SSPEC = pl.BlockSpec(memory_space=pltpu.SMEM)


def call(kernel, outs, args, scratch=(), smem=(), grant=16, cost=(1_000_000, 1_000_000)):
    return pl.pallas_call(
        kernel,
        out_shape=outs,
        in_specs=[SSPEC if i in smem else VSPEC for i in range(len(args))],
        out_specs=jax.tree.map(lambda _: VSPEC, outs),
        scratch_shapes=list(scratch),
        compiler_params=pltpu.CompilerParams(vmem_limit_bytes=grant << 20),
        cost_estimate=pl.CostEstimate(flops=cost[0], bytes_accessed=cost[1], transcendentals=0),
    )(*args)


def sds(shape, dtype=F32):
    return jax.ShapeDtypeStruct(shape, dtype)


def split(x):
    hi = x.astype(BF16)
    return hi, (x - hi.astype(F32)).astype(BF16)


def dot(a, b):
    return jnp.dot(a, b, preferred_element_type=F32)


def dot_nt(a, b):
    return lax.dot_general(a, b, (((1,), (1,)), ((), ())), preferred_element_type=F32)


def fetch(pairs, sems):
    copies = [pltpu.make_async_copy(src, dst, sems.at[i]) for i, (src, dst) in enumerate(pairs)]
    for copy in copies:
        copy.start()
    return copies


def lane_iota(shape):
    return lax.broadcasted_iota(I32, shape, len(shape) - 1)


def row_iota(shape):
    return lax.broadcasted_iota(I32, shape, 0)


def roll(x, shift, axis):
    shift = shift % x.shape[axis]
    return x if shift == 0 else pltpu.roll(x, shift, axis)


def lane_gather(row, index):
    return jnp.take_along_axis(jnp.broadcast_to(row, index.shape), index, axis=1)


def host_split(x):
    hi = np.asarray(x, np.float32).astype(BF16)
    lo = (np.asarray(x, np.float64) - hi.astype(np.float64)).astype(BF16)
    return hi, lo


UNROLL = 2


def filter_tables(block_rows):
    turn = 2.0 * math.pi / PATCH
    step = np.arange(PATCH)
    cosine = np.cos(turn * (step[:, None] * step[None, :] % PATCH))
    sine = np.sin(turn * (step[:, None] * step[None, :] % PATCH))
    count = block_rows * PATCH
    az = np.zeros((2 * PATCH, 2 * HALF))
    az[:PATCH, :HALF], az[:PATCH, HALF:] = cosine[:, :HALF], sine[:, :HALF]
    az[PATCH:, :HALF], az[PATCH:, HALF:] = -sine[:, :HALF], cosine[:, :HALF]
    pieces = LANES // HALF
    rg = np.zeros((2 * LANES, pieces * 2 * PATCH))
    for q in range(pieces):
        w = slice(q * HALF, (q + 1) * HALF)
        wi = slice(LANES + q * HALF, LANES + (q + 1) * HALF)
        lr = slice(q * 2 * PATCH, q * 2 * PATCH + PATCH)
        li = slice(q * 2 * PATCH + PATCH, (q + 1) * 2 * PATCH)
        rg[w, lr], rg[wi, lr] = cosine[:HALF], sine[:HALF]
        rg[w, li], rg[wi, li] = -sine[:HALF], cosine[:HALF]
    looks = STEP // LOOK
    core = cosine[RIM : RIM + STEP].reshape(looks, LOOK, PATCH).mean(axis=1)
    core_s = sine[RIM : RIM + STEP].reshape(looks, LOOK, PATCH).mean(axis=1)
    back = np.zeros((2 * block_rows * looks, count))
    for u in range(block_rows):
        k = slice(u * PATCH, (u + 1) * PATCH)
        back[u * looks : (u + 1) * looks, k] = core / PATCH
        back[(block_rows + u) * looks : (block_rows + u + 1) * looks, k] = core_s / PATCH
    c_l, s_l = core.T / PATCH, core_s.T / PATCH
    reps = LANES // looks
    last = np.concatenate(
        [
            np.concatenate([np.tile(c_l, reps), np.tile(s_l, reps)], axis=1),
            np.concatenate([np.tile(-s_l, reps), np.tile(c_l, reps)], axis=1),
            np.concatenate([np.tile(-s_l, reps), np.tile(c_l, reps)], axis=1),
            np.concatenate([np.tile(-c_l, reps), np.tile(-s_l, reps)], axis=1),
        ],
        axis=0,
    )
    return az, rg, back, last


def slice_kernel(width, dem_ref, list_ref, out_ref):
    tiles = out_ref.shape[0]
    lats, lons, _ = dem_ref.shape
    packed = LANES // width
    groups = lats // packed
    slots = list_ref.shape[1]
    lane = lane_iota((lons, LANES))
    listed = list_ref[...].astype(F32)
    for q in range(tiles):
        tile, offset = divmod(q * width, LANES)
        for g in range(groups):
            total = None
            for p in range(packed):
                x = dem_ref[p * groups + g, :, tile * LANES : (tile + 1) * LANES]
                x = roll(x, p * width - offset, 1)
                total = x if total is None else jnp.where(lane // width == p, x, total)
            out_ref[q, g * lons : (g + 1) * lons, :] = total
        out_ref[q, groups * lons : groups * lons + 1, 0:slots] = listed


def halo_kernel(par_ref, image_ref, factor_ref, position_ref, one_ref, two_ref):
    even = par_ref[0] == 0
    lines = factor_ref.shape[0]
    fields = (
        lambda s: image_ref[0, s, :],
        lambda s: image_ref[1, s, :],
        lambda s: factor_ref[s, :],
        lambda s: position_ref[s, :].astype(F32),
    )
    for i, field in enumerate(fields):
        first = field(slice(0, RIM))
        last = field(slice(lines - RIM, lines))
        one_ref[i] = jnp.where(even, last, first)
        two_ref[i] = jnp.where(even, first, last)


def border_sums(n_rg, tiles, values, owner_ref, base_ref, share_ref, w_ref, col_ref, here_ref, next_ref):
    channels = len(values)
    height, width = owner_ref.shape
    base = base_ref[...]
    last_line = jnp.right_shift(base, width.bit_length() - 1) == height - 1
    last_column = jnp.bitwise_and(base, width - 1) == width - 1
    owner = owner_ref[...]
    on_line = jnp.where(last_line, owner, -1)
    on_column = jnp.where(last_column, owner, -1)
    terms = []
    for c, value in enumerate(values):
        for i in range(2):
            spot = (i * channels + c) * tiles
            far = 4 * channels * tiles + spot
            for mask, k, row in ((0, 2, 2 * spot), (0, 3, 2 * spot + tiles), (1, 1, far), (1, 3, far + 2 * channels * tiles)):
                x = share_ref[k] if value is None else share_ref[k] * value
                high = x.astype(BF16).astype(F32)
                terms.append((mask, row, high if i == 0 else x - high))
    tile = row_iota((tiles, width))
    for m in range(height):
        cut = slice(m * width, (m + 1) * width)
        masks = (tile == on_line[m : m + 1], tile == on_column[m : m + 1])
        for mask, row, x in terms:
            w_ref[row : row + tiles, cut] = jnp.where(masks[mask], x[m : m + 1], 0.0).astype(BF16)
    size = channels * tiles
    b = dot_nt(w_ref[0 : 4 * size], col_ref[...])
    b = b[: 2 * size] + b[2 * size :]
    side = dot_nt(w_ref[4 * size : 6 * size], here_ref[...]) + dot_nt(w_ref[6 * size : 8 * size], next_ref[...])
    side = side[:size] + side[size:]
    results = []
    for c in range(channels):
        b0, b1 = b[2 * c * tiles : (2 * c + 1) * tiles], b[(2 * c + 1) * tiles : (2 * c + 2) * tiles]
        dest = row_iota(b0.shape)
        shifted = roll(b1, 1, 1)
        below = roll(b0, n_rg, 0)
        beside = roll(shifted, n_rg, 0)
        diagonal = jnp.where(dest % n_rg > 0, roll(shifted, n_rg + 1, 0), 0.0)
        beside = jnp.where(lane_iota(b0.shape) == 0, diagonal, beside)
        rows = jnp.where(dest >= n_rg, below + beside, 0.0)
        one = side[c * tiles : (c + 1) * tiles]
        one = jnp.concatenate([jnp.zeros((1, one.shape[1]), F32), one[:-1]], axis=0)
        results.append((rows, jnp.where(row_iota(one.shape) % n_rg > 0, one, 0.0)))
    return results


def add_edges(total, edges, channel, first):
    rows, lanes = row_iota(total.shape), lane_iota(total.shape)
    edge, side = edges[first + channel : first + channel + 1], edges[first + 3 : first + 4]
    column = jnp.sum(jnp.where(lanes == rows + channel * total.shape[0], side, 0.0), axis=1, keepdims=True)
    return total + jnp.where(rows == 0, edge, 0.0) + jnp.where(lanes == 0, column, 0.0)


def pack_kernel(n_rg, cap_rows, owner_ref, base_ref, share_ref, early_ref, cell_ref, rim_ref, side_ref, im_ref, in_ref, col_ref, here_ref, next_ref, hot_ref, lhs_ref, w_ref):
    tiles = early_ref.shape[0]
    height, width = owner_ref.shape
    owner = owner_ref[...]
    batch = min(tiles, 16)
    tri = (row_iota((width, width)) < lane_iota((width, width))).astype(BF16)
    ones = jnp.ones((width, width), BF16)
    size = batch * height
    r, c = row_iota((size, size)), lane_iota((size, size))
    lower = ((r // height == c // height) & (c < r)).astype(BF16)
    rank = jnp.zeros((height, width), F32)
    for b in range(tiles // batch):
        hot = jnp.concatenate([(owner == b * batch + o).astype(F32) for o in range(batch)], axis=0)
        hot16 = hot.astype(BF16)
        before = dot(hot16, tri) + dot(lower, dot(hot16, ones).astype(BF16))
        kept = hot * before
        for o in range(batch):
            rank = rank + kept[o * height : (o + 1) * height]
    rank = rank.astype(I32)
    base = base_ref[...]
    shift = width.bit_length() - 1
    column = jnp.bitwise_and(base, width - 1)
    line = jnp.right_shift(base, shift)
    cap = cap_rows * LANES
    for m in range(height):
        cut = slice(m * width, (m + 1) * width)
        hot_ref[:, cut] = (row_iota((cap, width)) == rank[m : m + 1]).astype(F32).astype(BF16)
        col_ref[:, cut] = (row_iota((width, width)) == column[m : m + 1]).astype(F32).astype(BF16)
        mine = row_iota((tiles, width)) == owner[m : m + 1]
        lhs_ref[0:tiles, cut] = mine.astype(F32).astype(BF16)
        lhs_ref[tiles : 2 * tiles, cut] = jnp.where(mine, float(m), 0.0).astype(BF16)
        lhs_ref[2 * tiles :, cut] = jnp.where(mine, lane_iota((tiles, width)).astype(F32), 0.0).astype(BF16)
        at = row_iota((height, width))
        here_ref[:, cut] = (at == line[m : m + 1]).astype(F32).astype(BF16)
        next_ref[:, cut] = (at == line[m : m + 1] + 1).astype(F32).astype(BF16)
    found = dot_nt(lhs_ref[...], hot_ref[...])
    valid = found[0:tiles] > 0.5
    at_m = found[tiles : 2 * tiles].astype(I32)
    at_n = found[2 * tiles :].astype(I32)
    im_ref[...] = at_m
    in_ref[...] = at_n
    cell = base.astype(F32)
    for channel in range(5):
        for k in range(cap_rows):
            cut = slice(k * LANES, (k + 1) * LANES)
            total = jnp.zeros((tiles, LANES), F32)
            for m in range(height):
                row = cell[m : m + 1] if channel == 4 else share_ref[channel, m : m + 1, :]
                total = jnp.where(at_m[:, cut] == m, lane_gather(row, at_n[:, cut]), total)
            total = jnp.where(valid[:, cut], total, 0.0)
            if channel == 4:
                cell_ref[:, cut] = total
            else:
                early_ref[:, channel * cap_rows + k, :] = total
    ((rows, side),) = border_sums(n_rg, tiles, [None], owner_ref, base_ref, share_ref, w_ref, col_ref, here_ref, next_ref)
    rim_ref[...] = rows
    side_ref[...] = side


def request_kernel(n_rg, grid, width, table_rows, slots, got_ref, early_ref, cell_ref, out_ref, turn_ref, list_ref, index_ref, sem):
    tiles, rows, _ = got_ref.shape
    lats, lons = grid
    packed = LANES // width
    groups = lats // packed
    listed = jnp.maximum(got_ref[:, rows - 8, :], 0.0)
    listed = jnp.where(lane_iota(listed.shape) < slots, listed, 0.0).astype(I32)
    lat, lon = listed // (lons * n_rg), listed % (lons * n_rg)
    key = lat // lats * n_rg + lon // lons
    list_ref[0] = key * rows + lat % lats % groups * lons + lon % lons
    list_ref[1] = lat % lats // groups
    (copy,) = fetch(((list_ref, index_ref),), sem)
    for t in range(tiles):
        x = got_ref[t]
        for p in range(packed):
            turn_ref[p, t * rows : (t + 1) * rows, :] = roll(x, p * width, 1)
        out_ref[t, table_rows:, :] = early_ref[t]
    for k in range(cell_ref.shape[1] // LANES):
        x = cell_ref[:, k * LANES : (k + 1) * LANES]
        for i in range(packed):
            place, line = divmod(3 * slots + k * packed + i, table_rows)
            cut = slice(place * width, (place + 1) * width)
            out_ref[:, line, cut] = roll(x, (place - i) * width, 1)[:, cut]
    copy.wait()
    for t in range(tiles):
        for f in range(slots):
            row, piece = index_ref[0, t, f], index_ref[1, t, f]
            for n, dest in ((0, t + n_rg), (1, t), (2, t - n_rg)):
                if 0 <= dest < tiles:
                    place, line = divmod(n * slots + f, table_rows)
                    turn = jnp.bitwise_and(place - piece, packed - 1)
                    put = turn_ref[turn, pl.ds(row, 1), :]
                    cut = slice(place * width, (place + 1) * width)
                    out_ref[dest, line : line + 1, cut] = put[:, cut]


def sincos(x):
    n = jnp.floor(x * (2.0 / math.pi) + 0.5)
    r = x - n * 1.5703125
    r = r - n * 4.837512969970703e-4
    r = r - n * 7.549789954891882e-8
    z = r * r
    s = ((-1.9515295891e-4 * z + 8.3321608736e-3) * z - 1.6666654611e-1) * z * r + r
    c = ((2.443315711809948e-5 * z - 1.388731625493765e-3) * z + 4.166664568298827e-2) * z * z - 0.5 * z + 1.0
    q = n.astype(I32)
    odd = (q & 1) == 1
    sine = jnp.where(odd, c, s)
    cosine = jnp.where(odd, s, c)
    sine = jnp.where((q & 2) == 2, -sine, sine)
    cosine = jnp.where(((q + 1) & 2) == 2, -cosine, cosine)
    return cosine, sine


def flatten_kernel(width, table_rows, slots, par_ref, got_ref, image_ref, factor_ref, position_ref, one_ref, two_ref, flat_ref, edge_ref, tab_ref, in_ref, at_ref):
    even = par_ref[0] == 0
    lines, samples = factor_ref.shape
    packed = LANES // width
    tiles = got_ref.shape[0]
    parts = tiles // packed
    lane = lane_iota((table_rows, LANES))
    for k in range(parts):
        for place in range(packed):
            total = None
            for j in range(packed):
                x = roll(got_ref[k * packed + j, 0:table_rows, :], (j - place) * width, 1)
                total = x if total is None else jnp.where(lane // width == j, x, total)
            tab_ref[k, place * table_rows : (place + 1) * table_rows, :] = total
    for i in range(3):
        top = jnp.where(even, two_ref[i], one_ref[i])
        low = jnp.where(even, one_ref[i], two_ref[i])
        in_ref[i, 0:RIM] = top
        in_ref[i, RIM + lines :] = low
    in_ref[0, RIM : RIM + lines] = image_ref[0]
    in_ref[1, RIM : RIM + lines] = image_ref[1]
    in_ref[2, RIM : RIM + lines] = factor_ref[...]
    at_ref[0:RIM] = jnp.where(even, two_ref[3], one_ref[3]).astype(I32)
    at_ref[RIM : RIM + lines] = position_ref[...]
    at_ref[RIM + lines :] = jnp.where(even, one_ref[3], two_ref[3]).astype(I32)
    pairs = samples // LANES // 2
    steps = (lines + 2 * RIM) // 8 * pairs
    rim_steps = RIM // 8 * pairs
    shift = LANES.bit_length() - 1

    def spots(i):
        start = pl.multiple_of(i // pairs * 8, 8)
        return [(pl.ds(start, 8), pl.ds(pl.multiple_of((i % pairs * 2 + j) * LANES, LANES), LANES)) for j in range(2)]

    def lookup(i):
        base = jnp.where(i < rim_steps, 0, jnp.where(i < steps - rim_steps, slots, 2 * slots))
        at = [at_ref[spot] for spot in spots(i)]
        lanes = [jnp.bitwise_and(x, LANES - 1) for x in at]
        lines_at = [jnp.right_shift(x, shift) for x in at]
        height = [jnp.zeros((8, LANES), F32) for _ in range(2)]
        for f in range(slots):
            for k in range(parts):
                row = jnp.broadcast_to(tab_ref[k, pl.ds(base + f, 1), :], (8, LANES))
                for j in range(2):
                    found = jnp.take_along_axis(row, lanes[j], axis=1)
                    height[j] = jnp.where(lines_at[j] == f * parts + k, found, height[j])
        return tuple(height)

    def finish(i, height):
        for spot, h in zip(spots(i), height):
            cosine, sine = sincos(in_ref[(2, *spot)] * h)
            a, b = in_ref[(0, *spot)], in_ref[(1, *spot)]
            flat_ref[(0, *spot)] = a * cosine + b * sine
            flat_ref[(1, *spot)] = b * cosine - a * sine

    def step(i, height):
        found = lookup(i)
        finish(i - 1, height)
        return found

    finish(steps - 1, lax.fori_loop(1, steps, step, lookup(0)))
    edge = lane_iota((lines + 2 * RIM, LANES))
    for c in range(2):
        first = flat_ref[c, :, 0:LANES]
        last = roll(flat_ref[c, :, samples - LANES : samples], 2 * RIM, 1)
        edge_ref[c] = jnp.where(edge < RIM, first, jnp.where(edge < 2 * RIM, last, 0.0))


def root(x):
    return x * lax.rsqrt(jnp.maximum(x, 1e-37))


def filter_kernel(n_rg, cap_rows, block_rows, rg_ref, flat_ref, edge_ref, rim_ref, side_ref, im_ref, in_ref, owner_ref, base_ref, share_ref, const_ref, col_ref, here_ref, next_ref, out_ref, x_ref, d_ref, s_ref, p_ref, z_ref, look_ref, w_ref):
    _, rows, samples = flat_ref.shape
    cols = samples // LANES
    wide = (cols + 1) * LANES
    lane = lane_iota((HALF, LANES))
    left = rg_ref[0] > 0
    right = rg_ref[0] < n_rg - 1
    strips = rows // HALF
    for p in range(strips):
        for c in range(2):
            cut = slice(p * HALF, (p + 1) * HALF)
            halo = edge_ref[c, cut]
            before = jnp.where(left, roll(halo, -RIM, 1), 0.0)
            after = jnp.where(right, roll(halo, RIM, 1), 0.0)
            for j in range(cols + 1):
                if j < cols:
                    now = roll(flat_ref[c, cut, j * LANES : (j + 1) * LANES], RIM, 1)
                else:
                    now = jnp.where(lane < 2 * RIM, after, 0.0)
                high, low = split(jnp.where(lane < RIM, before, now))
                before = now
                at = slice(p * wide + j * LANES, p * wide + (j + 1) * LANES)
                x_ref[c * HALF : (c + 1) * HALF, at] = high
                x_ref[(2 + c) * HALF : (3 + c) * HALF, at] = low
                x_ref[(4 + c) * HALF : (5 + c) * HALF, at] = high
    looks = block_rows * STEP // LOOK
    tall = [slice(i * 2 * LANES, (i + 1) * 2 * LANES) for i in range(3)]
    rg_h, rg_l = const_ref[tall[0]], const_ref[tall[1]]
    last_h, last_l = const_ref[tall[2], : 2 * LANES], const_ref[tall[2], 2 * LANES :]
    az = const_ref[6 * LANES : 6 * LANES + 2 * PATCH, : 6 * HALF]
    back = const_ref[6 * LANES : 6 * LANES + 4 * looks, 2 * LANES :]
    e = dot(az, x_ref[...])
    count = block_rows * PATCH
    pieces = LANES // HALF
    flip = jnp.where(row_iota((PATCH, LANES)) % 2 == 0, 1.0, -1.0)

    def spectrum(c, j):
        cells = []
        for u in range(block_rows):
            one = e[c * PATCH : (c + 1) * PATCH, u * wide + j * LANES : u * wide + (j + 1) * LANES]
            two = e[c * PATCH : (c + 1) * PATCH, (u + 1) * wide + j * LANES : (u + 1) * wide + (j + 1) * LANES]
            cells.append(one + flip * two)
        return jnp.concatenate(cells, axis=0)

    both = jnp.concatenate(
        [jnp.concatenate([spectrum(0, j), spectrum(1, j)], axis=1) for j in range(cols + 1)], axis=0
    )
    bh, bl = split(both)
    for start, stop, used in ((0, cols, pieces), (cols, cols + 1, 1)):
        span = slice(0, used * 2 * PATCH)
        tall = slice(start * count, stop * count)
        d = dot(bh[tall], rg_h[:, span]) + dot(bl[tall], rg_h[:, span]) + dot(bh[tall], rg_l[:, span])
        for j in range(start, stop):
            for q in range(used):
                d_ref[j * pieces + q] = d[(j - start) * count : (j - start + 1) * count, q * 2 * PATCH : (q + 1) * 2 * PATCH]
    sign = jnp.where(lane_iota((1, LANES)) % 2 == 0, 1.0, -1.0)
    patches = samples // STEP

    @pl.loop(0, patches, unroll=UNROLL)
    def _(v):
        z = d_ref[v] + sign * d_ref[v + 1]
        d_ref[v] = z
        q = z * z
        magnitude = root(q + pltpu.roll(q, PATCH, 1))
        s = magnitude + pltpu.roll(magnitude, 1, 1) + pltpu.roll(magnitude, LANES - 1, 1)
        for u in range(block_rows):
            cut = slice(u * PATCH, (u + 1) * PATCH)
            su = s[cut]
            s_ref[v, cut] = su + pltpu.roll(su, 1, 0) + pltpu.roll(su, PATCH - 1, 0)
            part = magnitude[u * PATCH : u * PATCH + 8]
            for i in range(1, PATCH // 8):
                part = part + magnitude[u * PATCH + 8 * i : u * PATCH + 8 * i + 8]
            p_ref[v, u] = part

    for v in range(patches):
        mean = jnp.sum(p_ref[v], axis=(1, 2), keepdims=True) * (1.0 / (2 * PATCH * PATCH))
        p_ref[v] = jnp.broadcast_to(1.0 / (9.0 * (mean + EPS)), p_ref.shape[1:])

    @pl.loop(0, patches, unroll=UNROLL)
    def _(v):
        at = pl.multiple_of(v * LANES, LANES)
        for u in range(block_rows):
            cut = slice(u * PATCH, (u + 1) * PATCH)
            factor = jnp.concatenate([p_ref[v, u]] * (PATCH // 8), axis=0)
            high, low = split(d_ref[v, cut] * root(s_ref[v, cut] * factor))
            z_ref[cut, pl.ds(at, LANES)] = high
            z_ref[count + u * PATCH : count + (u + 1) * PATCH, pl.ds(at, LANES)] = low

    t = dot(back, z_ref[...])
    t = t[: 2 * looks] + t[2 * looks :]
    stacked = jnp.concatenate(
        [
            jnp.concatenate([t[:looks, v * LANES : (v + 1) * LANES], t[looks:, v * LANES : (v + 1) * LANES]], axis=1)
            for v in range(patches)
        ],
        axis=0,
    )
    sh, sl = split(stacked)
    y = dot(sh, last_h) + dot(sl, last_h) + dot(sh, last_l)
    group = lane_iota((looks, LANES)) // (STEP // LOOK)
    for c in range(2):
        total = jnp.zeros((looks, LANES), F32)
        for v in range(patches):
            part = y[v * looks : (v + 1) * looks, c * LANES : (c + 1) * LANES]
            total = jnp.where(group == v, part, total)
        look_ref[c] = total
    tiles = out_ref.shape[0]
    for k in range(cap_rows):
        cut = slice(k * LANES, (k + 1) * LANES)
        at_m, at_n = im_ref[:, cut], in_ref[:, cut]
        for c in range(2):
            total = jnp.zeros((tiles, LANES), F32)
            for m in range(looks):
                total = jnp.where(at_m == m, lane_gather(look_ref[c, m : m + 1, :], at_n), total)
            out_ref[:, c * cap_rows + k, :] = total
    values = [look_ref[0], look_ref[1]]
    borders = border_sums(n_rg, tiles, values, owner_ref, base_ref, share_ref, w_ref, col_ref, here_ref, next_ref)
    for c, (rows, side) in enumerate(borders):
        out_ref[:, 2 * cap_rows + c, :] = rows
        out_ref[:, 2 * cap_rows + 3, c * looks : (c + 1) * looks] = side
    out_ref[:, 2 * cap_rows + 2, :] = rim_ref[...]
    out_ref[:, 2 * cap_rows + 3, 2 * looks : 3 * looks] = side_ref[...]


def prepare_kernel(cap_rows, table_rows, slots, width, map_lat, got_ref, hot_ref, row_ref, sum_ref):
    tiles = got_ref.shape[0]
    packed = LANES // width
    lane = lane_iota((1, LANES))
    for t in range(tiles):
        for k in range(cap_rows):
            def channel(c):
                return got_ref[t, table_rows + c * cap_rows + k : table_rows + c * cap_rows + k + 1, :]

            cell = None
            for i in range(packed):
                place, spot = divmod(3 * slots + k * packed + i, table_rows)
                x = roll(got_ref[t, spot : spot + 1, :], (i - place) * width, 1)
                cell = x if cell is None else jnp.where(lane // width == i, x, cell)
            cell = cell.astype(I32)
            line, column = jnp.right_shift(cell, LANES.bit_length() - 1), jnp.bitwise_and(cell, LANES - 1)
            at = (t * cap_rows + k) * LANES
            cut = slice(at, at + LANES)
            hot_ref[:, cut] = (row_iota((LANES, LANES)) == column).astype(F32).astype(BF16)
            rows = row_iota((map_lat, LANES))
            here, next_line = rows == line, rows == line + 1
            for d in range(2):
                row_ref[d * map_lat : (d + 1) * map_lat, cut] = jnp.where(here, channel(d), 0.0) + jnp.where(
                    next_line, channel(2 + d), 0.0
                )
    high, low = split(row_ref[...])
    acc = dot_nt(high, hot_ref[...]) + dot_nt(low, hot_ref[...])
    shifted = roll(acc[map_lat:], 1, 1)
    total = acc[:map_lat] + jnp.where(lane_iota(shifted.shape) == 0, 0.0, shifted)
    sum_ref[...] = total


def splat_kernel(cap_rows, map_lat, got_ref, hot_ref, row_ref, weight_ref, out_ref, x_ref):
    tiles = got_ref.shape[0]
    wide = 2 * map_lat
    for t in range(tiles):
        for k in range(cap_rows):
            cut = slice((t * cap_rows + k) * LANES, (t * cap_rows + k + 1) * LANES)
            for c in range(2):
                value = got_ref[t, c * cap_rows + k : c * cap_rows + k + 1, :]
                high, low = split(row_ref[:, cut] * value)
                x_ref[c * wide : (c + 1) * wide, cut] = high
                x_ref[(2 + c) * wide : (3 + c) * wide, cut] = low
    acc = dot_nt(x_ref[...], hot_ref[...])
    acc = acc[: 2 * wide] + acc[2 * wide :]
    edges = got_ref[0]
    for t in range(1, tiles):
        edges = edges + got_ref[t]
    weight = jnp.maximum(add_edges(weight_ref[...], edges, 2, 2 * cap_rows), 1.0)
    for c in range(2):
        shifted = roll(acc[c * wide + map_lat : (c + 1) * wide], 1, 1)
        total = acc[c * wide : c * wide + map_lat] + jnp.where(lane_iota(shifted.shape) == 0, 0.0, shifted)
        out_ref[c] = add_edges(total, edges, c, 2 * cap_rows) / weight


def filter_constants(block_rows):
    az, rg, back, last = filter_tables(block_rows)
    az_h, az_l = host_split(az)
    rg_h, rg_l = host_split(rg)
    back_h, back_l = host_split(back)
    last_h, last_l = host_split(last)
    zero = np.zeros_like(back_l)
    back = np.concatenate([np.concatenate([back_h, back_h], axis=1), np.concatenate([back_l, zero], axis=1)], axis=0)
    final = np.zeros((2 * PATCH, rg_h.shape[1]), BF16)
    final[:, : 6 * HALF] = np.concatenate([az_h, az_h, az_l], axis=1)
    final[: back.shape[0], 2 * LANES : 2 * LANES + back.shape[1]] = back
    return np.concatenate([rg_h, rg_l, np.concatenate([last_h, last_l], axis=1), final], axis=0)


def filter_scratch(rows, samples, block_rows, map_lat, map_lon, tiles):
    patches = samples // STEP
    count = block_rows * PATCH
    return (
        VMEM((6 * HALF, rows // HALF * (samples + LANES)), BF16),
        VMEM((patches + 1, count, 2 * PATCH), F32),
        VMEM((patches, count, 2 * PATCH), F32),
        VMEM((patches, block_rows, 8, LANES), F32),
        VMEM((2 * count, patches * LANES), BF16),
        VMEM((2, map_lat, map_lon), F32),
        VMEM((16 * tiles, map_lat * map_lon), BF16),
    )


def swap_pairs(count, first):
    return [p for i in range(first, count - 1, 2) for p in ((i, i + 1), (i + 1, i))]


def body(image, factor, heights, listing, position, owner, base, shares):
    n_az, n_rg = lax.axis_size("az"), lax.axis_size("rg")
    tiles = n_az * n_rg
    both = ("az", "rg")
    lats, lons, points = heights.shape
    slots = listing.shape[1]
    width = points // tiles
    packed = LANES // width
    lines, samples = factor.shape
    map_lat, map_lon = lines // LOOK, samples // LOOK
    block_rows = lines // STEP
    capacity = 2 * map_lat * map_lon // tiles
    cap_rows = -(-capacity // LANES)
    table_rows = -(-(3 * slots + cap_rows * packed) // packed)
    table_rows = -(-table_rows // 8) * 8
    early_rows = 4 * cap_rows
    late_rows = -(-(2 * cap_rows + 4) // 8) * 8
    slice_rows = lats * lons // packed
    parity = (lax.axis_index("az") % 2).astype(I32).reshape(1)
    rg = lax.axis_index("rg").astype(I32).reshape(1)

    def exchange(x):
        return lax.all_to_all(x, both, split_axis=0, concat_axis=0, tiled=True)

    slices = call(
        functools.partial(slice_kernel, width),
        sds((tiles, slice_rows + 8, LANES)),
        (heights, listing),
        grant=60,
    )
    got_slices = exchange(slices)
    one, two = call(halo_kernel, [sds((4, RIM, samples))] * 2, (parity, image, factor, position), smem=(0,))
    one = lax.ppermute(one, "az", swap_pairs(n_az, 0))
    two = lax.ppermute(two, "az", swap_pairs(n_az, 1))
    total = map_lat * map_lon
    looks_at = (owner.reshape(map_lat, map_lon), base.reshape(map_lat, map_lon), shares.reshape(4, map_lat, map_lon))
    early, cells, rim_sum, side_sum, at_m, at_n, *edges = call(
        functools.partial(pack_kernel, n_rg, cap_rows),
        [
            sds((tiles, early_rows, LANES)),
            sds((tiles, cap_rows * LANES)),
            sds((tiles, map_lon)),
            sds((tiles, map_lat)),
            sds((tiles, cap_rows * LANES), I32),
            sds((tiles, cap_rows * LANES), I32),
            sds((map_lon, total), BF16),
            sds((map_lat, total), BF16),
            sds((map_lat, total), BF16),
        ],
        looks_at,
        scratch=(VMEM((cap_rows * LANES, total), BF16), VMEM((3 * tiles, total), BF16), VMEM((8 * tiles, total), BF16)),
    )
    got_slices, early, one, two = lax.optimization_barrier((got_slices, early, one, two))
    request = call(
        functools.partial(request_kernel, n_rg, (lats, lons), width, table_rows, slots),
        sds((tiles, table_rows + early_rows, LANES)),
        (got_slices, early, cells),
        scratch=(
            VMEM((packed, tiles * (slice_rows + 8), LANES), F32),
            VMEM((2, tiles, LANES), I32),
            pltpu.SMEM((2, tiles, LANES), I32),
            pltpu.SemaphoreType.DMA((1,)),
        ),
    )
    tables = exchange(request)
    flat, edge = call(
        functools.partial(flatten_kernel, width, table_rows, slots),
        [sds((2, lines + 2 * RIM, samples)), sds((2, lines + 2 * RIM, LANES))],
        (parity, tables, image, factor, position, one, two),
        smem=(0,),
        scratch=(
            VMEM((tiles // packed, packed * table_rows, LANES), F32),
            VMEM((3, lines + 2 * RIM, samples), F32),
            VMEM((lines + 2 * RIM, samples), I32),
        ),
    )
    edge = lax.ppermute(edge, "rg", swap_pairs(n_rg, 0))
    rows = lines + 2 * RIM
    patches = samples // STEP
    count = block_rows * PATCH
    packed_looks = call(
        functools.partial(filter_kernel, n_rg, cap_rows, block_rows),
        sds((tiles, late_rows, LANES)),
        (rg, flat, edge, rim_sum, side_sum, at_m, at_n, *looks_at, filter_constants(block_rows), *edges),
        smem=(0,),
        scratch=filter_scratch(rows, samples, block_rows, map_lat, map_lon, tiles),
    )
    got = exchange(packed_looks)
    wide = tiles * cap_rows * LANES
    hot, row_weights, weight_sum = call(
        functools.partial(prepare_kernel, cap_rows, table_rows, slots, width, map_lat),
        [sds((LANES, wide), BF16), sds((2 * map_lat, wide)), sds((map_lat, map_lon))],
        (tables,),
    )
    return call(
        functools.partial(splat_kernel, cap_rows, map_lat),
        sds((2, map_lat, map_lon)),
        (got, hot, row_weights, weight_sum),
        scratch=(VMEM((8 * map_lat, wide), BF16),),
    )


def solution(mesh):
    return jax.shard_map(
        body,
        mesh=mesh,
        in_specs=(
            P(None, ("scene", "az"), "rg"),
            P(("scene", "az"), "rg"),
            P(("scene", "az"), "rg", None),
            P(("scene", "az", "rg"), None),
            P(("scene", "az"), "rg"),
            P(("scene", "az", "rg"), None),
            P(("scene", "az", "rg")),
            P(None, ("scene", "az", "rg")),
        ),
        out_specs=P(None, ("scene", "az"), "rg"),
        check_vma=False,
    )
```

time: 85.5 us -> 61 us (0.71)
  Pallas kernels: 38.7 us -> 18.5 us
  blocking collectives: 0 us -> 14.6 us
  starting transfers between devices: 22.9 us -> 13.7 us
  waiting for transfers between devices: 18.5 us -> 12.9 us
  local copies, waits for them, and re-layouts: 3.38 us -> 0.71 us
  other arithmetic: 1.27 us -> 0 us
    pallas_call x8, Pallas kernels: 38.7 us -> 18.5 us  [call(): pl.pallas_call(kernel, out_shape=outs, in_specs=[SSPEC if i in smem else...]
    all_to_all x0 -> x1, blocking collectives: none -> 14.6 us  [exchange(): return lax.all_to_all(x, both, split_axis=0, concat_axis=0, tiled=True)]
    all_to_all x3 -> x2, starting transfers between devices: 16.5 us -> 11 us  [exchange(): return lax.all_to_all(x, both, split_axis=0, concat_axis=0, tiled=True)]
    ppermute x2 -> x0, starting transfers between devices: 3.87 us -> none  [the longest x1 2.3 us: body(): weight_sum = weight_sum + lax.ppermute(weight_carry, 'rg', right)]
    all_to_all x3 -> x2, waiting for transfers between devices: 9.15 us -> 6.36 us  [exchange(): return lax.all_to_all(x, both, split_axis=0, concat_axis=0, tiled=True)]
    unnamed x19 -> x15, local copies, waits for them, and re-layouts: 3.38 us -> 0.71 us
    ppermute x1, waiting for transfers between devices: 6.8 us -> 5.3 us  [body(): one = lax.ppermute(one, 'az', swap_pairs(n_az, 0))]
    ppermute x2 -> x0, waiting for transfers between devices: 1 us -> none  [the longest x1 1 us: body(): sums = sums + lax.ppermute(carry, 'rg', right)]
  transfers between devices with their start and end apart: 8 -> 5, of which waited for: 5 -> 4; matrix products, arithmetic and copies ran while one was open for 1% -> 0% of each run, Pallas kernels for 12% -> 5%
where the time goes in v2:
time: 61 us; the launch traced here: 60.6 us
  Pallas kernels  18.5 us (30%)
  blocking collectives  14.6 us (24%)
  starting transfers between devices  13.7 us (22%)
  waiting for transfers between devices  12.9 us (21%)
  local copies, waits for them, and re-layouts  0.71 us (1%)
    pallas_call x8, Pallas kernels, call(): pl.pallas_call(kernel, out_shape=outs, in_specs=[SSPEC if i in smem else...  18.5 us
    all_to_all x1, blocking collectives, exchange(): return lax.all_to_all(x, both, split_axis=0, concat_axis=0, tiled=True)  14.6 us
    all_to_all x2, starting transfers between devices, exchange(): return lax.all_to_all(x, both, split_axis=0, concat_axis=0, tiled=True)  11 us
    all_to_all x2, waiting for transfers between devices, exchange(): return lax.all_to_all(x, both, split_axis=0, concat_axis=0, tiled=True)  6.36 us
    ppermute x1, waiting for transfers between devices, body(): one = lax.ppermute(one, 'az', swap_pairs(n_az, 0))  5.3 us
    ppermute x1, starting transfers between devices, body(): one = lax.ppermute(one, 'az', swap_pairs(n_az, 0))  1.97 us
    ppermute x1, waiting for transfers between devices, body(): edge = lax.ppermute(edge, 'rg', swap_pairs(n_rg, 0))  1.28 us
  transfers between devices with their start and end apart: 5, of which 4 were waited for; matrix products, arithmetic and copies ran while one was open for 0% of the time, Pallas kernels for 5%

profile of v2, /device:TPU:0, one launch (start us, length us, event | category | flops | bytes accessed | tf_op | source)
XLA Modules:
  0.0 60.6 jit_solution(17468679928765200033)
XLA Ops:
  0.0 1.8 %shard_map.91 = f32[16,40,128]{2,1,0:T(8,128)} custom-call(f32[8,8,1024]{2,1,0:T(8,128)} %dem_ref.1, s32[1,9]{1,0:T(1,128)} %list_ref.1), custom_call_target="tpu_custom_call" | custom-call | flops 1000000 | bytes 1000000 | tf_op jit(solution)/shard_map/pallas_call | solution.py:28
  1.8 0.0 copy-start
  1.8 0.0 copy-start.2
  1.8 0.0 copy-start.3
  1.8 7.5 %all-to-all-start = ((f32[16,40,128]{2,1,0:T(8,128)}), f32[16,40,128]{2,1,0:T(8,128)S(1)}, u32[]{:S(2)}, u32[]{:S(2)}) async-start(f32[16,40,128]{2,1,0:T(8,128)} %shard_map.91), calls=%async_computation | async-start | bytes 655360 | tf_op jit(solution)/shard_map/all_to_all | solution.py:634
  9.4 0.0 copy-done
  9.4 0.0 copy-done.2
  9.4 0.0 copy-done.3
  9.4 0.0 copy-start.6
  9.5 2.0 %collective-permute-start = (f32[4,16,512]{2,1,0:T(8,128)S(1)}, f32[4,16,512]{2,1,0:T(8,128)S(1)}, u32[]{:S(2)}, u32[]{:S(2)}) collective-permute-start(f32[4,16,512]{2,1,0:T(8,128)S(1)} %get-tuple-element.26), channel_id=1, source_target_pairs={{0,2},{2,0},{4,6},{6,4},{8,10},{10,8},{12,14},{14,12},{1,3},{3,1},... | collective-permute-start | bytes 393224 | tf_op jit(solution)/shard_map/ppermute | solution.py:644
  11.4 0.7 %collective-permute-start.1 = (f32[4,16,512]{2,1,0:T(8,128)S(1)}, f32[4,16,512]{2,1,0:T(8,128)S(1)}, u32[]{:S(2)}, u32[]{:S(2)}) collective-permute-start(f32[4,16,512]{2,1,0:T(8,128)S(1)} %get-tuple-element.27), channel_id=1, source_target_pairs={{2,4},{4,2},{6,8},{8,6},{10,12},{12,10},{3,5},{5,3},{7,9},{9,7},{1... | collective-permute-start | bytes 393224 | tf_op jit(solution)/shard_map/ppermute | solution.py:645
  12.1 0.0 copy-done.6
  12.1 0.0 copy-start.4
  12.1 0.0 copy-start.5
  12.1 0.7 %copy-done.4 = s32[2048,1]{0,1:T(1,128)S(1)} copy-done((s32[2048,1]{0,1:T(1,128)S(1)}, s32[2048,1]{0,1:T(1,128)}, u32[]{:S(2)}) %copy-start.4) | copy-done | bytes 8216
  12.8 0.0 copy-done.5
  12.8 1.8 %shard_map.92 = (f32[16,8,128]{2,1,0:T(8,128)S(1)}, f32[16,256]{1,0:T(8,128)S(1)}, f32[16,128]{1,0:T(8,128)S(1)}, f32[16,16]{1,0:T(8,128)S(1)}, s32[16,256]{1,0:...) custom-call(s32[16,128]{1,0:T(8,128)S(1)} %bitcast.10, ...), custom_call_target="tpu_custom_call" | custom-call | flops 1000000 | bytes 1000000 | tf_op jit(solution)/shard_map/pallas_call | solution.py:28
  14.6 5.3 %collective-permute-done.one_ref = f32[4,16,512]{2,1,0:T(8,128)S(1)} collective-permute-done((f32[4,16,512]{2,1,0:T(8,128)S(1)}, f32[4,16,512]{2,1,0:T(8,128)S(1)}, u32[]{:S(2)}, u32[]{:S(2)}) %collective-permute-start) | collective-permute-done | bytes 131104 | tf_op jit(solution)/shard_map/ppermute | solution.py:644
  19.9 0.0 collective-permute-done.1.two_ref
  19.9 0.5 all-to-all-done.got_ref
  20.4 0.0 copy-start.1
  20.4 1.5 %shard_map.94 = f32[16,24,128]{2,1,0:T(8,128)S(1)} custom-call(f32[16,40,128]{2,1,0:T(8,128)S(1)} %all-to-all-done.got_ref, f32[16,8,128]{2,1,0:T(8,128)S(1)} %get-tuple-element.29.early_ref, f32[16,256]{1,0:T(8,128)S(1)} %get-tuple-element.30.cell_ref), custom_call_target="tpu_custom_call" | custom-call | flops 1000000 | bytes 1000000 | tf_op jit(solution)/shard_map/pallas_call | solution.py:28
  21.9 14.6 %all_to_all.15.got_ref = f32[16,24,128]{2,1,0:T(8,128)S(1)} all-to-all(f32[16,24,128]{2,1,0:T(8,128)S(1)} %shard_map.94), channel_id=1, replica_groups=mesh['scene'=2,'az'=8,'rg'=2] {'az','rg'}, dimensions={0} | all-to-all | bytes 393216 | tf_op jit(solution)/shard_map/all_to_all | solution.py:634
  36.5 6.0 %shard_map.95 = (f32[2,96,512]{2,1,0:T(8,128)S(1)}, f32[2,96,128]{2,1,0:T(8,128)S(1)}) custom-call(s32[1]{0:T(128)} %bitcast.1.par_ref, f32[16,24,128]{2,1,0:T(8,128)S(1)} %all_to_all.15.got_ref, f32[2,64,512]{2,1,0:T(8,128)S(1)} %copy-done, f32[64,512]{1,0:T(8,128)S(1)} %copy-done.2, s32[64,512]{1,0:T(8,128)S(1)} %copy-done.3, ...), custom_call_target="tpu_custom_call" | custom-call | flops 1000000 | bytes 1000000 | tf_op jit(solution)/shard_map/pallas_call | solution.py:28
  42.5 0.1 collective-permute-start.2
  42.6 1.3 %collective-permute-done.2.edge_ref = f32[2,96,128]{2,1,0:T(8,128)S(1)} collective-permute-done((f32[2,96,128]{2,1,0:T(8,128)S(1)}, f32[2,96,128]{2,1,0:T(8,128)S(1)}, u32[]{:S(2)}, u32[]{:S(2)}) %collective-permute-start.2) | collective-permute-done | bytes 98336 | tf_op jit(solution)/shard_map/ppermute | solution.py:688
  43.9 0.0 copy-done.1
  43.9 5.2 %shard_map.96 = f32[16,8,128]{2,1,0:T(8,128)} custom-call(s32[1]{0:T(128)} %bitcast.rg_ref, f32[2,96,512]{2,1,0:T(8,128)S(1)} %get-tuple-element.33.flat_ref, f32[2,96,128]{2,1,0:T(8,128)S(1)} %collective-permute-done.2.edge_ref, f32[16,128]{1,0:T(8,128)S(1)} %get-tuple-element.35.rim_ref, f32[16,16]{1,0:T(8,128)S(1)} %get-tuple-element.36.side_ref, ...), custom_call_target="tpu_custom_call" | custom-call | flops 1000000 | bytes 1000000 | tf_op jit(solution)/shard_map/pallas_call | solution.py:28
  49.1 3.5 %all-to-all-start.2 = ((f32[16,8,128]{2,1,0:T(8,128)}), f32[16,8,128]{2,1,0:T(8,128)S(1)}, u32[]{:S(2)}, u32[]{:S(2)}) async-start(f32[16,8,128]{2,1,0:T(8,128)} %shard_map.96), calls=%async_computation.2 | async-start | bytes 131072 | tf_op jit(solution)/shard_map/all_to_all | solution.py:634
  52.6 1.0 %shard_map.97 = (bf16[128,4096]{1,0:T(8,128)(2,1)S(1)}, f32[32,4096]{1,0:T(8,128)S(1)}, f32[16,128]{1,0:T(8,128)S(1)}) custom-call(f32[16,24,128]{2,1,0:T(8,128)S(1)} %all_to_all.15.got_ref), custom_call_target="tpu_custom_call" | custom-call | flops 1000000 | bytes 1000000 | tf_op jit(solution)/shard_map/pallas_call | solution.py:28
  53.6 5.9 %all-to-all-done.2.got_ref = f32[16,8,128]{2,1,0:T(8,128)S(1)} async-done(((f32[16,8,128]{2,1,0:T(8,128)}), f32[16,8,128]{2,1,0:T(8,128)S(1)}, u32[]{:S(2)}, u32[]{:S(2)}) %all-to-all-start.2) | async-done | bytes 65568 | tf_op jit(solution)/shard_map/all_to_all | solution.py:634
  59.4 1.2 %shard_map.98 = f32[2,16,128]{2,1,0:T(8,128)} custom-call(f32[16,8,128]{2,1,0:T(8,128)S(1)} %all-to-all-done.2.got_ref, bf16[128,4096]{1,0:T(8,128)(2,1)S(1)} %get-tuple-element.42.hot_ref, f32[32,4096]{1,0:T(8,128)S(1)} %get-tuple-element.43.row_ref, f32[16,128]{1,0:T(8,128)S(1)} %get-tuple-element.44.weight_ref), custom_call_target="tpu_custom_call" | custom-call | flops 1000000 | bytes 1000000 | tf_op jit(solution)/shard_map/pallas_call | solution.py:28
  (2 shorter events, 0.0 us)
Async XLA Ops:
  1.8 7.6 %copy-start = (f32[2,64,512]{2,1,0:T(8,128)S(1)}, f32[2,64,512]{2,1,0:T(8,128)}, u32[]{:S(2)}) copy-start(f32[2,64,512]{2,1,0:T(8,128)} %image_ref.3) | copy-start | bytes 786436
  1.8 7.6 %copy-start.2 = (f32[64,512]{1,0:T(8,128)S(1)}, f32[64,512]{1,0:T(8,128)}, u32[]{:S(2)}) copy-start(f32[64,512]{1,0:T(8,128)} %factor_ref.3) | copy-start | bytes 393220
  1.8 7.6 %copy-start.3 = (s32[64,512]{1,0:T(8,128)S(1)}, s32[64,512]{1,0:T(8,128)}, u32[]{:S(2)}) copy-start(s32[64,512]{1,0:T(8,128)} %position_ref.3) | copy-start | bytes 393220
  1.8 18.6 %all-to-all-start = ((f32[16,40,128]{2,1,0:T(8,128)}), f32[16,40,128]{2,1,0:T(8,128)S(1)}, u32[]{:S(2)}, u32[]{:S(2)}) async-start(f32[16,40,128]{2,1,0:T(8,128)} %shard_map.91), calls=%async_computation | async-start | bytes 655360 | tf_op jit(solution)/shard_map/all_to_all | solution.py:634
  9.4 2.7 %copy-start.6 = (f32[4,2048]{1,0:T(4,128)S(1)}, f32[4,2048]{1,0:T(4,128)}, u32[]{:S(2)}) copy-start(f32[4,2048]{1,0:T(4,128)} %param.16) | copy-start | bytes 98308
  9.5 10.5 %collective-permute-start = (f32[4,16,512]{2,1,0:T(8,128)S(1)}, f32[4,16,512]{2,1,0:T(8,128)S(1)}, u32[]{:S(2)}, u32[]{:S(2)}) collective-permute-start(f32[4,16,512]{2,1,0:T(8,128)S(1)} %get-tuple-element.26), channel_id=1, source_target_pairs={{0,2},{2,0},{4,6},{6,4},{8,10},{10,8},{12,14},{14,12},{1,3},{3,1},... | collective-permute-start | bytes 393224 | tf_op jit(solution)/shard_map/ppermute | solution.py:644
  11.4 8.5 %collective-permute-start.1 = (f32[4,16,512]{2,1,0:T(8,128)S(1)}, f32[4,16,512]{2,1,0:T(8,128)S(1)}, u32[]{:S(2)}, u32[]{:S(2)}) collective-permute-start(f32[4,16,512]{2,1,0:T(8,128)S(1)} %get-tuple-element.27), channel_id=1, source_target_pairs={{2,4},{4,2},{6,8},{8,6},{10,12},{12,10},{3,5},{5,3},{7,9},{9,7},{1... | collective-permute-start | bytes 393224 | tf_op jit(solution)/shard_map/ppermute | solution.py:645
  12.1 0.7 %copy-start.4 = (s32[2048,1]{0,1:T(1,128)S(1)}, s32[2048,1]{0,1:T(1,128)}, u32[]{:S(2)}) copy-start(s32[2048,1]{0,1:T(1,128)} %param.14) | copy-start | bytes 24580
  12.1 0.7 %copy-start.5 = (s32[2048]{0:T(1024)S(1)}, s32[2048]{0:T(1024)}, u32[]{:S(2)}) copy-start(s32[2048]{0:T(1024)} %param.15) | copy-start | bytes 24580
  20.4 23.4 %copy-start.1 = (bf16[896,512]{1,0:T(8,128)(2,1)S(1)}, bf16[896,512]{1,0:T(8,128)(2,1)}, u32[]{:S(2)}) copy-start(bf16[896,512]{1,0:T(8,128)(2,1)} %constant.23.clone.const_ref) | copy-start | bytes 2752516
  42.5 1.4 %collective-permute-start.2 = (f32[2,96,128]{2,1,0:T(8,128)S(1)}, f32[2,96,128]{2,1,0:T(8,128)S(1)}, u32[]{:S(2)}, u32[]{:S(2)}) collective-permute-start(f32[2,96,128]{2,1,0:T(8,128)S(1)} %get-tuple-element.34), channel_id=1, source_target_pairs={{0,1},{1,0},{2,3},{3,2},{4,5},{5,4},{6,7},{7,6},{8,9},{9,8},{10,11... | collective-permute-start | bytes 294920 | tf_op jit(solution)/shard_map/ppermute | solution.py:688
  49.1 10.4 %all-to-all-start.2 = ((f32[16,8,128]{2,1,0:T(8,128)}), f32[16,8,128]{2,1,0:T(8,128)S(1)}, u32[]{:S(2)}, u32[]{:S(2)}) async-start(f32[16,8,128]{2,1,0:T(8,128)} %shard_map.96), calls=%async_computation.2 | async-start | bytes 131072 | tf_op jit(solution)/shard_map/all_to_all | solution.py:634

commit v3 on v2

--- a/solution.py
+++ b/solution.py
@@ -8,6 +8,7 @@
 from jax.experimental import pallas as pl
 from jax.experimental.pallas import tpu as pltpu
 from jax.sharding import PartitionSpec as P
+
 
 PATCH = 64
 LOOK = 4
@@ -83,7 +84,7 @@
     return hi, lo
 
 
-UNROLL = 2
+UNROLL = 4
 
 
 def filter_tables(block_rows):
@@ -95,15 +96,12 @@
     az = np.zeros((2 * PATCH, 2 * HALF))
     az[:PATCH, :HALF], az[:PATCH, HALF:] = cosine[:, :HALF], sine[:, :HALF]
     az[PATCH:, :HALF], az[PATCH:, HALF:] = -sine[:, :HALF], cosine[:, :HALF]
-    pieces = LANES // HALF
-    rg = np.zeros((2 * LANES, pieces * 2 * PATCH))
-    for q in range(pieces):
-        w = slice(q * HALF, (q + 1) * HALF)
-        wi = slice(LANES + q * HALF, LANES + (q + 1) * HALF)
-        lr = slice(q * 2 * PATCH, q * 2 * PATCH + PATCH)
-        li = slice(q * 2 * PATCH + PATCH, (q + 1) * 2 * PATCH)
-        rg[w, lr], rg[wi, lr] = cosine[:HALF], sine[:HALF]
-        rg[w, li], rg[wi, li] = -sine[:HALF], cosine[:HALF]
+    rg = np.zeros((2 * LANES, 4 * PATCH))
+    for p in range(2):
+        w, wi = slice(p * HALF, p * HALF + PATCH), slice(LANES + p * HALF, LANES + p * HALF + PATCH)
+        lr, li = slice(p * PATCH, (p + 1) * PATCH), slice(LANES + p * PATCH, LANES + (p + 1) * PATCH)
+        rg[w, lr], rg[wi, lr] = cosine, sine
+        rg[w, li], rg[wi, li] = -sine, cosine
     looks = STEP // LOOK
     core = cosine[RIM : RIM + STEP].reshape(looks, LOOK, PATCH).mean(axis=1)
     core_s = sine[RIM : RIM + STEP].reshape(looks, LOOK, PATCH).mean(axis=1)
@@ -114,15 +112,14 @@
         back[(block_rows + u) * looks : (block_rows + u + 1) * looks, k] = core_s / PATCH
     c_l, s_l = core.T / PATCH, core_s.T / PATCH
     reps = LANES // looks
-    last = np.concatenate(
-        [
-            np.concatenate([np.tile(c_l, reps), np.tile(s_l, reps)], axis=1),
-            np.concatenate([np.tile(-s_l, reps), np.tile(c_l, reps)], axis=1),
-            np.concatenate([np.tile(-s_l, reps), np.tile(c_l, reps)], axis=1),
-            np.concatenate([np.tile(-c_l, reps), np.tile(-s_l, reps)], axis=1),
-        ],
-        axis=0,
-    )
+    patch_of = np.arange(LANES) // looks % 2
+    last = np.zeros((4 * LANES, 2 * LANES))
+    terms = ((c_l, s_l), (-s_l, c_l), (-s_l, c_l), (-c_l, -s_l))
+    for i, (re, im) in enumerate(terms):
+        for p in range(2):
+            k = slice(i * LANES + p * PATCH, i * LANES + (p + 1) * PATCH)
+            last[k, :LANES] = np.tile(re, reps) * (patch_of == p)
+            last[k, LANES:] = np.tile(im, reps) * (patch_of == p)
     return az, rg, back, last
 
 
@@ -162,7 +159,7 @@
         two_ref[i] = jnp.where(even, first, last)
 
 
-def border_sums(n_rg, tiles, values, owner_ref, base_ref, share_ref, w_ref, col_ref, here_ref, next_ref):
+def border_sums(n_rg, tiles, values, owner_ref, base_ref, share_ref, w_ref, term_ref, col_ref, here_ref, next_ref):
     channels = len(values)
     height, width = owner_ref.shape
     base = base_ref[...]
@@ -179,13 +176,14 @@
             for mask, k, row in ((0, 2, 2 * spot), (0, 3, 2 * spot + tiles), (1, 1, far), (1, 3, far + 2 * channels * tiles)):
                 x = share_ref[k] if value is None else share_ref[k] * value
                 high = x.astype(BF16).astype(F32)
-                terms.append((mask, row, high if i == 0 else x - high))
+                term_ref[len(terms)] = high if i == 0 else x - high
+                terms.append((mask, row))
     tile = row_iota((tiles, width))
     for m in range(height):
         cut = slice(m * width, (m + 1) * width)
         masks = (tile == on_line[m : m + 1], tile == on_column[m : m + 1])
-        for mask, row, x in terms:
-            w_ref[row : row + tiles, cut] = jnp.where(masks[mask], x[m : m + 1], 0.0).astype(BF16)
+        for n, (mask, row) in enumerate(terms):
+            w_ref[row : row + tiles, cut] = jnp.where(masks[mask], term_ref[n, m : m + 1, :], 0.0).astype(BF16)
     size = channels * tiles
     b = dot_nt(w_ref[0 : 4 * size], col_ref[...])
     b = b[: 2 * size] + b[2 * size :]
@@ -214,7 +212,7 @@
     return total + jnp.where(rows == 0, edge, 0.0) + jnp.where(lanes == 0, column, 0.0)
 
 
-def pack_kernel(n_rg, cap_rows, owner_ref, base_ref, share_ref, early_ref, cell_ref, rim_ref, side_ref, im_ref, in_ref, col_ref, here_ref, next_ref, hot_ref, lhs_ref, w_ref):
+def pack_kernel(n_rg, cap_rows, owner_ref, base_ref, share_ref, early_ref, cell_ref, rim_ref, side_ref, im_ref, in_ref, col_ref, here_ref, next_ref, hot_ref, lhs_ref, w_ref, term_ref):
     tiles = early_ref.shape[0]
     height, width = owner_ref.shape
     owner = owner_ref[...]
@@ -268,7 +266,7 @@
                 cell_ref[:, cut] = total
             else:
                 early_ref[:, channel * cap_rows + k, :] = total
-    ((rows, side),) = border_sums(n_rg, tiles, [None], owner_ref, base_ref, share_ref, w_ref, col_ref, here_ref, next_ref)
+    ((rows, side),) = border_sums(n_rg, tiles, [None], owner_ref, base_ref, share_ref, w_ref, term_ref, col_ref, here_ref, next_ref)
     rim_ref[...] = rows
     side_ref[...] = side
 
@@ -351,42 +349,42 @@
     at_ref[0:RIM] = jnp.where(even, two_ref[3], one_ref[3]).astype(I32)
     at_ref[RIM : RIM + lines] = position_ref[...]
     at_ref[RIM + lines :] = jnp.where(even, one_ref[3], two_ref[3]).astype(I32)
-    pairs = samples // LANES // 2
-    steps = (lines + 2 * RIM) // 8 * pairs
-    rim_steps = RIM // 8 * pairs
+    W = 1
+    cols = samples // LANES
     shift = LANES.bit_length() - 1
-
-    def spots(i):
-        start = pl.multiple_of(i // pairs * 8, 8)
-        return [(pl.ds(start, 8), pl.ds(pl.multiple_of((i % pairs * 2 + j) * LANES, LANES), LANES)) for j in range(2)]
-
-    def lookup(i):
+    part_bits = parts.bit_length() - 1
+    groups = (lines + 2 * RIM) // 8
+    steps = groups * cols // W
+    rim_steps = RIM // 8 * cols // W
+
+    def step(i):
         base = jnp.where(i < rim_steps, 0, jnp.where(i < steps - rim_steps, slots, 2 * slots))
-        at = [at_ref[spot] for spot in spots(i)]
+        spots = []
+        for j in range(W):
+            n = i * W + j
+            if W >= cols:
+                spots.append((pl.ds(pl.multiple_of((i * (W // cols) + j // cols) * 8, 8), 8), pl.ds(j % cols * LANES, LANES)))
+            else:
+                spots.append((pl.ds(pl.multiple_of(n // cols * 8, 8), 8), pl.ds(pl.multiple_of(n % cols * LANES, LANES), LANES)))
+        at = [at_ref[spot] for spot in spots]
         lanes = [jnp.bitwise_and(x, LANES - 1) for x in at]
-        lines_at = [jnp.right_shift(x, shift) for x in at]
-        height = [jnp.zeros((8, LANES), F32) for _ in range(2)]
+        bits = [[jnp.bitwise_and(x, LANES << b) != 0 for b in range(part_bits)] for x in at]
+        slot = [jnp.right_shift(x, shift + part_bits) for x in at]
+        height = [None] * W
         for f in range(slots):
-            for k in range(parts):
-                row = jnp.broadcast_to(tab_ref[k, pl.ds(base + f, 1), :], (8, LANES))
-                for j in range(2):
-                    found = jnp.take_along_axis(row, lanes[j], axis=1)
-                    height[j] = jnp.where(lines_at[j] == f * parts + k, found, height[j])
-        return tuple(height)
-
-    def finish(i, height):
-        for spot, h in zip(spots(i), height):
+            rows = [jnp.broadcast_to(tab_ref[k, pl.ds(base + f, 1), :], (8, LANES)) for k in range(parts)]
+            for j in range(W):
+                x = [jnp.take_along_axis(row, lanes[j], axis=1) for row in rows]
+                for b in range(part_bits):
+                    x = [jnp.where(bits[j][b], x[n + 1], x[n]) for n in range(0, len(x), 2)]
+                height[j] = x[0] if f == 0 else jnp.where(slot[j] == f, x[0], height[j])
+        for spot, h in zip(spots, height):
             cosine, sine = sincos(in_ref[(2, *spot)] * h)
             a, b = in_ref[(0, *spot)], in_ref[(1, *spot)]
             flat_ref[(0, *spot)] = a * cosine + b * sine
             flat_ref[(1, *spot)] = b * cosine - a * sine
 
-    def step(i, height):
-        found = lookup(i)
-        finish(i - 1, height)
-        return found
-
-    finish(steps - 1, lax.fori_loop(1, steps, step, lookup(0)))
+    pl.loop(0, steps, unroll=16)(step)
     edge = lane_iota((lines + 2 * RIM, LANES))
     for c in range(2):
         first = flat_ref[c, :, 0:LANES]
@@ -398,7 +396,7 @@
     return x * lax.rsqrt(jnp.maximum(x, 1e-37))
 
 
-def filter_kernel(n_rg, cap_rows, block_rows, rg_ref, flat_ref, edge_ref, rim_ref, side_ref, im_ref, in_ref, owner_ref, base_ref, share_ref, const_ref, col_ref, here_ref, next_ref, out_ref, x_ref, d_ref, s_ref, p_ref, z_ref, look_ref, w_ref):
+def filter_kernel(n_rg, cap_rows, block_rows, rg_ref, flat_ref, edge_ref, rim_ref, side_ref, im_ref, in_ref, owner_ref, base_ref, share_ref, const_ref, col_ref, here_ref, next_ref, out_ref, x_ref, y_ref, m_ref, s_ref, p_ref, z_ref, look_ref, w_ref, term_ref):
     _, rows, samples = flat_ref.shape
     cols = samples // LANES
     wide = (cols + 1) * LANES
@@ -424,15 +422,21 @@
                 x_ref[(2 + c) * HALF : (3 + c) * HALF, at] = low
                 x_ref[(4 + c) * HALF : (5 + c) * HALF, at] = high
     looks = block_rows * STEP // LOOK
-    tall = [slice(i * 2 * LANES, (i + 1) * 2 * LANES) for i in range(3)]
-    rg_h, rg_l = const_ref[tall[0]], const_ref[tall[1]]
-    last_h, last_l = const_ref[tall[2], : 2 * LANES], const_ref[tall[2], 2 * LANES :]
-    az = const_ref[6 * LANES : 6 * LANES + 2 * PATCH, : 6 * HALF]
-    back = const_ref[6 * LANES : 6 * LANES + 4 * looks, 2 * LANES :]
+    block = const_ref[...]
+
+    def tripled(at, size):
+        return jnp.concatenate([block[at : at + size], block[at : at + size], block[at + size : at + 2 * size]], axis=0)
+
+    rg3 = tripled(0, 2 * LANES)
+    last3 = tripled(4 * LANES, 4 * LANES)
+    near = jnp.concatenate([block[12 * LANES : 13 * LANES, :LANES]] * 2, axis=0)
+    side = jnp.concatenate([block[12 * LANES : 13 * LANES, LANES:]] * 2, axis=0)
+    az = block[13 * LANES : 13 * LANES + 2 * PATCH, : 6 * HALF]
+    back = block[14 * LANES : 14 * LANES + 4 * looks, : 2 * block_rows * PATCH]
     e = dot(az, x_ref[...])
     count = block_rows * PATCH
-    pieces = LANES // HALF
     flip = jnp.where(row_iota((PATCH, LANES)) % 2 == 0, 1.0, -1.0)
+    half = lane_iota((count, LANES)) < PATCH
 
     def spectrum(c, j):
         cells = []
@@ -442,67 +446,72 @@
             cells.append(one + flip * two)
         return jnp.concatenate(cells, axis=0)
 
-    both = jnp.concatenate(
-        [jnp.concatenate([spectrum(0, j), spectrum(1, j)], axis=1) for j in range(cols + 1)], axis=0
-    )
-    bh, bl = split(both)
-    for start, stop, used in ((0, cols, pieces), (cols, cols + 1, 1)):
-        span = slice(0, used * 2 * PATCH)
-        tall = slice(start * count, stop * count)
-        d = dot(bh[tall], rg_h[:, span]) + dot(bl[tall], rg_h[:, span]) + dot(bh[tall], rg_l[:, span])
-        for j in range(start, stop):
-            for q in range(used):
-                d_ref[j * pieces + q] = d[(j - start) * count : (j - start + 1) * count, q * 2 * PATCH : (q + 1) * 2 * PATCH]
-    sign = jnp.where(lane_iota((1, LANES)) % 2 == 0, 1.0, -1.0)
-    patches = samples // STEP
-
-    @pl.loop(0, patches, unroll=UNROLL)
-    def _(v):
-        z = d_ref[v] + sign * d_ref[v + 1]
-        d_ref[v] = z
-        q = z * z
-        magnitude = root(q + pltpu.roll(q, PATCH, 1))
-        s = magnitude + pltpu.roll(magnitude, 1, 1) + pltpu.roll(magnitude, LANES - 1, 1)
+    parts = []
+    for c in range(2):
+        cells = [spectrum(c, j) for j in range(cols + 1)]
+        turned = [pltpu.roll(x, PATCH, 1) for x in cells]
+        windows = []
+        for j in range(cols):
+            windows += [cells[j], jnp.where(half, turned[j], turned[j + 1])]
+        parts.append(split(jnp.concatenate(windows, axis=0)))
+    (rh, rl), (ih, il) = parts
+    y_ref[...] = dot(jnp.concatenate([rh, ih, rl, il, rh, ih], axis=1), rg3)
+    pairs = 2 * cols
+
+    def measure(w):
+        at = pl.multiple_of(w * count, count)
+        re, im = y_ref[pl.ds(at, count), :LANES], y_ref[pl.ds(at, count), LANES:]
+        magnitude = root(re * re + im * im)
+        high, low = split(magnitude)
+        m_ref[pl.ds(at, count), :LANES] = high
+        m_ref[pl.ds(at, count), LANES:] = low
         for u in range(block_rows):
-            cut = slice(u * PATCH, (u + 1) * PATCH)
-            su = s[cut]
-            s_ref[v, cut] = su + pltpu.roll(su, 1, 0) + pltpu.roll(su, PATCH - 1, 0)
             part = magnitude[u * PATCH : u * PATCH + 8]
             for i in range(1, PATCH // 8):
                 part = part + magnitude[u * PATCH + 8 * i : u * PATCH + 8 * i + 8]
-            p_ref[v, u] = part
-
-    for v in range(patches):
-        mean = jnp.sum(p_ref[v], axis=(1, 2), keepdims=True) * (1.0 / (2 * PATCH * PATCH))
-        p_ref[v] = jnp.broadcast_to(1.0 / (9.0 * (mean + EPS)), p_ref.shape[1:])
-
-    @pl.loop(0, patches, unroll=UNROLL)
-    def _(v):
-        at = pl.multiple_of(v * LANES, LANES)
+            p_ref[pl.ds(pl.multiple_of((w * block_rows + u) * 8, 8), 8), :] = part
+
+    pl.loop(0, pairs, unroll=UNROLL)(measure)
+    s_ref[...] = dot(m_ref[...], near)
+    ph, plow = split(p_ref[...])
+    sums = dot(jnp.concatenate([ph, plow], axis=1), side)
+    for n in range(pairs * block_rows):
+        x = sums[8 * n : 8 * n + 8]
+        for shift in (4, 2, 1):
+            x = x + pltpu.roll(x, shift, 0)
+        p_ref[8 * n : 8 * n + 8, :] = 1.0 / (9.0 * (x * (1.0 / (PATCH * PATCH)) + EPS))
+
+    def weigh(w):
+        at = pl.multiple_of(w * 2 * LANES, 2 * LANES)
         for u in range(block_rows):
-            cut = slice(u * PATCH, (u + 1) * PATCH)
-            factor = jnp.concatenate([p_ref[v, u]] * (PATCH // 8), axis=0)
-            high, low = split(d_ref[v, cut] * root(s_ref[v, cut] * factor))
-            z_ref[cut, pl.ds(at, LANES)] = high
-            z_ref[count + u * PATCH : count + (u + 1) * PATCH, pl.ds(at, LANES)] = low
-
+            cut = pl.ds(pl.multiple_of(w * count + u * PATCH, PATCH), PATCH)
+            su = s_ref[cut, :]
+            su = su + pltpu.roll(su, 1, 0) + pltpu.roll(su, PATCH - 1, 0)
+            factor = p_ref[pl.ds(pl.multiple_of((w * block_rows + u) * 8, 8), 8), :]
+            gain = root(su * jnp.concatenate([factor] * (PATCH // 8), axis=0))
+            for c in range(2):
+                high, low = split(y_ref[cut, c * LANES : (c + 1) * LANES] * gain)
+                span = pl.ds(pl.multiple_of(at + c * LANES, LANES), LANES)
+                z_ref[u * PATCH : (u + 1) * PATCH, span] = high
+                z_ref[count + u * PATCH : count + (u + 1) * PATCH, span] = low
+
+    pl.loop(0, pairs, unroll=UNROLL)(weigh)
     t = dot(back, z_ref[...])
     t = t[: 2 * looks] + t[2 * looks :]
     stacked = jnp.concatenate(
         [
-            jnp.concatenate([t[:looks, v * LANES : (v + 1) * LANES], t[looks:, v * LANES : (v + 1) * LANES]], axis=1)
-            for v in range(patches)
+            jnp.concatenate([t[i * looks : (i + 1) * looks, w * 2 * LANES : (w + 1) * 2 * LANES] for i in range(2)], axis=1)
+            for w in range(pairs)
         ],
         axis=0,
     )
     sh, sl = split(stacked)
-    y = dot(sh, last_h) + dot(sl, last_h) + dot(sh, last_l)
-    group = lane_iota((looks, LANES)) // (STEP // LOOK)
+    y = dot(jnp.concatenate([sh, sl, sh], axis=1), last3)
+    group = lane_iota((looks, LANES)) // (2 * STEP // LOOK)
     for c in range(2):
         total = jnp.zeros((looks, LANES), F32)
-        for v in range(patches):
-            part = y[v * looks : (v + 1) * looks, c * LANES : (c + 1) * LANES]
-            total = jnp.where(group == v, part, total)
+        for w in range(pairs):
+            total = jnp.where(group == w, y[w * looks : (w + 1) * looks, c * LANES : (c + 1) * LANES], total)
         look_ref[c] = total
     tiles = out_ref.shape[0]
     for k in range(cap_rows):
@@ -514,7 +523,7 @@
                 total = jnp.where(at_m == m, lane_gather(look_ref[c, m : m + 1, :], at_n), total)
             out_ref[:, c * cap_rows + k, :] = total
     values = [look_ref[0], look_ref[1]]
-    borders = border_sums(n_rg, tiles, values, owner_ref, base_ref, share_ref, w_ref, col_ref, here_ref, next_ref)
+    borders = border_sums(n_rg, tiles, values, owner_ref, base_ref, share_ref, w_ref, term_ref, col_ref, here_ref, next_ref)
     for c, (rows, side) in enumerate(borders):
         out_ref[:, 2 * cap_rows + c, :] = rows
         out_ref[:, 2 * cap_rows + 3, c * looks : (c + 1) * looks] = side
@@ -584,11 +593,18 @@
     back_h, back_l = host_split(back)
     last_h, last_l = host_split(last)
     zero = np.zeros_like(back_l)
-    back = np.concatenate([np.concatenate([back_h, back_h], axis=1), np.concatenate([back_l, zero], axis=1)], axis=0)
-    final = np.zeros((2 * PATCH, rg_h.shape[1]), BF16)
-    final[:, : 6 * HALF] = np.concatenate([az_h, az_h, az_l], axis=1)
-    final[: back.shape[0], 2 * LANES : 2 * LANES + back.shape[1]] = back
-    return np.concatenate([rg_h, rg_l, np.concatenate([last_h, last_l], axis=1), final], axis=0)
+    lane = np.arange(LANES)
+    same = lane[:, None] // PATCH == lane[None, :] // PATCH
+    apart = (lane[:, None] - lane[None, :]) % PATCH
+    near = (same & ((apart <= 1) | (apart == PATCH - 1))).astype(BF16)
+    blocks = (
+        np.concatenate([rg_h, rg_l], axis=0),
+        np.concatenate([last_h, last_l], axis=0),
+        np.concatenate([near, same.astype(BF16)], axis=1),
+        np.concatenate([az_h, az_h, az_l], axis=1),
+        np.concatenate([np.concatenate([back_h, back_h], axis=1), np.concatenate([back_l, zero], axis=1)], axis=0),
+    )
+    return np.concatenate([np.pad(b, ((0, 0), (0, 2 * LANES - b.shape[1]))) for b in blocks], axis=0)
 
 
 def filter_scratch(rows, samples, block_rows, map_lat, map_lon, tiles):
@@ -596,12 +612,14 @@
     count = block_rows * PATCH
     return (
         VMEM((6 * HALF, rows // HALF * (samples + LANES)), BF16),
-        VMEM((patches + 1, count, 2 * PATCH), F32),
-        VMEM((patches, count, 2 * PATCH), F32),
-        VMEM((patches, block_rows, 8, LANES), F32),
+        VMEM((patches // 2 * count, 2 * LANES), F32),
+        VMEM((patches // 2 * count, 2 * LANES), BF16),
+        VMEM((patches // 2 * count, LANES), F32),
+        VMEM((patches // 2 * block_rows * 8, LANES), F32),
         VMEM((2 * count, patches * LANES), BF16),
         VMEM((2, map_lat, map_lon), F32),
         VMEM((16 * tiles, map_lat * map_lon), BF16),
+        VMEM((16, map_lat, map_lon), F32),
     )
 
 
@@ -609,7 +627,7 @@
     return [p for i in range(first, count - 1, 2) for p in ((i, i + 1), (i + 1, i))]
 
 
-def body(image, factor, heights, listing, position, owner, base, shares):
+def scene(image, factor, heights, listing, position, owner, base, shares):
     n_az, n_rg = lax.axis_size("az"), lax.axis_size("rg")
     tiles = n_az * n_rg
     both = ("az", "rg")
@@ -659,9 +677,8 @@
             sds((map_lat, total), BF16),
         ],
         looks_at,
-        scratch=(VMEM((cap_rows * LANES, total), BF16), VMEM((3 * tiles, total), BF16), VMEM((8 * tiles, total), BF16)),
-    )
-    got_slices, early, one, two = lax.optimization_barrier((got_slices, early, one, two))
+        scratch=(VMEM((cap_rows * LANES, total), BF16), VMEM((3 * tiles, total), BF16), VMEM((8 * tiles, total), BF16), VMEM((8, map_lat, map_lon), F32)),
+    )
     request = call(
         functools.partial(request_kernel, n_rg, (lats, lons), width, table_rows, slots),
         sds((tiles, table_rows + early_rows, LANES)),
@@ -687,8 +704,6 @@
     )
     edge = lax.ppermute(edge, "rg", swap_pairs(n_rg, 0))
     rows = lines + 2 * RIM
-    patches = samples // STEP
-    count = block_rows * PATCH
     packed_looks = call(
         functools.partial(filter_kernel, n_rg, cap_rows, block_rows),
         sds((tiles, late_rows, LANES)),
@@ -713,7 +728,7 @@
 
 def solution(mesh):
     return jax.shard_map(
-        body,
+        scene,
         mesh=mesh,
         in_specs=(
             P(None, ("scene", "az"), "rg"),

time: 61 us -> 60.5 us (level)
  blocking collectives: 14.6 us -> 0 us
  waiting for transfers between devices: 12.9 us -> 22.4 us
  starting transfers between devices: 13.7 us -> 19.9 us
  Pallas kernels: 18.5 us -> 16.8 us
    all_to_all x1 -> x0, blocking collectives: 14.6 us -> none  [exchange(): return lax.all_to_all(x, both, split_axis=0, concat_axis=0, tiled=True)]
    all_to_all x2 -> x3, waiting for transfers between devices: 6.36 us -> 14.4 us  [exchange(): return lax.all_to_all(x, both, split_axis=0, concat_axis=0, tiled=True)]
    all_to_all x2 -> x3, starting transfers between devices: 11 us -> 17.3 us  [exchange(): return lax.all_to_all(x, both, split_axis=0, concat_axis=0, tiled=True)]
    pallas_call x8, Pallas kernels: 18.5 us -> 16.8 us  [call(): pl.pallas_call(kernel, out_shape=outs, in_specs=[SSPEC if i in smem else...]
    ppermute x3, waiting for transfers between devices: 6.58 us -> 8 us  [the longest x1 6.71 us: scene(): one = lax.ppermute(one, 'az', swap_pairs(n_az, 0))]
  transfers between devices with their start and end apart: 5 -> 6, of which waited for: 4 -> 4; matrix products, arithmetic and copies ran while one was open for 0% -> 0% of each run, Pallas kernels for 5% -> 5%
where the time goes in v3:
time: 60.5 us; the launch traced here: 60 us
  waiting for transfers between devices  22.4 us (37%)
  starting transfers between devices  19.9 us (33%)
  Pallas kernels  16.8 us (28%)
  local copies, waits for them, and re-layouts  0.72 us (1%)
    all_to_all x3, starting transfers between devices, exchange(): return lax.all_to_all(x, both, split_axis=0, concat_axis=0, tiled=True)  17.3 us
    pallas_call x8, Pallas kernels, call(): pl.pallas_call(kernel, out_shape=outs, in_specs=[SSPEC if i in smem else...  16.8 us
    all_to_all x3, waiting for transfers between devices, exchange(): return lax.all_to_all(x, both, split_axis=0, concat_axis=0, tiled=True)  14.4 us
    ppermute x1, waiting for transfers between devices, scene(): one = lax.ppermute(one, 'az', swap_pairs(n_az, 0))  6.71 us
    ppermute x1, starting transfers between devices, scene(): one = lax.ppermute(one, 'az', swap_pairs(n_az, 0))  1.86 us
    ppermute x1, waiting for transfers between devices, scene(): edge = lax.ppermute(edge, 'rg', swap_pairs(n_rg, 0))  1.28 us
  transfers between devices with their start and end apart: 6, of which 4 were waited for; matrix products, arithmetic and copies ran while one was open for 0% of the time, Pallas kernels for 5%

profile of v3, /device:TPU:0, one launch (start us, length us, event | category | flops | bytes accessed | tf_op | source)
XLA Modules:
  0.0 60.0 jit_solution(2456833673580606283)
XLA Ops:
  0.0 1.8 %shard_map.91 = f32[16,40,128]{2,1,0:T(8,128)} custom-call(f32[8,8,1024]{2,1,0:T(8,128)} %dem_ref.1, s32[1,9]{1,0:T(1,128)} %list_ref.1), custom_call_target="tpu_custom_call" | custom-call | flops 1000000 | bytes 1000000 | tf_op jit(solution)/shard_map/pallas_call | solution.py:29
  1.8 0.0 copy-start.6
  1.8 7.5 %all-to-all-start = ((f32[16,40,128]{2,1,0:T(8,128)}), f32[16,40,128]{2,1,0:T(8,128)S(1)}, u32[]{:S(2)}, u32[]{:S(2)}) async-start(f32[16,40,128]{2,1,0:T(8,128)} %shard_map.91), calls=%async_computation | async-start | bytes 655360 | tf_op jit(solution)/shard_map/all_to_all | solution.py:652
  9.4 0.0 copy-done.6
  9.4 0.0 copy-start.4
  9.4 0.0 copy-start.5
  9.4 0.7 %copy-done.4 = s32[2048,1]{0,1:T(1,128)S(1)} copy-done((s32[2048,1]{0,1:T(1,128)S(1)}, s32[2048,1]{0,1:T(1,128)}, u32[]{:S(2)}) %copy-start.4) | copy-done | bytes 8216
  10.1 0.0 copy-done.5
  10.1 1.8 %shard_map.92 = (f32[16,8,128]{2,1,0:T(8,128)S(1)}, f32[16,256]{1,0:T(8,128)S(1)}, f32[16,128]{1,0:T(8,128)S(1)}, f32[16,16]{1,0:T(8,128)S(1)}, s32[16,256]{1,0:...) custom-call(s32[16,128]{1,0:T(8,128)S(1)} %bitcast.10, ...), custom_call_target="tpu_custom_call" | custom-call | flops 1000000 | bytes 1000000 | tf_op jit(solution)/shard_map/pallas_call | solution.py:29
  11.9 8.5 %all-to-all-done.got_ref = f32[16,40,128]{2,1,0:T(8,128)S(1)} async-done(((f32[16,40,128]{2,1,0:T(8,128)}), f32[16,40,128]{2,1,0:T(8,128)S(1)}, u32[]{:S(2)}, u32[]{:S(2)}) %all-to-all-start) | async-done | bytes 327712 | tf_op jit(solution)/shard_map/all_to_all | solution.py:652
  20.4 0.0 copy-start.2
  20.4 2.1 %shard_map.93 = f32[16,24,128]{2,1,0:T(8,128)} custom-call(f32[16,40,128]{2,1,0:T(8,128)S(1)} %all-to-all-done.got_ref, f32[16,8,128]{2,1,0:T(8,128)S(1)} %get-tuple-element.21.early_ref, f32[16,256]{1,0:T(8,128)S(1)} %get-tuple-element.22.cell_ref), custom_call_target="tpu_custom_call" | custom-call | flops 1000000 | bytes 1000000 | tf_op jit(solution)/shard_map/pallas_call | solution.py:29
  22.6 0.0 copy-start
  22.6 0.0 copy-start.1
  22.6 3.7 %all-to-all-start.1 = ((f32[16,24,128]{2,1,0:T(8,128)}), f32[16,24,128]{2,1,0:T(8,128)S(1)}, u32[]{:S(2)}, u32[]{:S(2)}) async-start(f32[16,24,128]{2,1,0:T(8,128)} %shard_map.93), calls=%async_computation.1 | async-start | bytes 393216 | tf_op jit(solution)/shard_map/all_to_all | solution.py:652
  26.3 0.0 copy-done.2
  26.3 0.0 copy-done.3
  26.3 0.0 copy-done
  26.4 1.9 %collective-permute-start = (f32[4,16,512]{2,1,0:T(8,128)S(1)}, f32[4,16,512]{2,1,0:T(8,128)S(1)}, u32[]{:S(2)}, u32[]{:S(2)}) collective-permute-start(f32[4,16,512]{2,1,0:T(8,128)S(1)} %get-tuple-element.23), channel_id=1, source_target_pairs={{0,2},{2,0},{4,6},{6,4},{8,10},{10,8},{12,14},{14,12},{1,3},{3,1},... | collective-permute-start | bytes 393224 | tf_op jit(solution)/shard_map/ppermute | solution.py:662
  28.2 0.7 %collective-permute-start.1 = (f32[4,16,512]{2,1,0:T(8,128)S(1)}, f32[4,16,512]{2,1,0:T(8,128)S(1)}, u32[]{:S(2)}, u32[]{:S(2)}) collective-permute-start(f32[4,16,512]{2,1,0:T(8,128)S(1)} %get-tuple-element.24), channel_id=1, source_target_pairs={{2,4},{4,2},{6,8},{8,6},{10,12},{12,10},{3,5},{5,3},{7,9},{9,7},{1... | collective-permute-start | bytes 393224 | tf_op jit(solution)/shard_map/ppermute | solution.py:663
  28.9 6.7 %collective-permute-done.one_ref = f32[4,16,512]{2,1,0:T(8,128)S(1)} collective-permute-done((f32[4,16,512]{2,1,0:T(8,128)S(1)}, f32[4,16,512]{2,1,0:T(8,128)S(1)}, u32[]{:S(2)}, u32[]{:S(2)}) %collective-permute-start) | collective-permute-done | bytes 131104 | tf_op jit(solution)/shard_map/ppermute | solution.py:662
  35.6 0.0 collective-permute-done.1.two_ref
  35.6 0.0 all-to-all-done.1.got_ref
  35.6 4.4 %shard_map.95 = (f32[2,96,512]{2,1,0:T(8,128)S(1)}, f32[2,96,128]{2,1,0:T(8,128)S(1)}) custom-call(s32[1]{0:T(128)} %bitcast.1.par_ref, f32[16,24,128]{2,1,0:T(8,128)S(1)} %all-to-all-done.1.got_ref, f32[2,64,512]{2,1,0:T(8,128)S(1)} %copy-done, f32[64,512]{1,0:T(8,128)S(1)} %copy-done.2, s32[64,512]{1,0:T(8,128)S(1)} %copy-done.3, ...), custom_call_target="tpu_custom_call" | custom-call | flops 1000000 | bytes 1000000 | tf_op jit(solution)/shard_map/pallas_call | solution.py:29
  40.0 0.1 collective-permute-start.2
  40.1 1.3 %collective-permute-done.2.edge_ref = f32[2,96,128]{2,1,0:T(8,128)S(1)} collective-permute-done((f32[2,96,128]{2,1,0:T(8,128)S(1)}, f32[2,96,128]{2,1,0:T(8,128)S(1)}, u32[]{:S(2)}, u32[]{:S(2)}) %collective-permute-start.2) | collective-permute-done | bytes 98336 | tf_op jit(solution)/shard_map/ppermute | solution.py:705
  41.4 0.0 copy-done.1
  41.4 4.4 %shard_map.96 = f32[16,8,128]{2,1,0:T(8,128)} custom-call(s32[1]{0:T(128)} %bitcast.rg_ref, f32[2,96,512]{2,1,0:T(8,128)S(1)} %get-tuple-element.25.flat_ref, f32[2,96,128]{2,1,0:T(8,128)S(1)} %collective-permute-done.2.edge_ref, f32[16,128]{1,0:T(8,128)S(1)} %get-tuple-element.27.rim_ref, f32[16,16]{1,0:T(8,128)S(1)} %get-tuple-element.28.side_ref, ...), custom_call_target="tpu_custom_call" | custom-call | flops 1000000 | bytes 1000000 | tf_op jit(solution)/shard_map/pallas_call | solution.py:29
  45.8 6.1 %all-to-all-start.2 = ((f32[16,8,128]{2,1,0:T(8,128)}), f32[16,8,128]{2,1,0:T(8,128)S(1)}, u32[]{:S(2)}, u32[]{:S(2)}) async-start(f32[16,8,128]{2,1,0:T(8,128)} %shard_map.96), calls=%async_computation.2 | async-start | bytes 131072 | tf_op jit(solution)/shard_map/all_to_all | solution.py:652
  52.0 1.0 %shard_map.97 = (bf16[128,4096]{1,0:T(8,128)(2,1)S(1)}, f32[32,4096]{1,0:T(8,128)S(1)}, f32[16,128]{1,0:T(8,128)S(1)}) custom-call(f32[16,24,128]{2,1,0:T(8,128)S(1)} %all-to-all-done.1.got_ref), custom_call_target="tpu_custom_call" | custom-call | flops 1000000 | bytes 1000000 | tf_op jit(solution)/shard_map/pallas_call | solution.py:29
  52.9 5.9 %all-to-all-done.2.got_ref = f32[16,8,128]{2,1,0:T(8,128)S(1)} async-done(((f32[16,8,128]{2,1,0:T(8,128)}), f32[16,8,128]{2,1,0:T(8,128)S(1)}, u32[]{:S(2)}, u32[]{:S(2)}) %all-to-all-start.2) | async-done | bytes 65568 | tf_op jit(solution)/shard_map/all_to_all | solution.py:652
  58.9 1.2 %shard_map.98 = f32[2,16,128]{2,1,0:T(8,128)} custom-call(f32[16,8,128]{2,1,0:T(8,128)S(1)} %all-to-all-done.2.got_ref, bf16[128,4096]{1,0:T(8,128)(2,1)S(1)} %get-tuple-element.34.hot_ref, f32[32,4096]{1,0:T(8,128)S(1)} %get-tuple-element.35.row_ref, f32[16,128]{1,0:T(8,128)S(1)} %get-tuple-element.36.weight_ref), custom_call_target="tpu_custom_call" | custom-call | flops 1000000 | bytes 1000000 | tf_op jit(solution)/shard_map/pallas_call | solution.py:29
  (3 shorter events, 0.0 us)
Async XLA Ops:
  1.8 7.6 %copy-start.6 = (f32[4,2048]{1,0:T(4,128)S(1)}, f32[4,2048]{1,0:T(4,128)}, u32[]{:S(2)}) copy-start(f32[4,2048]{1,0:T(4,128)} %param.16) | copy-start | bytes 98308
  1.8 18.6 %all-to-all-start = ((f32[16,40,128]{2,1,0:T(8,128)}), f32[16,40,128]{2,1,0:T(8,128)S(1)}, u32[]{:S(2)}, u32[]{:S(2)}) async-start(f32[16,40,128]{2,1,0:T(8,128)} %shard_map.91), calls=%async_computation | async-start | bytes 655360 | tf_op jit(solution)/shard_map/all_to_all | solution.py:652
  9.4 0.7 %copy-start.4 = (s32[2048,1]{0,1:T(1,128)S(1)}, s32[2048,1]{0,1:T(1,128)}, u32[]{:S(2)}) copy-start(s32[2048,1]{0,1:T(1,128)} %param.14) | copy-start | bytes 24580
  9.4 0.7 %copy-start.5 = (s32[2048]{0:T(1024)S(1)}, s32[2048]{0:T(1024)}, u32[]{:S(2)}) copy-start(s32[2048]{0:T(1024)} %param.15) | copy-start | bytes 24580
  20.4 5.9 %copy-start.2 = (f32[64,512]{1,0:T(8,128)S(1)}, f32[64,512]{1,0:T(8,128)}, u32[]{:S(2)}) copy-start(f32[64,512]{1,0:T(8,128)} %factor_ref.3) | copy-start | bytes 393220
  20.4 5.9 %copy-start.3 = (s32[64,512]{1,0:T(8,128)S(1)}, s32[64,512]{1,0:T(8,128)}, u32[]{:S(2)}) copy-start(s32[64,512]{1,0:T(8,128)} %position_ref.3) | copy-start | bytes 393220
  22.6 3.7 %copy-start = (f32[2,64,512]{2,1,0:T(8,128)S(1)}, f32[2,64,512]{2,1,0:T(8,128)}, u32[]{:S(2)}) copy-start(f32[2,64,512]{2,1,0:T(8,128)} %image_ref.3) | copy-start | bytes 786436
  22.6 18.8 %copy-start.1 = (bf16[1856,256]{1,0:T(8,128)(2,1)S(1)}, bf16[1856,256]{1,0:T(8,128)(2,1)}, u32[]{:S(2)}) copy-start(bf16[1856,256]{1,0:T(8,128)(2,1)} %constant.23.clone.const_ref) | copy-start | bytes 2850820
  22.6 13.0 %all-to-all-start.1 = ((f32[16,24,128]{2,1,0:T(8,128)}), f32[16,24,128]{2,1,0:T(8,128)S(1)}, u32[]{:S(2)}, u32[]{:S(2)}) async-start(f32[16,24,128]{2,1,0:T(8,128)} %shard_map.93), calls=%async_computation.1 | async-start | bytes 393216 | tf_op jit(solution)/shard_map/all_to_all | solution.py:652
  26.4 9.2 %collective-permute-start = (f32[4,16,512]{2,1,0:T(8,128)S(1)}, f32[4,16,512]{2,1,0:T(8,128)S(1)}, u32[]{:S(2)}, u32[]{:S(2)}) collective-permute-start(f32[4,16,512]{2,1,0:T(8,128)S(1)} %get-tuple-element.23), channel_id=1, source_target_pairs={{0,2},{2,0},{4,6},{6,4},{8,10},{10,8},{12,14},{14,12},{1,3},{3,1},... | collective-permute-start | bytes 393224 | tf_op jit(solution)/shard_map/ppermute | solution.py:662
  28.2 7.4 %collective-permute-start.1 = (f32[4,16,512]{2,1,0:T(8,128)S(1)}, f32[4,16,512]{2,1,0:T(8,128)S(1)}, u32[]{:S(2)}, u32[]{:S(2)}) collective-permute-start(f32[4,16,512]{2,1,0:T(8,128)S(1)} %get-tuple-element.24), channel_id=1, source_target_pairs={{2,4},{4,2},{6,8},{8,6},{10,12},{12,10},{3,5},{5,3},{7,9},{9,7},{1... | collective-permute-start | bytes 393224 | tf_op jit(solution)/shard_map/ppermute | solution.py:663
  40.0 1.4 %collective-permute-start.2 = (f32[2,96,128]{2,1,0:T(8,128)S(1)}, f32[2,96,128]{2,1,0:T(8,128)S(1)}, u32[]{:S(2)}, u32[]{:S(2)}) collective-permute-start(f32[2,96,128]{2,1,0:T(8,128)S(1)} %get-tuple-element.26), channel_id=1, source_target_pairs={{0,1},{1,0},{2,3},{3,2},{4,5},{5,4},{6,7},{7,6},{8,9},{9,8},{10,11... | collective-permute-start | bytes 294920 | tf_op jit(solution)/shard_map/ppermute | solution.py:705
  45.8 13.0 %all-to-all-start.2 = ((f32[16,8,128]{2,1,0:T(8,128)}), f32[16,8,128]{2,1,0:T(8,128)S(1)}, u32[]{:S(2)}, u32[]{:S(2)}) async-start(f32[16,8,128]{2,1,0:T(8,128)} %shard_map.96), calls=%async_computation.2 | async-start | bytes 131072 | tf_op jit(solution)/shard_map/all_to_all | solution.py:652

commit v4 on v3

--- a/solution.py
+++ b/solution.py
@@ -82,9 +82,6 @@
     hi = np.asarray(x, np.float32).astype(BF16)
     lo = (np.asarray(x, np.float64) - hi.astype(np.float64)).astype(BF16)
     return hi, lo
-
-
-UNROLL = 4
 
 
 def filter_tables(block_rows):
@@ -280,13 +277,15 @@
     listed = jnp.where(lane_iota(listed.shape) < slots, listed, 0.0).astype(I32)
     lat, lon = listed // (lons * n_rg), listed % (lons * n_rg)
     key = lat // lats * n_rg + lon // lons
-    list_ref[0] = key * rows + lat % lats % groups * lons + lon % lons
-    list_ref[1] = lat % lats // groups
+    row, piece = key * rows + lat % lats % groups * lons + lon % lons, lat % lats // groups
+    for place in range(packed):
+        list_ref[place] = jnp.bitwise_and(place - piece, packed - 1) * (tiles * rows) + row
     (copy,) = fetch(((list_ref, index_ref),), sem)
     for t in range(tiles):
         x = got_ref[t]
         for p in range(packed):
-            turn_ref[p, t * rows : (t + 1) * rows, :] = roll(x, p * width, 1)
+            at = (p * tiles + t) * rows
+            turn_ref[at : at + rows, :] = roll(x, p * width, 1)
         out_ref[t, table_rows:, :] = early_ref[t]
     for k in range(cell_ref.shape[1] // LANES):
         x = cell_ref[:, k * LANES : (k + 1) * LANES]
@@ -297,14 +296,14 @@
     copy.wait()
     for t in range(tiles):
         for f in range(slots):
-            row, piece = index_ref[0, t, f], index_ref[1, t, f]
+            found = {}
             for n, dest in ((0, t + n_rg), (1, t), (2, t - n_rg)):
                 if 0 <= dest < tiles:
                     place, line = divmod(n * slots + f, table_rows)
-                    turn = jnp.bitwise_and(place - piece, packed - 1)
-                    put = turn_ref[turn, pl.ds(row, 1), :]
+                    if place not in found:
+                        found[place] = turn_ref[pl.ds(index_ref[place, t, f], 1), :]
                     cut = slice(place * width, (place + 1) * width)
-                    out_ref[dest, line : line + 1, cut] = put[:, cut]
+                    out_ref[dest, line : line + 1, cut] = found[place][:, cut]
 
 
 def sincos(x):
@@ -324,7 +323,7 @@
     return cosine, sine
 
 
-def flatten_kernel(width, table_rows, slots, par_ref, got_ref, image_ref, factor_ref, position_ref, one_ref, two_ref, flat_ref, edge_ref, tab_ref, in_ref, at_ref):
+def flatten_kernel(width, table_rows, slots, par_ref, got_ref, image_ref, factor_ref, position_ref, one_ref, two_ref, flat_ref, edge_ref, tab_ref):
     even = par_ref[0] == 0
     lines, samples = factor_ref.shape
     packed = LANES // width
@@ -338,53 +337,44 @@
                 x = roll(got_ref[k * packed + j, 0:table_rows, :], (j - place) * width, 1)
                 total = x if total is None else jnp.where(lane // width == j, x, total)
             tab_ref[k, place * table_rows : (place + 1) * table_rows, :] = total
-    for i in range(3):
-        top = jnp.where(even, two_ref[i], one_ref[i])
-        low = jnp.where(even, one_ref[i], two_ref[i])
-        in_ref[i, 0:RIM] = top
-        in_ref[i, RIM + lines :] = low
-    in_ref[0, RIM : RIM + lines] = image_ref[0]
-    in_ref[1, RIM : RIM + lines] = image_ref[1]
-    in_ref[2, RIM : RIM + lines] = factor_ref[...]
-    at_ref[0:RIM] = jnp.where(even, two_ref[3], one_ref[3]).astype(I32)
-    at_ref[RIM : RIM + lines] = position_ref[...]
-    at_ref[RIM + lines :] = jnp.where(even, one_ref[3], two_ref[3]).astype(I32)
-    W = 1
     cols = samples // LANES
     shift = LANES.bit_length() - 1
     part_bits = parts.bit_length() - 1
-    groups = (lines + 2 * RIM) // 8
-    steps = groups * cols // W
-    rim_steps = RIM // 8 * cols // W
-
-    def step(i):
-        base = jnp.where(i < rim_steps, 0, jnp.where(i < steps - rim_steps, slots, 2 * slots))
-        spots = []
-        for j in range(W):
-            n = i * W + j
-            if W >= cols:
-                spots.append((pl.ds(pl.multiple_of((i * (W // cols) + j // cols) * 8, 8), 8), pl.ds(j % cols * LANES, LANES)))
-            else:
-                spots.append((pl.ds(pl.multiple_of(n // cols * 8, 8), 8), pl.ds(pl.multiple_of(n % cols * LANES, LANES), LANES)))
-        at = [at_ref[spot] for spot in spots]
-        lanes = [jnp.bitwise_and(x, LANES - 1) for x in at]
-        bits = [[jnp.bitwise_and(x, LANES << b) != 0 for b in range(part_bits)] for x in at]
-        slot = [jnp.right_shift(x, shift + part_bits) for x in at]
-        height = [None] * W
-        for f in range(slots):
-            rows = [jnp.broadcast_to(tab_ref[k, pl.ds(base + f, 1), :], (8, LANES)) for k in range(parts)]
-            for j in range(W):
-                x = [jnp.take_along_axis(row, lanes[j], axis=1) for row in rows]
-                for b in range(part_bits):
-                    x = [jnp.where(bits[j][b], x[n + 1], x[n]) for n in range(0, len(x), 2)]
-                height[j] = x[0] if f == 0 else jnp.where(slot[j] == f, x[0], height[j])
-        for spot, h in zip(spots, height):
-            cosine, sine = sincos(in_ref[(2, *spot)] * h)
-            a, b = in_ref[(0, *spot)], in_ref[(1, *spot)]
-            flat_ref[(0, *spot)] = a * cosine + b * sine
-            flat_ref[(1, *spot)] = b * cosine - a * sine
-
-    pl.loop(0, steps, unroll=16)(step)
+    own = (lambda c: (lambda spot: image_ref[(c, *spot)]))
+
+    def rim_field(n, below):
+        def read(spot):
+            a, b = one_ref[(n, *spot)], two_ref[(n, *spot)]
+            return jnp.where(even, a, b) if below else jnp.where(even, b, a)
+
+        return read
+
+    fields = [own(0), own(1), lambda spot: factor_ref[spot], lambda spot: position_ref[spot]]
+    strips = [(0, [rim_field(n, False) for n in range(4)], RIM), (1, fields, lines), (2, [rim_field(n, True) for n in range(4)], RIM)]
+    line = 0
+    for table, sources, height in strips:
+        for start in range(0, height, 8):
+            for c in range(cols):
+                spot = (slice(start, start + 8), slice(c * LANES, (c + 1) * LANES))
+                re, im, factor, at = [read(spot) for read in sources]
+                at = at.astype(I32)
+                lanes = jnp.bitwise_and(at, LANES - 1)
+                bits = [jnp.bitwise_and(at, LANES << b) != 0 for b in range(part_bits)]
+                slot = jnp.right_shift(at, shift + part_bits)
+                found = None
+                for f in range(slots):
+                    row = table * slots + f
+                    x = [
+                        jnp.take_along_axis(jnp.broadcast_to(tab_ref[k, row : row + 1, :], (8, LANES)), lanes, axis=1)
+                        for k in range(parts)
+                    ]
+                    for bit in bits:
+                        x = [jnp.where(bit, x[n + 1], x[n]) for n in range(0, len(x), 2)]
+                    found = x[0] if f == 0 else jnp.where(slot == f, x[0], found)
+                cosine, sine = sincos(factor * found)
+                flat_ref[0, line : line + 8, spot[1]] = re * cosine + im * sine
+                flat_ref[1, line : line + 8, spot[1]] = im * cosine - re * sine
+            line += 8
     edge = lane_iota((lines + 2 * RIM, LANES))
     for c in range(2):
         first = flat_ref[c, :, 0:LANES]
@@ -396,71 +386,99 @@
     return x * lax.rsqrt(jnp.maximum(x, 1e-37))
 
 
-def filter_kernel(n_rg, cap_rows, block_rows, rg_ref, flat_ref, edge_ref, rim_ref, side_ref, im_ref, in_ref, owner_ref, base_ref, share_ref, const_ref, col_ref, here_ref, next_ref, out_ref, x_ref, y_ref, m_ref, s_ref, p_ref, z_ref, look_ref, w_ref, term_ref):
+def stack_parts(x_ref, c, at, x):
+    high, low = split(x)
+    x_ref[c * HALF : (c + 1) * HALF, at] = high
+    x_ref[(2 + c) * HALF : (3 + c) * HALF, at] = low
+    x_ref[(4 + c) * HALF : (5 + c) * HALF, at] = high
+
+
+def spectrum(strips):
+    flip = jnp.where(row_iota(strips[0].shape) % 2 == 0, 1.0, -1.0)
+    return jnp.concatenate([one + flip * two for one, two in zip(strips[:-1], strips[1:])], axis=0)
+
+
+def range_dft(windows, const_ref):
+    (rh, rl), (ih, il) = [split(jnp.concatenate(x, axis=0)) for x in windows]
+    size = 2 * LANES
+    main, rest = const_ref[:size], const_ref[size : 2 * size]
+    return dot(jnp.concatenate([rh, ih, rl, il, rh, ih], axis=1), jnp.concatenate([main, main, rest], axis=0))
+
+
+def transform_kernel(flat_ref, az_ref, const_ref, out_ref, x_ref):
     _, rows, samples = flat_ref.shape
     cols = samples // LANES
     wide = (cols + 1) * LANES
     lane = lane_iota((HALF, LANES))
+    for p in range(rows // HALF):
+        for c in range(2):
+            before = 0.0
+            for j in range(cols + 1):
+                now = 0.0
+                if j < cols:
+                    now = roll(flat_ref[c, p * HALF : (p + 1) * HALF, j * LANES : (j + 1) * LANES], RIM, 1)
+                at = slice(p * wide + j * LANES, p * wide + (j + 1) * LANES)
+                stack_parts(x_ref, c, at, jnp.where(lane < RIM, before, now))
+                before = now
+    e = dot(az_ref[...], x_ref[...])
+    windows = []
+    for c in range(2):
+        cut = slice(c * PATCH, (c + 1) * PATCH)
+        cells = [
+            spectrum([e[cut, p * wide + j * LANES : p * wide + (j + 1) * LANES] for p in range(rows // HALF)])
+            for j in range(cols + 1)
+        ]
+        half = lane_iota(cells[0].shape) < PATCH
+        turned = [pltpu.roll(x, PATCH, 1) for x in cells]
+        found = []
+        for j in range(cols):
+            found += [cells[j], jnp.where(half, turned[j], turned[j + 1])]
+        windows.append(found)
+    out_ref[...] = range_dft(windows, const_ref)
+
+
+def filter_kernel(n_rg, cap_rows, block_rows, rg_ref, y_ref, edge_ref, rim_ref, side_ref, im_ref, in_ref, owner_ref, base_ref, share_ref, az_ref, const_ref, col_ref, here_ref, next_ref, out_ref, x_ref, rim_y_ref, m_ref, s_ref, p_ref, z_ref, look_ref, w_ref, term_ref):
+    strips = edge_ref.shape[1] // HALF
+    lane = lane_iota((HALF, LANES))
     left = rg_ref[0] > 0
     right = rg_ref[0] < n_rg - 1
-    strips = rows // HALF
     for p in range(strips):
         for c in range(2):
-            cut = slice(p * HALF, (p + 1) * HALF)
-            halo = edge_ref[c, cut]
+            halo = edge_ref[c, p * HALF : (p + 1) * HALF]
             before = jnp.where(left, roll(halo, -RIM, 1), 0.0)
-            after = jnp.where(right, roll(halo, RIM, 1), 0.0)
-            for j in range(cols + 1):
-                if j < cols:
-                    now = roll(flat_ref[c, cut, j * LANES : (j + 1) * LANES], RIM, 1)
-                else:
-                    now = jnp.where(lane < 2 * RIM, after, 0.0)
-                high, low = split(jnp.where(lane < RIM, before, now))
-                before = now
-                at = slice(p * wide + j * LANES, p * wide + (j + 1) * LANES)
-                x_ref[c * HALF : (c + 1) * HALF, at] = high
-                x_ref[(2 + c) * HALF : (3 + c) * HALF, at] = low
-                x_ref[(4 + c) * HALF : (5 + c) * HALF, at] = high
+            after = jnp.where(right & (lane < 2 * RIM), roll(halo, RIM, 1), 0.0)
+            stack_parts(x_ref, c, slice(p * LANES, (p + 1) * LANES), jnp.where(lane < RIM, before, after))
     looks = block_rows * STEP // LOOK
     block = const_ref[...]
 
     def tripled(at, size):
         return jnp.concatenate([block[at : at + size], block[at : at + size], block[at + size : at + 2 * size]], axis=0)
 
-    rg3 = tripled(0, 2 * LANES)
     last3 = tripled(4 * LANES, 4 * LANES)
     near = jnp.concatenate([block[12 * LANES : 13 * LANES, :LANES]] * 2, axis=0)
     side = jnp.concatenate([block[12 * LANES : 13 * LANES, LANES:]] * 2, axis=0)
-    az = block[13 * LANES : 13 * LANES + 2 * PATCH, : 6 * HALF]
-    back = block[14 * LANES : 14 * LANES + 4 * looks, : 2 * block_rows * PATCH]
-    e = dot(az, x_ref[...])
+    back = block[13 * LANES : 13 * LANES + 4 * looks, : 2 * block_rows * PATCH]
+    rim = dot(az_ref[...], x_ref[...])
     count = block_rows * PATCH
-    flip = jnp.where(row_iota((PATCH, LANES)) % 2 == 0, 1.0, -1.0)
-    half = lane_iota((count, LANES)) < PATCH
-
-    def spectrum(c, j):
-        cells = []
-        for u in range(block_rows):
-            one = e[c * PATCH : (c + 1) * PATCH, u * wide + j * LANES : u * wide + (j + 1) * LANES]
-            two = e[c * PATCH : (c + 1) * PATCH, (u + 1) * wide + j * LANES : (u + 1) * wide + (j + 1) * LANES]
-            cells.append(one + flip * two)
-        return jnp.concatenate(cells, axis=0)
-
-    parts = []
+    pairs = y_ref.shape[0] // count
+    windows = []
     for c in range(2):
-        cells = [spectrum(c, j) for j in range(cols + 1)]
-        turned = [pltpu.roll(x, PATCH, 1) for x in cells]
-        windows = []
-        for j in range(cols):
-            windows += [cells[j], jnp.where(half, turned[j], turned[j + 1])]
-        parts.append(split(jnp.concatenate(windows, axis=0)))
-    (rh, rl), (ih, il) = parts
-    y_ref[...] = dot(jnp.concatenate([rh, ih, rl, il, rh, ih], axis=1), rg3)
-    pairs = 2 * cols
-
-    def measure(w):
+        x = spectrum([rim[c * PATCH : (c + 1) * PATCH, p * LANES : (p + 1) * LANES] for p in range(strips)])
+        first = lane_iota(x.shape) < RIM
+        windows.append([jnp.where(first, x, 0.0), pltpu.roll(jnp.where(first, 0.0, x), PATCH, 1)])
+    rim_y_ref[...] = range_dft(windows, const_ref)
+    rim_y_ref[:count] = rim_y_ref[:count] + y_ref[:count]
+    rim_y_ref[count:] = rim_y_ref[count:] + y_ref[(pairs - 1) * count :]
+
+    def everywhere(step):
+        step(0, rim_y_ref, 0)
+        pl.loop(1, pairs - 1, unroll=3)(lambda w: step(w, y_ref, w))
+        step(pairs - 1, rim_y_ref, 1)
+
+    def measure(w, ref, place):
         at = pl.multiple_of(w * count, count)
-        re, im = y_ref[pl.ds(at, count), :LANES], y_ref[pl.ds(at, count), LANES:]
+        cut = pl.ds(pl.multiple_of(place * count, count), count)
+        re, im = ref[cut, :LANES], ref[cut, LANES:]
         magnitude = root(re * re + im * im)
         high, low = split(magnitude)
         m_ref[pl.ds(at, count), :LANES] = high
@@ -471,7 +489,7 @@
                 part = part + magnitude[u * PATCH + 8 * i : u * PATCH + 8 * i + 8]
             p_ref[pl.ds(pl.multiple_of((w * block_rows + u) * 8, 8), 8), :] = part
 
-    pl.loop(0, pairs, unroll=UNROLL)(measure)
+    everywhere(measure)
     s_ref[...] = dot(m_ref[...], near)
     ph, plow = split(p_ref[...])
     sums = dot(jnp.concatenate([ph, plow], axis=1), side)
@@ -481,7 +499,7 @@
             x = x + pltpu.roll(x, shift, 0)
         p_ref[8 * n : 8 * n + 8, :] = 1.0 / (9.0 * (x * (1.0 / (PATCH * PATCH)) + EPS))
 
-    def weigh(w):
+    def weigh(w, ref, place):
         at = pl.multiple_of(w * 2 * LANES, 2 * LANES)
         for u in range(block_rows):
             cut = pl.ds(pl.multiple_of(w * count + u * PATCH, PATCH), PATCH)
@@ -490,12 +508,13 @@
             factor = p_ref[pl.ds(pl.multiple_of((w * block_rows + u) * 8, 8), 8), :]
             gain = root(su * jnp.concatenate([factor] * (PATCH // 8), axis=0))
             for c in range(2):
-                high, low = split(y_ref[cut, c * LANES : (c + 1) * LANES] * gain)
+                source = pl.ds(pl.multiple_of(place * count + u * PATCH, PATCH), PATCH)
+                high, low = split(ref[source, c * LANES : (c + 1) * LANES] * gain)
                 span = pl.ds(pl.multiple_of(at + c * LANES, LANES), LANES)
                 z_ref[u * PATCH : (u + 1) * PATCH, span] = high
                 z_ref[count + u * PATCH : count + (u + 1) * PATCH, span] = low
 
-    pl.loop(0, pairs, unroll=UNROLL)(weigh)
+    everywhere(weigh)
     t = dot(back, z_ref[...])
     t = t[: 2 * looks] + t[2 * looks :]
     stacked = jnp.concatenate(
@@ -601,18 +620,18 @@
         np.concatenate([rg_h, rg_l], axis=0),
         np.concatenate([last_h, last_l], axis=0),
         np.concatenate([near, same.astype(BF16)], axis=1),
-        np.concatenate([az_h, az_h, az_l], axis=1),
         np.concatenate([np.concatenate([back_h, back_h], axis=1), np.concatenate([back_l, zero], axis=1)], axis=0),
     )
-    return np.concatenate([np.pad(b, ((0, 0), (0, 2 * LANES - b.shape[1]))) for b in blocks], axis=0)
+    wide = [np.pad(b, ((0, 0), (0, 2 * LANES - b.shape[1]))) for b in blocks]
+    return np.concatenate([az_h, az_h, az_l], axis=1), np.concatenate(wide, axis=0)
 
 
 def filter_scratch(rows, samples, block_rows, map_lat, map_lon, tiles):
     patches = samples // STEP
     count = block_rows * PATCH
     return (
-        VMEM((6 * HALF, rows // HALF * (samples + LANES)), BF16),
-        VMEM((patches // 2 * count, 2 * LANES), F32),
+        VMEM((6 * HALF, rows // HALF * LANES), BF16),
+        VMEM((2 * count, 2 * LANES), F32),
         VMEM((patches // 2 * count, 2 * LANES), BF16),
         VMEM((patches // 2 * count, LANES), F32),
         VMEM((patches // 2 * block_rows * 8, LANES), F32),
@@ -684,9 +703,9 @@
         sds((tiles, table_rows + early_rows, LANES)),
         (got_slices, early, cells),
         scratch=(
-            VMEM((packed, tiles * (slice_rows + 8), LANES), F32),
-            VMEM((2, tiles, LANES), I32),
-            pltpu.SMEM((2, tiles, LANES), I32),
+            VMEM((packed * tiles * (slice_rows + 8), LANES), F32),
+            VMEM((packed, tiles, LANES), I32),
+            pltpu.SMEM((packed, tiles, LANES), I32),
             pltpu.SemaphoreType.DMA((1,)),
         ),
     )
@@ -698,16 +717,26 @@
         smem=(0,),
         scratch=(
             VMEM((tiles // packed, packed * table_rows, LANES), F32),
-            VMEM((3, lines + 2 * RIM, samples), F32),
-            VMEM((lines + 2 * RIM, samples), I32),
         ),
     )
     edge = lax.ppermute(edge, "rg", swap_pairs(n_rg, 0))
+    az_parts, constants = filter_constants(block_rows)
+    wide = (lines + 2 * RIM) // HALF * (samples + LANES)
+    patches = samples // STEP
+    count = block_rows * PATCH
+    lines_done = call(
+        transform_kernel,
+        sds((patches // 2 * count, 2 * LANES)),
+        (flat, az_parts, constants),
+        scratch=(VMEM((6 * HALF, wide), BF16),),
+    )
     rows = lines + 2 * RIM
+    patches = samples // STEP
+    count = block_rows * PATCH
     packed_looks = call(
         functools.partial(filter_kernel, n_rg, cap_rows, block_rows),
         sds((tiles, late_rows, LANES)),
-        (rg, flat, edge, rim_sum, side_sum, at_m, at_n, *looks_at, filter_constants(block_rows), *edges),
+        (rg, lines_done, edge, rim_sum, side_sum, at_m, at_n, *looks_at, az_parts, constants, *edges),
         smem=(0,),
         scratch=filter_scratch(rows, samples, block_rows, map_lat, map_lon, tiles),
     )

time: 60.5 us -> 58.8 us (0.972)
  waiting for transfers between devices: 22.4 us -> 21.3 us
  Pallas kernels: 16.8 us -> 16.1 us
    ppermute x1, waiting for transfers between devices: 1.28 us -> 0.29 us  [scene(): edge = lax.ppermute(edge, 'rg', swap_pairs(n_rg, 0))]
    pallas_call x8 -> x9, Pallas kernels: 16.8 us -> 16.1 us  [call(): pl.pallas_call(kernel, out_shape=outs, in_specs=[SSPEC if i in smem else...]
  transfers between devices with their start and end apart: 6 -> 6, of which waited for: 4 -> 4; matrix products, arithmetic and copies ran while one was open for 0% -> 0% of each run, Pallas kernels for 5% -> 7%
where the time goes in v4:
time: 58.8 us; the launch traced here: 58.3 us
  waiting for transfers between devices  21.3 us (36%)
  starting transfers between devices  20.1 us (34%)
  Pallas kernels  16.1 us (27%)
  local copies, waits for them, and re-layouts  0.72 us (1%)
    all_to_all x3, starting transfers between devices, exchange(): return lax.all_to_all(x, both, split_axis=0, concat_axis=0, tiled=True)  17.3 us
    pallas_call x9, Pallas kernels, call(): pl.pallas_call(kernel, out_shape=outs, in_specs=[SSPEC if i in smem else...  16.1 us
    all_to_all x3, waiting for transfers between devices, exchange(): return lax.all_to_all(x, both, split_axis=0, concat_axis=0, tiled=True)  14.4 us
    ppermute x1, waiting for transfers between devices, scene(): one = lax.ppermute(one, 'az', swap_pairs(n_az, 0))  6.58 us
    ppermute x1, starting transfers between devices, scene(): one = lax.ppermute(one, 'az', swap_pairs(n_az, 0))  1.86 us
  transfers between devices with their start and end apart: 6, of which 4 were waited for; matrix products, arithmetic and copies ran while one was open for 0% of the time, Pallas kernels for 7%

profile of v4, /device:TPU:0, one launch (start us, length us, event | category | flops | bytes accessed | tf_op | source)
XLA Modules:
  0.0 58.3 jit_solution(5499021364182746087)
XLA Ops:
  0.0 1.8 %shard_map.100 = f32[16,40,128]{2,1,0:T(8,128)} custom-call(f32[8,8,1024]{2,1,0:T(8,128)} %dem_ref.1, s32[1,9]{1,0:T(1,128)} %list_ref.1), custom_call_target="tpu_custom_call" | custom-call | flops 1000000 | bytes 1000000 | tf_op jit(solution)/shard_map/pallas_call | solution.py:29
  1.8 0.0 copy-start.7
  1.8 7.5 %all-to-all-start = ((f32[16,40,128]{2,1,0:T(8,128)}), f32[16,40,128]{2,1,0:T(8,128)S(1)}, u32[]{:S(2)}, u32[]{:S(2)}) async-start(f32[16,40,128]{2,1,0:T(8,128)} %shard_map.100), calls=%async_computation | async-start | bytes 655360 | tf_op jit(solution)/shard_map/all_to_all | solution.py:671
  9.4 0.0 copy-done.7
  9.4 0.0 copy-start.5
  9.4 0.0 copy-start.6
  9.4 0.7 %copy-done.5 = s32[2048,1]{0,1:T(1,128)S(1)} copy-done((s32[2048,1]{0,1:T(1,128)S(1)}, s32[2048,1]{0,1:T(1,128)}, u32[]{:S(2)}) %copy-start.5) | copy-done | bytes 8216
  10.1 0.0 copy-done.6
  10.1 1.8 %shard_map.101 = (f32[16,8,128]{2,1,0:T(8,128)S(1)}, f32[16,256]{1,0:T(8,128)S(1)}, f32[16,128]{1,0:T(8,128)S(1)}, f32[16,16]{1,0:T(8,128)S(1)}, s32[16,256]{1,0...) custom-call(s32[16,128]{1,0:T(8,128)S(1)} %bitcast.10, ...), custom_call_target="tpu_custom_call" | custom-call | flops 1000000 | bytes 1000000 | tf_op jit(solution)/shard_map/pallas_call | solution.py:29
  11.9 8.5 %all-to-all-done.got_ref = f32[16,40,128]{2,1,0:T(8,128)S(1)} async-done(((f32[16,40,128]{2,1,0:T(8,128)}), f32[16,40,128]{2,1,0:T(8,128)S(1)}, u32[]{:S(2)}, u32[]{:S(2)}) %all-to-all-start) | async-done | bytes 327712 | tf_op jit(solution)/shard_map/all_to_all | solution.py:671
  20.4 1.8 %shard_map.102 = f32[16,24,128]{2,1,0:T(8,128)} custom-call(f32[16,40,128]{2,1,0:T(8,128)S(1)} %all-to-all-done.got_ref, f32[16,8,128]{2,1,0:T(8,128)S(1)} %get-tuple-element.21.early_ref, f32[16,256]{1,0:T(8,128)S(1)} %get-tuple-element.22.cell_ref), custom_call_target="tpu_custom_call" | custom-call | flops 1000000 | bytes 1000000 | tf_op jit(solution)/shard_map/pallas_call | solution.py:29
  22.2 0.0 copy-start
  22.3 3.7 %all-to-all-start.1 = ((f32[16,24,128]{2,1,0:T(8,128)}), f32[16,24,128]{2,1,0:T(8,128)S(1)}, u32[]{:S(2)}, u32[]{:S(2)}) async-start(f32[16,24,128]{2,1,0:T(8,128)} %shard_map.102), calls=%async_computation.1 | async-start | bytes 393216 | tf_op jit(solution)/shard_map/all_to_all | solution.py:671
  25.9 0.0 copy-done.1
  26.0 0.0 copy-done.2
  26.0 0.0 copy-done.3
  26.0 1.9 %collective-permute-start = (f32[4,16,512]{2,1,0:T(8,128)S(1)}, f32[4,16,512]{2,1,0:T(8,128)S(1)}, u32[]{:S(2)}, u32[]{:S(2)}) collective-permute-start(f32[4,16,512]{2,1,0:T(8,128)S(1)} %get-tuple-element.23), channel_id=1, source_target_pairs={{0,2},{2,0},{4,6},{6,4},{8,10},{10,8},{12,14},{14,12},{1,3},{3,1},... | collective-permute-start | bytes 393224 | tf_op jit(solution)/shard_map/ppermute | solution.py:681
  27.9 0.8 %collective-permute-start.1 = (f32[4,16,512]{2,1,0:T(8,128)S(1)}, f32[4,16,512]{2,1,0:T(8,128)S(1)}, u32[]{:S(2)}, u32[]{:S(2)}) collective-permute-start(f32[4,16,512]{2,1,0:T(8,128)S(1)} %get-tuple-element.24), channel_id=1, source_target_pairs={{2,4},{4,2},{6,8},{8,6},{10,12},{12,10},{3,5},{5,3},{7,9},{9,7},{1... | collective-permute-start | bytes 393224 | tf_op jit(solution)/shard_map/ppermute | solution.py:682
  28.7 6.6 %collective-permute-done.one_ref = f32[4,16,512]{2,1,0:T(8,128)S(1)} collective-permute-done((f32[4,16,512]{2,1,0:T(8,128)S(1)}, f32[4,16,512]{2,1,0:T(8,128)S(1)}, u32[]{:S(2)}, u32[]{:S(2)}) %collective-permute-start) | collective-permute-done | bytes 131104 | tf_op jit(solution)/shard_map/ppermute | solution.py:681
  35.2 0.0 collective-permute-done.1.two_ref
  35.2 0.0 all-to-all-done.1.got_ref
  35.2 4.1 %shard_map.104 = (f32[2,96,512]{2,1,0:T(8,128)S(1)}, f32[2,96,128]{2,1,0:T(8,128)S(1)}) custom-call(s32[1]{0:T(128)} %bitcast.1.par_ref, f32[16,24,128]{2,1,0:T(8,128)S(1)} %all-to-all-done.1.got_ref, f32[2,64,512]{2,1,0:T(8,128)S(1)} %copy-done.1, f32[64,512]{1,0:T(8,128)S(1)} %copy-done.2, s32[64,512]{1,0:T(8,128)S(1)} %copy-done.3, ...), custom_call_target="tpu_custom_call" | custom-call | flops 1000000 | bytes 1000000 | tf_op jit(solution)/shard_map/pallas_call | solution.py:29
  39.3 0.1 collective-permute-start.2
  39.4 0.0 copy-done
  39.4 0.0 copy-done.4
  39.4 1.0 %shard_map.105.y_ref = f32[1024,256]{1,0:T(8,128)S(1)} custom-call(f32[2,96,512]{2,1,0:T(8,128)S(1)} %get-tuple-element.25.flat_ref, bf16[128,192]{1,0:T(8,128)(2,1)S(1)} %copy-done.4, bf16[1728,256]{1,0:T(8,128)(2,1)S(1)} %copy-done), custom_call_target="tpu_custom_call" | custom-call | flops 1000000 | bytes 1000000 | tf_op jit(solution)/shard_map/pallas_call | solution.py:29
  40.4 0.3 collective-permute-done.2.edge_ref
  40.7 3.4 %shard_map.106 = f32[16,8,128]{2,1,0:T(8,128)} custom-call(s32[1]{0:T(128)} %bitcast.rg_ref, f32[1024,256]{1,0:T(8,128)S(1)} %shard_map.105.y_ref, f32[2,96,128]{2,1,0:T(8,128)S(1)} %collective-permute-done.2.edge_ref, f32[16,128]{1,0:T(8,128)S(1)} %get-tuple-element.27.rim_ref, f32[16,16]{1,0:T(8,128)S(1)} %get-tuple-element.28.side_ref, ...), custom_call_target="tpu_custom_call" | custom-call | flops 1000000 | bytes 1000000 | tf_op jit(solution)/shard_map/pallas_call | solution.py:29
  44.1 6.1 %all-to-all-start.2 = ((f32[16,8,128]{2,1,0:T(8,128)}), f32[16,8,128]{2,1,0:T(8,128)S(1)}, u32[]{:S(2)}, u32[]{:S(2)}) async-start(f32[16,8,128]{2,1,0:T(8,128)} %shard_map.106), calls=%async_computation.2 | async-start | bytes 131072 | tf_op jit(solution)/shard_map/all_to_all | solution.py:671
  50.2 1.0 %shard_map.107 = (bf16[128,4096]{1,0:T(8,128)(2,1)S(1)}, f32[32,4096]{1,0:T(8,128)S(1)}, f32[16,128]{1,0:T(8,128)S(1)}) custom-call(f32[16,24,128]{2,1,0:T(8,128)S(1)} %all-to-all-done.1.got_ref), custom_call_target="tpu_custom_call" | custom-call | flops 1000000 | bytes 1000000 | tf_op jit(solution)/shard_map/pallas_call | solution.py:29
  51.2 5.9 %all-to-all-done.2.got_ref = f32[16,8,128]{2,1,0:T(8,128)S(1)} async-done(((f32[16,8,128]{2,1,0:T(8,128)}), f32[16,8,128]{2,1,0:T(8,128)S(1)}, u32[]{:S(2)}, u32[]{:S(2)}) %all-to-all-start.2) | async-done | bytes 65568 | tf_op jit(solution)/shard_map/all_to_all | solution.py:671
  57.1 1.2 %shard_map.108 = f32[2,16,128]{2,1,0:T(8,128)} custom-call(f32[16,8,128]{2,1,0:T(8,128)S(1)} %all-to-all-done.2.got_ref, bf16[128,4096]{1,0:T(8,128)(2,1)S(1)} %get-tuple-element.34.hot_ref, f32[32,4096]{1,0:T(8,128)S(1)} %get-tuple-element.35.row_ref, f32[16,128]{1,0:T(8,128)S(1)} %get-tuple-element.36.weight_ref), custom_call_target="tpu_custom_call" | custom-call | flops 1000000 | bytes 1000000 | tf_op jit(solution)/shard_map/pallas_call | solution.py:29
  (6 shorter events, 0.0 us)
Async XLA Ops:
  1.8 7.6 %copy-start.7 = (f32[4,2048]{1,0:T(4,128)S(1)}, f32[4,2048]{1,0:T(4,128)}, u32[]{:S(2)}) copy-start(f32[4,2048]{1,0:T(4,128)} %param.17) | copy-start | bytes 98308
  1.8 18.6 %all-to-all-start = ((f32[16,40,128]{2,1,0:T(8,128)}), f32[16,40,128]{2,1,0:T(8,128)S(1)}, u32[]{:S(2)}, u32[]{:S(2)}) async-start(f32[16,40,128]{2,1,0:T(8,128)} %shard_map.100), calls=%async_computation | async-start | bytes 655360 | tf_op jit(solution)/shard_map/all_to_all | solution.py:671
  9.4 0.7 %copy-start.5 = (s32[2048,1]{0,1:T(1,128)S(1)}, s32[2048,1]{0,1:T(1,128)}, u32[]{:S(2)}) copy-start(s32[2048,1]{0,1:T(1,128)} %param.15) | copy-start | bytes 24580
  9.4 0.7 %copy-start.6 = (s32[2048]{0:T(1024)S(1)}, s32[2048]{0:T(1024)}, u32[]{:S(2)}) copy-start(s32[2048]{0:T(1024)} %param.16) | copy-start | bytes 24580
  20.4 5.5 %copy-start.1 = (f32[2,64,512]{2,1,0:T(8,128)S(1)}, f32[2,64,512]{2,1,0:T(8,128)}, u32[]{:S(2)}) copy-start(f32[2,64,512]{2,1,0:T(8,128)} %image_ref.3) | copy-start | bytes 786436
  20.4 5.5 %copy-start.2 = (f32[64,512]{1,0:T(8,128)S(1)}, f32[64,512]{1,0:T(8,128)}, u32[]{:S(2)}) copy-start(f32[64,512]{1,0:T(8,128)} %factor_ref.3) | copy-start | bytes 393220
  20.4 5.5 %copy-start.3 = (s32[64,512]{1,0:T(8,128)S(1)}, s32[64,512]{1,0:T(8,128)}, u32[]{:S(2)}) copy-start(s32[64,512]{1,0:T(8,128)} %position_ref.3) | copy-start | bytes 393220
  22.2 17.2 %copy-start = (bf16[1728,256]{1,0:T(8,128)(2,1)S(1)}, bf16[1728,256]{1,0:T(8,128)(2,1)}, u32[]{:S(2)}) copy-start(bf16[1728,256]{1,0:T(8,128)(2,1)} %constant.26.clone.const_ref) | copy-start | bytes 2654212
  22.3 13.0 %all-to-all-start.1 = ((f32[16,24,128]{2,1,0:T(8,128)}), f32[16,24,128]{2,1,0:T(8,128)S(1)}, u32[]{:S(2)}, u32[]{:S(2)}) async-start(f32[16,24,128]{2,1,0:T(8,128)} %shard_map.102), calls=%async_computation.1 | async-start | bytes 393216 | tf_op jit(solution)/shard_map/all_to_all | solution.py:671
  26.0 9.2 %collective-permute-start = (f32[4,16,512]{2,1,0:T(8,128)S(1)}, f32[4,16,512]{2,1,0:T(8,128)S(1)}, u32[]{:S(2)}, u32[]{:S(2)}) collective-permute-start(f32[4,16,512]{2,1,0:T(8,128)S(1)} %get-tuple-element.23), channel_id=1, source_target_pairs={{0,2},{2,0},{4,6},{6,4},{8,10},{10,8},{12,14},{14,12},{1,3},{3,1},... | collective-permute-start | bytes 393224 | tf_op jit(solution)/shard_map/ppermute | solution.py:681
  27.9 11.6 %copy-start.4 = (bf16[128,192]{1,0:T(8,128)(2,1)S(1)}, bf16[128,192]{1,0:T(8,128)(2,1)}, u32[]{:S(2)}) copy-start(bf16[128,192]{1,0:T(8,128)(2,1)} %constant.25.clone.az_ref) | copy-start | bytes 147460
  27.9 7.4 %collective-permute-start.1 = (f32[4,16,512]{2,1,0:T(8,128)S(1)}, f32[4,16,512]{2,1,0:T(8,128)S(1)}, u32[]{:S(2)}, u32[]{:S(2)}) collective-permute-start(f32[4,16,512]{2,1,0:T(8,128)S(1)} %get-tuple-element.24), channel_id=1, source_target_pairs={{2,4},{4,2},{6,8},{8,6},{10,12},{12,10},{3,5},{5,3},{7,9},{9,7},{1... | collective-permute-start | bytes 393224 | tf_op jit(solution)/shard_map/ppermute | solution.py:682
  39.3 1.4 %collective-permute-start.2 = (f32[2,96,128]{2,1,0:T(8,128)S(1)}, f32[2,96,128]{2,1,0:T(8,128)S(1)}, u32[]{:S(2)}, u32[]{:S(2)}) collective-permute-start(f32[2,96,128]{2,1,0:T(8,128)S(1)} %get-tuple-element.26), channel_id=1, source_target_pairs={{0,1},{1,0},{2,3},{3,2},{4,5},{5,4},{6,7},{7,6},{8,9},{9,8},{10,11... | collective-permute-start | bytes 294920 | tf_op jit(solution)/shard_map/ppermute | solution.py:722
  44.1 13.0 %all-to-all-start.2 = ((f32[16,8,128]{2,1,0:T(8,128)}), f32[16,8,128]{2,1,0:T(8,128)S(1)}, u32[]{:S(2)}, u32[]{:S(2)}) async-start(f32[16,8,128]{2,1,0:T(8,128)} %shard_map.106), calls=%async_computation.2 | async-start | bytes 131072 | tf_op jit(solution)/shard_map/all_to_all | solution.py:671

commit v5 on v4

--- a/solution.py
+++ b/solution.py
@@ -14,6 +14,7 @@
 LOOK = 4
 EPS = 1e-06
 LANES = 128
+QUAD = 1
 RIM = PATCH // 4
 STEP = PATCH // 2
 HALF = PATCH // 2
@@ -136,8 +137,9 @@
                 x = dem_ref[p * groups + g, :, tile * LANES : (tile + 1) * LANES]
                 x = roll(x, p * width - offset, 1)
                 total = x if total is None else jnp.where(lane // width == p, x, total)
-            out_ref[q, g * lons : (g + 1) * lons, :] = total
-        out_ref[q, groups * lons : groups * lons + 1, 0:slots] = listed
+            for i in range(lons // QUAD):
+                out_ref[q, g * (lons // QUAD) + i] = total[i * QUAD : (i + 1) * QUAD]
+        out_ref[q, groups * lons // QUAD, 0:1, 0:slots] = listed
 
 
 def halo_kernel(par_ref, image_ref, factor_ref, position_ref, one_ref, two_ref):
@@ -269,11 +271,13 @@
 
 
 def request_kernel(n_rg, grid, width, table_rows, slots, got_ref, early_ref, cell_ref, out_ref, turn_ref, list_ref, index_ref, sem):
-    tiles, rows, _ = got_ref.shape
+    tiles, quads = got_ref.shape[:2]
+    rows = (quads - 1) * QUAD
     lats, lons = grid
     packed = LANES // width
     groups = lats // packed
-    listed = jnp.maximum(got_ref[:, rows - 8, :], 0.0)
+    listed = jnp.concatenate([got_ref[t, quads - 1, 0:1, :] for t in range(tiles)], axis=0)
+    listed = jnp.maximum(listed, 0.0)
     listed = jnp.where(lane_iota(listed.shape) < slots, listed, 0.0).astype(I32)
     lat, lon = listed // (lons * n_rg), listed % (lons * n_rg)
     key = lat // lats * n_rg + lon // lons
@@ -282,11 +286,15 @@
         list_ref[place] = jnp.bitwise_and(place - piece, packed - 1) * (tiles * rows) + row
     (copy,) = fetch(((list_ref, index_ref),), sem)
     for t in range(tiles):
-        x = got_ref[t]
-        for p in range(packed):
+        for i in range(rows // QUAD):
+            turn_ref[t * rows + i * QUAD : t * rows + (i + 1) * QUAD, :] = got_ref[t, i]
+        x = turn_ref[t * rows : (t + 1) * rows, :]
+        for p in range(1, packed):
             at = (p * tiles + t) * rows
             turn_ref[at : at + rows, :] = roll(x, p * width, 1)
         out_ref[t, table_rows:, :] = early_ref[t]
+        if t < n_rg or t >= tiles - n_rg:
+            out_ref[t, 0:table_rows, :] = jnp.zeros((table_rows, LANES), F32)
     for k in range(cell_ref.shape[1] // LANES):
         x = cell_ref[:, k * LANES : (k + 1) * LANES]
         for i in range(packed):
@@ -472,7 +480,7 @@
 
     def everywhere(step):
         step(0, rim_y_ref, 0)
-        pl.loop(1, pairs - 1, unroll=3)(lambda w: step(w, y_ref, w))
+        pl.loop(1, pairs - 1, unroll=pairs - 2)(lambda w: step(w, y_ref, w))
         step(pairs - 1, rim_y_ref, 1)
 
     def measure(w, ref, place):
@@ -672,7 +680,7 @@
 
     slices = call(
         functools.partial(slice_kernel, width),
-        sds((tiles, slice_rows + 8, LANES)),
+        sds((tiles, slice_rows // QUAD + 1, QUAD, LANES)),
         (heights, listing),
         grant=60,
     )
@@ -703,7 +711,7 @@
         sds((tiles, table_rows + early_rows, LANES)),
         (got_slices, early, cells),
         scratch=(
-            VMEM((packed * tiles * (slice_rows + 8), LANES), F32),
+            VMEM((packed * tiles * slice_rows, LANES), F32),
             VMEM((packed, tiles, LANES), I32),
             pltpu.SMEM((packed, tiles, LANES), I32),
             pltpu.SemaphoreType.DMA((1,)),

time: 58.8 us -> 57.4 us (0.976)
  waiting for transfers between devices: 21.3 us -> 20.4 us
    all_to_all x3, waiting for transfers between devices: 14.4 us -> 13.5 us  [exchange(): return lax.all_to_all(x, both, split_axis=0, concat_axis=0, tiled=True)]
where the time goes in v5:
time: 57.4 us; the launch traced here: 56.9 us
  waiting for transfers between devices  20.4 us (36%)
  starting transfers between devices  20.1 us (35%)
  Pallas kernels  15.6 us (27%)
  local copies, waits for them, and re-layouts  0.72 us (1%)
    all_to_all x3, starting transfers between devices, exchange(): return lax.all_to_all(x, both, split_axis=0, concat_axis=0, tiled=True)  17.3 us
    pallas_call x9, Pallas kernels, call(): pl.pallas_call(kernel, out_shape=outs, in_specs=[SSPEC if i in smem else...  15.6 us
    all_to_all x3, waiting for transfers between devices, exchange(): return lax.all_to_all(x, both, split_axis=0, concat_axis=0, tiled=True)  13.5 us
    ppermute x1, waiting for transfers between devices, scene(): one = lax.ppermute(one, 'az', swap_pairs(n_az, 0))  6.58 us
    ppermute x1, starting transfers between devices, scene(): one = lax.ppermute(one, 'az', swap_pairs(n_az, 0))  1.86 us
  transfers between devices with their start and end apart: 6, of which 4 were waited for; matrix products, arithmetic and copies ran while one was open for 0% of the time, Pallas kernels for 7%

profile of v5, /device:TPU:0, one launch (start us, length us, event | category | flops | bytes accessed | tf_op | source)
XLA Modules:
  0.0 56.9 jit_solution(3349612823957363511)
XLA Ops:
  0.0 1.8 %shard_map.100 = f32[16,33,1,128]{3,2,1,0:T(1,128)} custom-call(f32[8,8,1024]{2,1,0:T(8,128)} %dem_ref.1, s32[1,9]{1,0:T(1,128)} %list_ref.1), custom_call_target="tpu_custom_call" | custom-call | flops 1000000 | bytes 1000000 | tf_op jit(solution)/shard_map/pallas_call | solution.py:30
  1.8 0.0 copy-start.7
  1.8 7.5 %all-to-all-start = ((f32[16,33,1,128]{3,2,1,0:T(1,128)}), f32[16,33,1,128]{3,2,1,0:T(1,128)S(1)}, u32[]{:S(2)}, u32[]{:S(2)}) async-start(f32[16,33,1,128]{3,2,1,0:T(1,128)} %shard_map.100), calls=%async_computation | async-start | bytes 540672 | tf_op jit(solution)/shard_map/all_to_all | solution.py:679
  9.3 0.0 copy-done.7
  9.4 0.0 copy-start.5
  9.4 0.0 copy-start.6
  9.4 0.7 %copy-done.5 = s32[2048,1]{0,1:T(1,128)S(1)} copy-done((s32[2048,1]{0,1:T(1,128)S(1)}, s32[2048,1]{0,1:T(1,128)}, u32[]{:S(2)}) %copy-start.5) | copy-done | bytes 8216
  10.1 0.0 copy-done.6
  10.1 1.8 %shard_map.101 = (f32[16,8,128]{2,1,0:T(8,128)S(1)}, f32[16,256]{1,0:T(8,128)S(1)}, f32[16,128]{1,0:T(8,128)S(1)}, f32[16,16]{1,0:T(8,128)S(1)}, s32[16,256]{1,0...) custom-call(s32[16,128]{1,0:T(8,128)S(1)} %bitcast.10, ...), custom_call_target="tpu_custom_call" | custom-call | flops 1000000 | bytes 1000000 | tf_op jit(solution)/shard_map/pallas_call | solution.py:30
  11.9 7.6 %all-to-all-done.got_ref = f32[16,33,1,128]{3,2,1,0:T(1,128)S(1)} async-done(((f32[16,33,1,128]{3,2,1,0:T(1,128)}), f32[16,33,1,128]{3,2,1,0:T(1,128)S(1)}, u32[]{:S(2)}, u32[]{:S(2)}) %all-to-all-start) | async-done | bytes 270368 | tf_op jit(solution)/shard_map/all_to_all | solution.py:679
  19.5 1.8 %shard_map.102 = f32[16,24,128]{2,1,0:T(8,128)} custom-call(f32[16,33,1,128]{3,2,1,0:T(1,128)S(1)} %all-to-all-done.got_ref, f32[16,8,128]{2,1,0:T(8,128)S(1)} %get-tuple-element.21.early_ref, f32[16,256]{1,0:T(8,128)S(1)} %get-tuple-element.22.cell_ref), custom_call_target="tpu_custom_call" | custom-call | flops 1000000 | bytes 1000000 | tf_op jit(solution)/shard_map/pallas_call | solution.py:30
  21.3 0.0 copy-start
  21.3 3.7 %all-to-all-start.1 = ((f32[16,24,128]{2,1,0:T(8,128)}), f32[16,24,128]{2,1,0:T(8,128)S(1)}, u32[]{:S(2)}, u32[]{:S(2)}) async-start(f32[16,24,128]{2,1,0:T(8,128)} %shard_map.102), calls=%async_computation.1 | async-start | bytes 393216 | tf_op jit(solution)/shard_map/all_to_all | solution.py:679
  25.0 0.0 copy-done.1
  25.0 0.0 copy-done.2
  25.0 0.0 copy-done.3
  25.0 1.9 %collective-permute-start = (f32[4,16,512]{2,1,0:T(8,128)S(1)}, f32[4,16,512]{2,1,0:T(8,128)S(1)}, u32[]{:S(2)}, u32[]{:S(2)}) collective-permute-start(f32[4,16,512]{2,1,0:T(8,128)S(1)} %get-tuple-element.23), channel_id=1, source_target_pairs={{0,2},{2,0},{4,6},{6,4},{8,10},{10,8},{12,14},{14,12},{1,3},{3,1},... | collective-permute-start | bytes 393224 | tf_op jit(solution)/shard_map/ppermute | solution.py:689
  26.9 0.8 %collective-permute-start.1 = (f32[4,16,512]{2,1,0:T(8,128)S(1)}, f32[4,16,512]{2,1,0:T(8,128)S(1)}, u32[]{:S(2)}, u32[]{:S(2)}) collective-permute-start(f32[4,16,512]{2,1,0:T(8,128)S(1)} %get-tuple-element.24), channel_id=1, source_target_pairs={{2,4},{4,2},{6,8},{8,6},{10,12},{12,10},{3,5},{5,3},{7,9},{9,7},{1... | collective-permute-start | bytes 393224 | tf_op jit(solution)/shard_map/ppermute | solution.py:690
  27.7 6.6 %collective-permute-done.one_ref = f32[4,16,512]{2,1,0:T(8,128)S(1)} collective-permute-done((f32[4,16,512]{2,1,0:T(8,128)S(1)}, f32[4,16,512]{2,1,0:T(8,128)S(1)}, u32[]{:S(2)}, u32[]{:S(2)}) %collective-permute-start) | collective-permute-done | bytes 131104 | tf_op jit(solution)/shard_map/ppermute | solution.py:689
  34.3 0.0 collective-permute-done.1.two_ref
  34.3 0.0 all-to-all-done.1.got_ref
  34.3 4.1 %shard_map.104 = (f32[2,96,512]{2,1,0:T(8,128)S(1)}, f32[2,96,128]{2,1,0:T(8,128)S(1)}) custom-call(s32[1]{0:T(128)} %bitcast.1.par_ref, f32[16,24,128]{2,1,0:T(8,128)S(1)} %all-to-all-done.1.got_ref, f32[2,64,512]{2,1,0:T(8,128)S(1)} %copy-done.1, f32[64,512]{1,0:T(8,128)S(1)} %copy-done.2, s32[64,512]{1,0:T(8,128)S(1)} %copy-done.3, ...), custom_call_target="tpu_custom_call" | custom-call | flops 1000000 | bytes 1000000 | tf_op jit(solution)/shard_map/pallas_call | solution.py:30
  38.4 0.1 collective-permute-start.2
  38.4 0.0 copy-done
  38.5 0.0 copy-done.4
  38.5 1.0 %shard_map.105.y_ref = f32[1024,256]{1,0:T(8,128)S(1)} custom-call(f32[2,96,512]{2,1,0:T(8,128)S(1)} %get-tuple-element.25.flat_ref, bf16[128,192]{1,0:T(8,128)(2,1)S(1)} %copy-done.4, bf16[1728,256]{1,0:T(8,128)(2,1)S(1)} %copy-done), custom_call_target="tpu_custom_call" | custom-call | flops 1000000 | bytes 1000000 | tf_op jit(solution)/shard_map/pallas_call | solution.py:30
  39.4 0.3 collective-permute-done.2.edge_ref
  39.7 2.9 %shard_map.106 = f32[16,8,128]{2,1,0:T(8,128)} custom-call(s32[1]{0:T(128)} %bitcast.rg_ref, f32[1024,256]{1,0:T(8,128)S(1)} %shard_map.105.y_ref, f32[2,96,128]{2,1,0:T(8,128)S(1)} %collective-permute-done.2.edge_ref, f32[16,128]{1,0:T(8,128)S(1)} %get-tuple-element.27.rim_ref, f32[16,16]{1,0:T(8,128)S(1)} %get-tuple-element.28.side_ref, ...), custom_call_target="tpu_custom_call" | custom-call | flops 1000000 | bytes 1000000 | tf_op jit(solution)/shard_map/pallas_call | solution.py:30
  42.7 6.1 %all-to-all-start.2 = ((f32[16,8,128]{2,1,0:T(8,128)}), f32[16,8,128]{2,1,0:T(8,128)S(1)}, u32[]{:S(2)}, u32[]{:S(2)}) async-start(f32[16,8,128]{2,1,0:T(8,128)} %shard_map.106), calls=%async_computation.2 | async-start | bytes 131072 | tf_op jit(solution)/shard_map/all_to_all | solution.py:679
  48.8 1.0 %shard_map.107 = (bf16[128,4096]{1,0:T(8,128)(2,1)S(1)}, f32[32,4096]{1,0:T(8,128)S(1)}, f32[16,128]{1,0:T(8,128)S(1)}) custom-call(f32[16,24,128]{2,1,0:T(8,128)S(1)} %all-to-all-done.1.got_ref), custom_call_target="tpu_custom_call" | custom-call | flops 1000000 | bytes 1000000 | tf_op jit(solution)/shard_map/pallas_call | solution.py:30
  49.8 5.9 %all-to-all-done.2.got_ref = f32[16,8,128]{2,1,0:T(8,128)S(1)} async-done(((f32[16,8,128]{2,1,0:T(8,128)}), f32[16,8,128]{2,1,0:T(8,128)S(1)}, u32[]{:S(2)}, u32[]{:S(2)}) %all-to-all-start.2) | async-done | bytes 65568 | tf_op jit(solution)/shard_map/all_to_all | solution.py:679
  55.7 1.2 %shard_map.108 = f32[2,16,128]{2,1,0:T(8,128)} custom-call(f32[16,8,128]{2,1,0:T(8,128)S(1)} %all-to-all-done.2.got_ref, bf16[128,4096]{1,0:T(8,128)(2,1)S(1)} %get-tuple-element.34.hot_ref, f32[32,4096]{1,0:T(8,128)S(1)} %get-tuple-element.35.row_ref, f32[16,128]{1,0:T(8,128)S(1)} %get-tuple-element.36.weight_ref), custom_call_target="tpu_custom_call" | custom-call | flops 1000000 | bytes 1000000 | tf_op jit(solution)/shard_map/pallas_call | solution.py:30
  (6 shorter events, 0.0 us)
Async XLA Ops:
  1.8 7.6 %copy-start.7 = (f32[4,2048]{1,0:T(4,128)S(1)}, f32[4,2048]{1,0:T(4,128)}, u32[]{:S(2)}) copy-start(f32[4,2048]{1,0:T(4,128)} %param.17) | copy-start | bytes 98308
  1.8 17.7 %all-to-all-start = ((f32[16,33,1,128]{3,2,1,0:T(1,128)}), f32[16,33,1,128]{3,2,1,0:T(1,128)S(1)}, u32[]{:S(2)}, u32[]{:S(2)}) async-start(f32[16,33,1,128]{3,2,1,0:T(1,128)} %shard_map.100), calls=%async_computation | async-start | bytes 540672 | tf_op jit(solution)/shard_map/all_to_all | solution.py:679
  9.4 0.7 %copy-start.5 = (s32[2048,1]{0,1:T(1,128)S(1)}, s32[2048,1]{0,1:T(1,128)}, u32[]{:S(2)}) copy-start(s32[2048,1]{0,1:T(1,128)} %param.15) | copy-start | bytes 24580
  9.4 0.7 %copy-start.6 = (s32[2048]{0:T(1024)S(1)}, s32[2048]{0:T(1024)}, u32[]{:S(2)}) copy-start(s32[2048]{0:T(1024)} %param.16) | copy-start | bytes 24580
  19.5 5.5 %copy-start.1 = (f32[2,64,512]{2,1,0:T(8,128)S(1)}, f32[2,64,512]{2,1,0:T(8,128)}, u32[]{:S(2)}) copy-start(f32[2,64,512]{2,1,0:T(8,128)} %image_ref.3) | copy-start | bytes 786436
  19.5 5.5 %copy-start.2 = (f32[64,512]{1,0:T(8,128)S(1)}, f32[64,512]{1,0:T(8,128)}, u32[]{:S(2)}) copy-start(f32[64,512]{1,0:T(8,128)} %factor_ref.3) | copy-start | bytes 393220
  19.5 5.5 %copy-start.3 = (s32[64,512]{1,0:T(8,128)S(1)}, s32[64,512]{1,0:T(8,128)}, u32[]{:S(2)}) copy-start(s32[64,512]{1,0:T(8,128)} %position_ref.3) | copy-start | bytes 393220
  21.3 17.2 %copy-start = (bf16[1728,256]{1,0:T(8,128)(2,1)S(1)}, bf16[1728,256]{1,0:T(8,128)(2,1)}, u32[]{:S(2)}) copy-start(bf16[1728,256]{1,0:T(8,128)(2,1)} %constant.26.clone.const_ref) | copy-start | bytes 2654212
  21.3 13.0 %all-to-all-start.1 = ((f32[16,24,128]{2,1,0:T(8,128)}), f32[16,24,128]{2,1,0:T(8,128)S(1)}, u32[]{:S(2)}, u32[]{:S(2)}) async-start(f32[16,24,128]{2,1,0:T(8,128)} %shard_map.102), calls=%async_computation.1 | async-start | bytes 393216 | tf_op jit(solution)/shard_map/all_to_all | solution.py:679
  25.0 9.2 %collective-permute-start = (f32[4,16,512]{2,1,0:T(8,128)S(1)}, f32[4,16,512]{2,1,0:T(8,128)S(1)}, u32[]{:S(2)}, u32[]{:S(2)}) collective-permute-start(f32[4,16,512]{2,1,0:T(8,128)S(1)} %get-tuple-element.23), channel_id=1, source_target_pairs={{0,2},{2,0},{4,6},{6,4},{8,10},{10,8},{12,14},{14,12},{1,3},{3,1},... | collective-permute-start | bytes 393224 | tf_op jit(solution)/shard_map/ppermute | solution.py:689
  26.9 11.6 %copy-start.4 = (bf16[128,192]{1,0:T(8,128)(2,1)S(1)}, bf16[128,192]{1,0:T(8,128)(2,1)}, u32[]{:S(2)}) copy-start(bf16[128,192]{1,0:T(8,128)(2,1)} %constant.25.clone.az_ref) | copy-start | bytes 147460
  26.9 7.4 %collective-permute-start.1 = (f32[4,16,512]{2,1,0:T(8,128)S(1)}, f32[4,16,512]{2,1,0:T(8,128)S(1)}, u32[]{:S(2)}, u32[]{:S(2)}) collective-permute-start(f32[4,16,512]{2,1,0:T(8,128)S(1)} %get-tuple-element.24), channel_id=1, source_target_pairs={{2,4},{4,2},{6,8},{8,6},{10,12},{12,10},{3,5},{5,3},{7,9},{9,7},{1... | collective-permute-start | bytes 393224 | tf_op jit(solution)/shard_map/ppermute | solution.py:690
  38.4 1.4 %collective-permute-start.2 = (f32[2,96,128]{2,1,0:T(8,128)S(1)}, f32[2,96,128]{2,1,0:T(8,128)S(1)}, u32[]{:S(2)}, u32[]{:S(2)}) collective-permute-start(f32[2,96,128]{2,1,0:T(8,128)S(1)} %get-tuple-element.26), channel_id=1, source_target_pairs={{0,1},{1,0},{2,3},{3,2},{4,5},{5,4},{6,7},{7,6},{8,9},{9,8},{10,11... | collective-permute-start | bytes 294920 | tf_op jit(solution)/shard_map/ppermute | solution.py:730
  42.7 13.0 %all-to-all-start.2 = ((f32[16,8,128]{2,1,0:T(8,128)}), f32[16,8,128]{2,1,0:T(8,128)S(1)}, u32[]{:S(2)}, u32[]{:S(2)}) async-start(f32[16,8,128]{2,1,0:T(8,128)} %shard_map.106), calls=%async_computation.2 | async-start | bytes 131072 | tf_op jit(solution)/shard_map/all_to_all | solution.py:679
